TPU v7x, 32 devices: a whole 2x2x4 slice. The times are simulated.
32 devices in a mesh: dp: 2 (over x), row: 4 (over z), col: 4 (over y, core).
Axes of the slice: x: 2, y: 2, z: 4, core: 2. Of those that a mesh axis runs over, the one named last changes fastest.
Arguments:
- inputs: bfloat16 [1458, 1152], P('dp', 'row'), may hold values from -40 to 40
- pre_gain: float32 [1152], P('row'), may hold values from 0.5 to 1.5
- pre_shift: float32 [1152], P('row'), may hold values from -1.5 to 1.5
- joint_weight: bfloat16 [1152, 3456], P('row', 'col'), may hold values from -0.1875 to 0.1875
- joint_bias: float32 [4, 4, 144], P('col', 'row'), may hold values from -0.5 to 0.5
- merge_weight: bfloat16 [1152, 1152], P('col', 'row'), may hold values from -4 to 4
- merge_bias: float32 [1152], P('row'), may hold values from -2.5 to 2.5
- mid_gain: float32 [1152], P('row'), may hold values from 0.5 to 1.5
- mid_shift: float32 [1152], P('row'), may hold values from -1.5 to 1.5
- expand_weight: bfloat16 [1152, 4304], P('row', 'col'), may hold values from -0.1875 to 0.1875
- expand_bias: float32 [4304], P('col'), may hold values from -1.5 to 1.5
- reduce_weight: bfloat16 [4304, 1152], P('col', 'row'), may hold values from -0.09375 to 0.09375
- reduce_bias: float32 [1152], P('row'), may hold values from -2.5 to 2.5
- cotangent: bfloat16 [1458, 1152], P('dp', 'row'), may hold values from -6 to 6
Outputs:
- outputs: bfloat16 [1458, 1152], P('dp', 'row')
- inputs_grad: float32 [1458, 1152], P('dp', 'row')
- pre_gain_grad: float32 [1152], P('row')
- pre_shift_grad: float32 [1152], P('row')
- joint_weight_grad: float32 [1152, 3456], P('row', 'col')
- joint_bias_grad: float32 [4, 4, 144], P('col', 'row')
- merge_weight_grad: float32 [1152, 1152], P('col', 'row')
- merge_bias_grad: float32 [1152], P('row')
- mid_gain_grad: float32 [1152], P('row')
- mid_shift_grad: float32 [1152], P('row')
- expand_weight_grad: float32 [1152, 4304], P('row', 'col')
- expand_bias_grad: float32 [4304], P('col')
- reduce_weight_grad: float32 [4304, 1152], P('col', 'row')
- reduce_bias_grad: float32 [1152], P('row')
All inputs are finite; a program needn't handle non-finite values.
Results may differ from a plain program's by a relative error of at most 0.015.
Values may be sent and summed in bfloat16 or wider, within the bound.
No kernel may reach another device: no remote copies, remote signals or barrier semaphores. Data moves between devices by JAX's collectives and lax.ppermute only.
A program may use at most 64 MiB of HBM per device.

v0:
```python
import jax
import jax.numpy as jnp
from jax import lax
from jax.experimental.layout import Layout, with_layout_constraint
from jax.sharding import PartitionSpec as P

D = 1152
SEQ = 729


NORM_EPSILON = 1e-06
TANH_SLOPE = 0.7978845608028654
CUBIC_TERM = 0.044715
LOW = jnp.bfloat16
WIDE = jnp.float32


def gelu_pair(preact):
    inner_tanh = jnp.tanh(TANH_SLOPE * (preact + CUBIC_TERM * preact * preact * preact))
    value = 0.5 * preact * (1.0 + inner_tanh)
    slope = 0.5 * (1.0 + inner_tanh) + 0.5 * preact * (
        1.0 - inner_tanh * inner_tanh
    ) * TANH_SLOPE * (1.0 + 3.0 * CUBIC_TERM * preact * preact)
    return value, slope


def dot(left, right, left_dim, right_dim):
    return lax.dot_general(
        left, right, (((left_dim,), (right_dim,)), ((), ())), preferred_element_type=WIDE
    )


def pick(blocks, index, axis=0):
    return lax.dynamic_index_in_dim(blocks, index, axis, keepdims=False)


def place(blocks, block, index):
    return lax.dynamic_update_index_in_dim(blocks, block, index, 0)


def after(values, *others):
    return lax.optimization_barrier((values,) + others)[0]


def straight(values):
    return with_layout_constraint(values, Layout(tuple(range(values.ndim))))


def norm_forward(values):
    row_mean = jnp.mean(values, axis=-1, keepdims=True)
    row_var = jnp.mean(values * values, axis=-1, keepdims=True) - row_mean * row_mean
    inv_scale = lax.rsqrt(row_var + NORM_EPSILON)
    return (values - row_mean) * inv_scale, inv_scale


def norm_backward(upstream, unit_rows, inv_scale, norm_gain):
    scaled = upstream * norm_gain
    first = jnp.mean(scaled, axis=-1, keepdims=True)
    second = jnp.mean(scaled * unit_rows, axis=-1, keepdims=True)
    return inv_scale * (scaled - first - unit_rows * second)


def attend(query_rows, key_rows, value_rows, factor, keep):
    scores = dot(query_rows, key_rows, 1, 1) * factor
    totals = jnp.log(jnp.sum(jnp.exp(scores) * keep, axis=-1, keepdims=True))
    softmax_rows = (jnp.exp(scores - totals) * keep).astype(LOW)
    return dot(value_rows, softmax_rows, 0, 1).astype(LOW), totals


def attend_back(query_rows, key_rows, value_rows, context, totals, upstream, factor, keep):
    scores = dot(query_rows, key_rows, 1, 1) * factor
    weights = jnp.exp(scores - totals) * keep
    value_grad = dot(weights.astype(LOW), upstream, 0, 0)
    prob_grad = dot(upstream, value_rows, 1, 1)
    row_delta = jnp.sum(
        upstream.astype(WIDE) * context.T.astype(WIDE), axis=-1, keepdims=True
    )
    score_grad = (weights * (prob_grad - row_delta)).astype(LOW)
    scale = query_rows.shape[-1] ** (-0.5)
    query_grad = dot(score_grad, key_rows, 1, 0) * scale
    key_grad = dot(score_grad, query_rows, 0, 0) * scale
    return query_grad, key_grad, value_grad


def split_wide(value):
    high = value.astype(LOW)
    rest = value - high.astype(WIDE)
    middle = rest.astype(LOW)
    last = (rest - middle.astype(WIDE)).astype(LOW)
    return jnp.concatenate([high, middle, last], axis=0)


def merge_wide(rows):
    high, middle, last = jnp.split(rows.astype(WIDE), 3, axis=-2)
    return high + (middle + last)


def make_body(n_dp, n_row, n_col):
    masks = []
    while (1 << len(masks)) < n_col:
        masks.append(1 << len(masks))
    paired = n_dp == 2

    def col_swap(value, mask):
        return lax.ppermute(value, "col", [(i, i ^ mask) for i in range(n_col)])

    def dp_swap(value):
        return lax.ppermute(value, "dp", [(0, 1), (1, 0)])

    def row_exchange(blocks):
        return lax.all_to_all(blocks, "row", 0, 0, tiled=True)

    def row_gather(value):
        return row_exchange(jnp.broadcast_to(value[None], (n_row,) + value.shape))

    def col_parts(value):
        parts = [value]
        for mask in reversed(masks):
            parts = parts + [col_swap(part, mask) for part in parts]
        return parts

    def align_lanes(part, offset, near):
        size = part.shape[1] // n_col
        source = [near.index(mine ^ offset) for mine in near]
        return jnp.concatenate([part[:, i * size : (i + 1) * size] for i in source], axis=1)

    def col_gather(value):
        return jnp.concatenate(col_parts(value), axis=0)

    def body(
        inputs,
        pre_gain,
        pre_shift,
        joint_weight,
        joint_bias,
        merge_weight,
        merge_bias,
        mid_gain,
        mid_shift,
        expand_weight,
        expand_bias,
        reduce_weight,
        reduce_bias,
        cotangent,
    ):
        row = lax.axis_index("row")
        col = lax.axis_index("col")
        rank = lax.axis_index("dp")
        near = [0]
        for mask in reversed(masks):
            near = near + [offset ^ mask for offset in near]
        tokens, feats = inputs.shape
        width = feats * n_row
        images = tokens // SEQ
        head_size = joint_bias.shape[2] // 2
        span = -(-tokens // (n_row * n_col * 16)) * 16
        padded = span * n_row * n_col
        block = span * n_row
        units = expand_weight.shape[1] // n_row
        trio = joint_weight.shape[1] // n_row

        def pad_rows(value):
            return jnp.pad(value, ((0, padded - value.shape[0]), (0, 0)))

        def join(value, other, bit, axis):
            low = jnp.where(bit == 0, value, other)
            high = jnp.where(bit == 0, other, value)
            return straight(jnp.concatenate([low, high], axis=axis))

        def half_of(value, index, axis):
            size = value.shape[axis] // 2
            return lax.dynamic_slice_in_dim(value, index * size, size, axis)

        def own_rows(value):
            return lax.dynamic_slice_in_dim(value, row * span, span, 0)

        def own_block(value):
            return lax.dynamic_slice_in_dim(pad_rows(value), col * block, block, 0)

        def everywhere(value):
            return [value] * n_row

        def fit_lanes(blocks):
            return [jnp.pad(b, ((0, 0), (0, feats - b.shape[1]))) for b in blocks]

        def pack(*pieces):
            return straight(jnp.stack([jnp.concatenate(group, axis=0) for group in zip(*pieces)]))

        def height(piece):
            return piece[0].shape[0]

        def lanes(blocks):
            return jnp.concatenate([blocks[i] for i in range(n_row)], axis=-1)

        def weight_move(value, parts):
            mine = half_of(value, rank, 0) if paired else value
            return [mine[:, j * parts : (j + 1) * parts] for j in range(n_row)]

        def weight_move_rows(value, parts):
            mine = half_of(value, rank, 1) if paired else value
            return [mine[j * parts : (j + 1) * parts].T for j in range(n_row)]

        def weight_join(moved):
            if paired:
                moved = join(moved, dp_swap(moved), rank, 1)
            return moved.reshape(-1, moved.shape[-1])

        def grad_start(blocks):
            low = blocks.astype(LOW)
            if paired:
                sent = half_of(low, 1 - rank, 1)
                kept = half_of(low, rank, 1)
                low = (kept.astype(WIDE) + dp_swap(sent).astype(WIDE)).astype(LOW)
            elif n_dp > 1:
                low = lax.psum(blocks.astype(WIDE), "dp").astype(LOW)
            return low

        def grad_join(moved):
            return join(moved, dp_swap(moved), rank, 1) if paired else moved

        def sum_rows(product, rows, late=None):
            size = padded // 2
            got = col_swap(product(rows[size:]).astype(LOW), masks[0])
            total = product(rows[:size]) + got.astype(WIDE)
            for mask in masks[1:]:
                size //= 2
                total = total[:size] + col_swap(total[size:].astype(LOW), mask).astype(WIDE)
            total = total.astype(LOW)
            if late is not None:
                total = after(total, late)
            parts = row_exchange(total.reshape(n_row, span, width))
            return jnp.sum(parts.astype(WIDE), axis=0)

        def feature_blocks(rows):
            return [rows[:, j * feats : (j + 1) * feats] for j in range(n_row)]

        small = split_wide(
            jnp.stack([pre_gain, pre_shift, merge_bias, mid_gain, mid_shift, reduce_bias])
        )
        joint_wide = weight_move(joint_weight, trio)
        first = row_exchange(
            pack(everywhere(own_block(inputs)), everywhere(small), fit_lanes(joint_wide))
        )
        pieces = [
            everywhere(own_block(cotangent)),
            everywhere(half_of(merge_weight, rank, 0) if paired else merge_weight),
            fit_lanes(weight_move(expand_weight, units)),
            fit_lanes(weight_move_rows(reduce_weight, units)),
        ]
        second = row_exchange(after(pack(*pieces), first))
        ends = [sum(height(piece) for piece in pieces[:i]) for i in range(5)]
        cot_moved, merge_moved, expand_moved, reduce_moved = [
            second[:, low:high] for low, high in zip(ends, ends[1:])
        ]
        inner = block + small.shape[0]
        small_full = merge_wide(lanes(first[:, block:inner]))
        gain1, shift1, bias1, gain2, shift2, bias2 = [small_full[i : i + 1] for i in range(6)]
        x_full = col_gather(lanes(first[:, :block]))
        joint_own = weight_join(first[:, inner:, :trio])

        residual = x_full.astype(WIDE)
        unit1, inv1 = norm_forward(residual)
        normed1 = (unit1 * gain1 + shift1).astype(LOW)
        own_bias = joint_bias.reshape(2 * head_size)
        bias_row = jnp.concatenate(
            [own_bias[:head_size], jnp.zeros((head_size,), WIDE), own_bias[head_size:]]
        )
        joint_rows = (dot(normed1, joint_own, 1, 0) + bias_row).astype(LOW)
        query_rows = joint_rows[:, :head_size]
        key_rows = joint_rows[:, head_size : 2 * head_size]
        value_rows = joint_rows[:, 2 * head_size :]
        order = jnp.concatenate([(col ^ offset) * block + jnp.arange(block) for offset in near])
        real = (order < tokens).astype(WIDE)
        factor = real[:, None] * head_size ** (-0.5)
        keep = real[None]
        if images > 1:
            keep = keep * (order[:, None] // SEQ == order[None] // SEQ).astype(WIDE)
        own_context, totals = attend(query_rows, key_rows, value_rows, factor, keep)

        cot_full = col_gather(lanes(cot_moved))
        merge_rows = lanes(merge_moved)
        if paired:
            merge_rows = join(merge_rows, dp_swap(merge_rows), rank, 0)
        merge_full = col_gather(merge_rows)
        expand_own = weight_join(expand_moved[..., :units])
        reduce_own = weight_join(reduce_moved[..., :units])

        group_context = row_gather(after(own_context, second)).reshape(n_row * head_size, padded)
        context_full = jnp.concatenate(
            [
                align_lanes(part, offset, near) if offset else part
                for part, offset in zip(col_parts(group_context), near)
            ],
            axis=0,
        )
        mixed1 = residual + dot(context_full, merge_full, 0, 0) + bias1
        unit2, inv2 = norm_forward(mixed1)
        normed2 = (unit2 * gain2 + shift2).astype(LOW)

        own_units = lax.dynamic_slice_in_dim(expand_bias, row * units, units, 0)
        hidden_pre = dot(normed2, expand_own, 1, 0) + own_units
        value, slope = gelu_pair(hidden_pre)
        active = value.astype(LOW)
        hidden_grad = (dot(cot_full, reduce_own, 1, 0) * slope).astype(LOW)
        normed2_grad = sum_rows(lambda rows: dot(rows, expand_own, 1, 1), hidden_grad)

        unit2_own = own_rows(unit2)
        cot_own = own_rows(cot_full).astype(WIDE)
        mixed_grad = cot_own + norm_backward(normed2_grad, unit2_own, own_rows(inv2), gain2)
        mixed_block = row_gather(mixed_grad.astype(LOW)).reshape(block, width)
        mixed_low = col_gather(mixed_block)
        out_rows = sum_rows(
            lambda rows: dot(rows, reduce_own, 1, 1), after(active, normed2_grad), mixed_block
        )
        out_rows = (own_rows(mixed1) + out_rows + bias2).astype(LOW)

        expand_grad = dot(normed2, hidden_grad, 0, 0).reshape(n_row, feats, units)
        reduce_grad = dot(cot_full, active, 0, 0).reshape(n_row, feats, units)
        mlp_grad = grad_start(
            jnp.concatenate([expand_grad.astype(LOW), reduce_grad.astype(LOW)], axis=2)
        )
        mlp_grad = grad_join(row_exchange(after(mlp_grad, out_rows)))
        expand_weight_grad = (
            lanes(mlp_grad[..., :units]).astype(WIDE)
        )
        reduce_weight_grad = (
            jnp.concatenate([mlp_grad[j, :, units:].T for j in range(n_row)]).astype(WIDE)
        )

        head_rows = lax.dynamic_slice_in_dim(merge_full, row * head_size, head_size, 0)
        context_grad = dot(mixed_low, head_rows, 1, 1).astype(LOW)
        query_grad, key_grad, value_grad = attend_back(
            query_rows, key_rows, value_rows, own_context, totals, context_grad, factor, keep
        )
        joint_grad = jnp.concatenate([query_grad, key_grad, value_grad], axis=-1).astype(LOW)
        joint_bias_grad = jnp.concatenate(
            [jnp.sum(query_grad, axis=0), jnp.sum(value_grad, axis=0)]
        )
        normed1_grad = sum_rows(lambda rows: dot(rows, joint_own, 1, 1), joint_grad)
        unit1_own = own_rows(unit1)
        inputs_rows = mixed_grad + norm_backward(normed1_grad, unit1_own, own_rows(inv1), gain1)

        joint_blocks = grad_start(dot(normed1, joint_grad, 0, 0).reshape(n_row, feats, trio))
        own_mixed = lax.dynamic_slice_in_dim(mixed_low, row * feats, feats, 1)
        merge_weight_grad = dot(group_context, own_mixed, 1, 0)
        if paired:
            merge_grad_low = merge_weight_grad.astype(LOW)
            merge_weight_grad = merge_grad_low.astype(WIDE) + dp_swap(merge_grad_low).astype(WIDE)
        elif n_dp > 1:
            merge_weight_grad = lax.psum(merge_weight_grad, "dp")

        sums = jnp.stack(
            [
                jnp.sum(normed2_grad * unit2_own, axis=0),
                jnp.sum(normed2_grad, axis=0),
                jnp.sum(mixed_grad, axis=0),
                jnp.sum(normed1_grad * unit1_own, axis=0),
                jnp.sum(normed1_grad, axis=0),
            ]
        )
        hidden_sum = jnp.pad(
            jnp.sum(hidden_grad, axis=0, dtype=WIDE), (0, -(-units // feats) * feats - units)
        ).reshape(-1, feats)
        hidden_rows = hidden_sum.shape[0]
        hidden_low = split_wide(hidden_sum)
        sums_low = [jnp.concatenate([p, hidden_low]) for p in feature_blocks(split_wide(sums))]
        final = row_exchange(
            pack(
                feature_blocks(out_rows),
                feature_blocks(inputs_rows.astype(LOW)),
                sums_low,
                fit_lanes([joint_blocks[j] for j in range(n_row)]),
            )
        )
        ends = 2 * span + height(sums_low)
        vectors = final[:, 2 * span : ends]
        joint_blocks = grad_join(final[:, ends:, :trio])
        joint_weight_grad = lanes(joint_blocks).astype(WIDE)
        partial = jnp.sum(merge_wide(vectors[:, :15]), axis=0)
        hidden_all = merge_wide(vectors[:, 15:]).reshape(n_row, -1)[:, :units].reshape(-1)
        local = jnp.concatenate([hidden_all, joint_bias_grad])
        local = jnp.pad(local, (0, -local.shape[0] % feats)).reshape(-1, feats)
        local = jnp.concatenate(
            [partial, jnp.sum(cotangent.astype(WIDE), axis=0)[None], local], axis=0
        )
        shared = lax.all_gather(
            jnp.concatenate(
                [final[:, : 2 * span].reshape(2 * block, feats), split_wide(local)], axis=0
            ),
            "col",
        )
        spread = shared[:, : 2 * block].reshape(n_col, n_row, 2 * span, feats)
        outputs = spread[:, :, :span].reshape(padded, feats)[:tokens]
        inputs_grad = spread[:, :, span:].reshape(padded, feats)[:tokens].astype(WIDE)
        shared = merge_wide(shared[:, 2 * block :])
        vector_sums = jnp.concatenate([jnp.sum(shared[:, :5], axis=0), pick(shared, col)[5:]])
        if paired:
            vector_sums = vector_sums + dp_swap(vector_sums)
        elif n_dp > 1:
            vector_sums = lax.psum(vector_sums, "dp")
        reduce_bias_grad = vector_sums[5]
        own_sums = vector_sums[6:].reshape(-1)
        mid_gain_grad, mid_shift_grad, merge_bias_grad, pre_gain_grad, pre_shift_grad = [
            vector_sums[i] for i in range(5)
        ]
        tail = n_row * units
        expand_bias_grad = own_sums[:tail]
        joint_bias_grad = own_sums[tail : tail + 2 * head_size].reshape(joint_bias.shape)
        return (
            outputs,
            inputs_grad,
            pre_gain_grad,
            pre_shift_grad,
            joint_weight_grad,
            joint_bias_grad,
            merge_weight_grad,
            merge_bias_grad,
            mid_gain_grad,
            mid_shift_grad,
            expand_weight_grad,
            expand_bias_grad,
            reduce_weight_grad,
            reduce_bias_grad,
        )

    return body


def solution(mesh):
    in_specs = (
        P("dp", "row"),
        P("row"),
        P("row"),
        P("row", "col"),
        P("col", "row", None),
        P("col", "row"),
        P("row"),
        P("row"),
        P("row"),
        P("row", "col"),
        P("col"),
        P("col", "row"),
        P("row"),
        P("dp", "row"),
    )
    out_specs = (
        P("dp", "row"),
        P("dp", "row"),
        P("row"),
        P("row"),
        P("row", "col"),
        P("col", "row", None),
        P("col", "row"),
        P("row"),
        P("row"),
        P("row"),
        P("row", "col"),
        P("col"),
        P("col", "row"),
        P("row"),
    )
    body = make_body(mesh.shape["dp"], mesh.shape["row"], mesh.shape["col"])
    return jax.shard_map(body, mesh=mesh, in_specs=in_specs, out_specs=out_specs, check_vma=False)
```

profile of v0, /device:TPU:0, one launch (start us, length us, event | category | flops | bytes accessed | tf_op | source)
XLA Modules:
  0.0 364.2 jit_solution(17627631218448958483)
XLA Ops:
  15.1 6.3 %all-to-all-start = ((bf16[4,354,288]{1,2,0:T(8,128)(2,1)}), bf16[4,354,288]{1,2,0:T(8,128)(2,1)S(1)}, u32[]{:S(2)}, u32[]{:S(2)}) async-start(bf16[4,354,288]{1,2,0:T(8,128)(2,1)} %copy.141), calls=%async_computation | async-start | bytes 1769472 | tf_op jit(solution)/shard_map/all_to_all | solution.py:111
  23.6 20.1 %all-to-all-done = bf16[4,354,288]{1,2,0:T(8,128)(2,1)S(1)} async-done(((bf16[4,354,288]{1,2,0:T(8,128)(2,1)}), bf16[4,354,288]{1,2,0:T(8,128)(2,1)S(1)}, u32[]{:S(2)}, u32[]{:S(2)}) %all-to-all-start) | async-done | bytes 815648 | tf_op jit(solution)/shard_map/all_to_all | solution.py:111
  49.9 2.5 copy.152
  52.4 4.1 %all-to-all-start.1 = ((bf16[4,624,288]{1,2,0:T(8,128)(2,1)}), bf16[4,624,288]{1,2,0:T(8,128)(2,1)S(1)}, u32[]{:S(2)}, u32[]{:S(2)}) async-start(bf16[4,624,288]{1,2,0:T(8,128)(2,1)} %copy.152), calls=%async_computation.1 | async-start | bytes 2949120 | tf_op jit(solution)/shard_map/all_to_all | solution.py:111
  61.6 7.5 %collective-permute-done.3 = bf16[4,144,216]{2,1,0:T(8,128)(2,1)S(1)} collective-permute-done((bf16[4,144,216]{2,1,0:T(8,128)(2,1)S(1)}, bf16[4,144,216]{2,1,0:T(8,128)(2,1)S(1)}, u32[]{:S(2)}, u32[]{:S(2)}) %collective-permute-start.3) | collective-permute-done | bytes 248864 | tf_op jit(solution)/shard_map/ppermute | solution.py:108
  69.4 2.1 convert_reduce_fusion
  71.5 2.3 fusion.26
  76.4 15.8 %all-to-all-done.1 = bf16[4,624,288]{1,2,0:T(8,128)(2,1)S(1)} async-done(((bf16[4,624,288]{1,2,0:T(8,128)(2,1)}), bf16[4,624,288]{1,2,0:T(8,128)(2,1)S(1)}, u32[]{:S(2)}, u32[]{:S(2)}) %all-to-all-start.1) | async-done | bytes 1437728 | tf_op jit(solution)/shard_map/all_to_all | solution.py:111
  93.7 2.1 copy.194
  104.0 2.0 concatenate.164
  111.3 2.0 concatenate.168
  117.2 4.3 %all-to-all-start.2 = ((bf16[4,72,768]{2,1,0:T(8,128)(2,1)}), bf16[4,72,768]{2,1,0:T(8,128)(2,1)}, u32[]{:S(2)}, u32[]{:S(2)}) async-start(bf16[4,72,768]{2,1,0:T(8,128)(2,1)} %broadcast_in_dim.9), calls=%async_computation.2 | async-start | bytes 884736 | tf_op jit(solution)/shard_map/all_to_all | solution.py:111
  121.5 2.0 broadcast_select_fusion.3
  127.7 2.0 broadcast_select_fusion.5
  129.7 5.2 %all-to-all-done.2 = bf16[4,72,768]{2,1,0:T(8,128)(2,1)} async-done(((bf16[4,72,768]{2,1,0:T(8,128)(2,1)}), bf16[4,72,768]{2,1,0:T(8,128)(2,1)}, u32[]{:S(2)}, u32[]{:S(2)}) %all-to-all-start.2) | async-done | bytes 442400 | tf_op jit(solution)/shard_map/all_to_all | solution.py:111
  141.1 2.7 collective-permute-done.8
  143.8 8.6 %collective-permute-done.4 = bf16[288,768]{1,0:T(8,128)(2,1)S(1)} collective-permute-done((bf16[288,768]{1,0:T(8,128)(2,1)}, bf16[288,768]{1,0:T(8,128)(2,1)S(1)}, u32[]{:S(2)}, u32[]{:S(2)}) %collective-permute-start.4) | collective-permute-done | bytes 442400 | tf_op jit(solution)/shard_map/ppermute | solution.py:105
  154.4 5.4 %fusion.111 = (f32[768]{0:T(1024)S(1)}, f32[768]{0:T(1024)S(1)}, f32[768,1152]{1,0:T(8,128)S(1)}) fusion(f32[1152]{0:T(1024)S(1)} %get-tuple-element.111, bf16[288,1152]{1,0:T(8,128)(2,1)S(1)} %collective-permute-done.10, bf16[288,1152]{1,0:T(8,128)(2,1)S(1)} %collective-permute-done.9, bf16[288,1152]{1,0:T(8,128)(2,1)} %collective-permute-done.8, ...), kind=kOutput, calls=%fused_computation.292 | convolution fusion | flops 2082667008 | bytes 9742848 | tf_op jit(solution)/shard_map/dot_general | solution.py:28
  161.6 1.9 multiply_convert_fusion.1
  165.7 2.3 collective-permute-done.16
  170.4 10.7 %collective-permute-done.17 = bf16[192,1152]{1,0:T(8,128)(2,1)S(1)} collective-permute-done((bf16[192,1152]{1,0:T(8,128)(2,1)S(1)}, bf16[192,1152]{1,0:T(8,128)(2,1)S(1)}, u32[]{:S(2)}, u32[]{:S(2)}) %collective-permute-start.17) | collective-permute-done | bytes 442400 | tf_op jit(solution)/shard_map/ppermute | solution.py:105
  182.0 4.8 %all-to-all-start.3 = ((bf16[4,48,1152]{2,1,0:T(8,128)(2,1)}), bf16[4,48,1152]{2,1,0:T(8,128)(2,1)S(1)}, u32[]{:S(2)}, u32[]{:S(2)}) async-start(bf16[4,48,1152]{2,1,0:T(8,128)(2,1)} %bitcast.34), calls=%async_computation.3 | async-start | bytes 884736 | tf_op jit(solution)/shard_map/all_to_all | solution.py:111
  187.3 3.5 fusion.1
  190.9 8.1 %all-to-all-done.3 = bf16[4,48,1152]{2,1,0:T(8,128)(2,1)S(1)} async-done(((bf16[4,48,1152]{2,1,0:T(8,128)(2,1)}), bf16[4,48,1152]{2,1,0:T(8,128)(2,1)S(1)}, u32[]{:S(2)}, u32[]{:S(2)}) %all-to-all-start.3) | async-done | bytes 442400 | tf_op jit(solution)/shard_map/all_to_all | solution.py:111
  200.2 2.6 convolution_convert_fusion
  204.8 4.3 %all-to-all-start.4 = ((bf16[4,48,1152]{2,1,0:T(8,128)(2,1)}), bf16[4,48,1152]{2,1,0:T(8,128)(2,1)}, u32[]{:S(2)}, u32[]{:S(2)}) async-start(bf16[4,48,1152]{2,1,0:T(8,128)(2,1)} %broadcast_in_dim.10), calls=%async_computation.4 | async-start | bytes 884736 | tf_op jit(solution)/shard_map/all_to_all | solution.py:111
  209.1 3.6 convolution_convert_fusion.4
  214.2 3.4 convolution_convert_fusion.3
  217.6 2.3 copy.174
  219.9 2.2 fusion.41
  224.4 2.0 convolution_add_fusion.1
  227.0 2.9 pad_maximum_fusion
  230.5 5.7 %collective-permute-done.20 = bf16[192,1152]{1,0:T(8,128)(2,1)} collective-permute-done((bf16[192,1152]{1,0:T(8,128)(2,1)}, bf16[192,1152]{1,0:T(8,128)(2,1)}, u32[]{:S(2)}, u32[]{:S(2)}) %collective-permute-start.20) | collective-permute-done | bytes 442400 | tf_op jit(solution)/shard_map/ppermute | solution.py:105
  236.2 8.4 %collective-permute-done.19 = bf16[192,1152]{1,0:T(8,128)(2,1)S(1)} collective-permute-done((bf16[192,1152]{1,0:T(8,128)(2,1)S(1)}, bf16[192,1152]{1,0:T(8,128)(2,1)S(1)}, u32[]{:S(2)}, u32[]{:S(2)}) %collective-permute-start.19) | collective-permute-done | bytes 442400 | tf_op jit(solution)/shard_map/ppermute | solution.py:105
  245.5 4.9 %all-to-all-start.5 = ((bf16[4,48,1152]{2,1,0:T(8,128)(2,1)}), bf16[4,48,1152]{2,1,0:T(8,128)(2,1)}, u32[]{:S(2)}, u32[]{:S(2)}) async-start(bf16[4,48,1152]{2,1,0:T(8,128)(2,1)} %bitcast.36), calls=%async_computation.5 | async-start | bytes 884736 | tf_op jit(solution)/shard_map/all_to_all | solution.py:111
  252.7 1.8 fusion.67
  259.6 2.3 add_convert_fusion.2
  264.6 5.1 %all-to-all-start.8 = ((bf16[4,144,538]{2,1,0:T(8,128)(2,1)}), bf16[4,144,538]{2,1,0:T(8,128)(2,1)}, u32[]{:S(2)}, u32[]{:S(2)}) async-start(bf16[4,144,538]{2,1,0:T(8,128)(2,1)} %add_convert_fusion.2), calls=%async_computation.8 | async-start | bytes 1474560 | tf_op jit(solution)/shard_map/all_to_all | solution.py:111
  275.2 2.9 convolution_convert_fusion.5
  281.6 4.6 %collective-permute-done.24 = bf16[192,1152]{1,0:T(8,128)(2,1)} collective-permute-done((bf16[192,1152]{1,0:T(8,128)(2,1)}, bf16[192,1152]{1,0:T(8,128)(2,1)}, u32[]{:S(2)}, u32[]{:S(2)}) %collective-permute-start.24) | collective-permute-done | bytes 442400 | tf_op jit(solution)/shard_map/ppermute | solution.py:105
  286.2 2.1 fusion.33
  289.5 3.7 %all-to-all-start.6 = ((bf16[4,48,1152]{2,1,0:T(8,128)(2,1)}), bf16[4,48,1152]{2,1,0:T(8,128)(2,1)S(1)}, u32[]{:S(2)}, u32[]{:S(2)}) async-start(bf16[4,48,1152]{2,1,0:T(8,128)(2,1)} %bitcast.38), calls=%async_computation.6 | async-start | bytes 884736 | tf_op jit(solution)/shard_map/all_to_all | solution.py:111
  295.1 10.4 %all-to-all-done.6 = bf16[4,48,1152]{2,1,0:T(8,128)(2,1)S(1)} async-done(((bf16[4,48,1152]{2,1,0:T(8,128)(2,1)}), bf16[4,48,1152]{2,1,0:T(8,128)(2,1)S(1)}, u32[]{:S(2)}, u32[]{:S(2)}) %all-to-all-start.6) | async-done | bytes 442400 | tf_op jit(solution)/shard_map/all_to_all | solution.py:111
  311.7 3.7 %all-to-all-start.7 = ((bf16[4,258,288]{2,1,0:T(8,128)(2,1)}), bf16[4,258,288]{2,1,0:T(8,128)(2,1)S(1)}, u32[]{:S(2)}, u32[]{:S(2)}) async-start(bf16[4,258,288]{2,1,0:T(8,128)(2,1)} %pad_maximum_fusion.8), calls=%async_computation.7 | async-start | bytes 1622016 | tf_op jit(solution)/shard_map/all_to_all | solution.py:111
  319.8 3.8 %collective-permute-done.28 = bf16[288,288]{1,0:T(8,128)(2,1)S(1)} collective-permute-done((bf16[288,288]{1,0:T(8,128)(2,1)S(1)}, bf16[288,288]{1,0:T(8,128)(2,1)S(1)}, u32[]{:S(2)}, u32[]{:S(2)}) %collective-permute-start.28) | collective-permute-done | bytes 165920 | tf_op jit(solution)/shard_map/ppermute | solution.py:108
  329.8 5.9 %all-to-all-done.7 = bf16[4,258,288]{2,1,0:T(8,128)(2,1)S(1)} async-done(((bf16[4,258,288]{2,1,0:T(8,128)(2,1)}), bf16[4,258,288]{2,1,0:T(8,128)(2,1)S(1)}, u32[]{:S(2)}, u32[]{:S(2)}) %all-to-all-start.7) | async-done | bytes 594464 | tf_op jit(solution)/shard_map/all_to_all | solution.py:111
  336.8 10.8 %all-gather.1 = bf16[4,417,288]{1,2,0:T(8,128)(2,1)S(1)} all-gather(bf16[1,417,288]{1,2,0:T(8,128)(2,1)S(1)} %maximum_bitcast_fusion), channel_id=2, replica_groups=mesh['dp'=2,'row'=4,'col'=4] {'col'}, dimensions={0}, use_global_device_ids=true | all-gather | bytes 1200960 | tf_op jit(solution)/shard_map/all_gather | solution.py:386
  355.4 7.1 %collective-permute-done.27 = bf16[4,144,216]{2,1,0:T(8,128)(2,1)S(1)} collective-permute-done((bf16[4,144,216]{2,1,0:T(8,128)(2,1)S(1)}, bf16[4,144,216]{2,1,0:T(8,128)(2,1)S(1)}, u32[]{:S(2)}, u32[]{:S(2)}) %collective-permute-start.27) | collective-permute-done | bytes 248864 | tf_op jit(solution)/shard_map/ppermute | solution.py:108
  (381 shorter events, 126.9 us)
Async XLA Ops:
  15.1 28.6 %all-to-all-start = ((bf16[4,354,288]{1,2,0:T(8,128)(2,1)}), bf16[4,354,288]{1,2,0:T(8,128)(2,1)S(1)}, u32[]{:S(2)}, u32[]{:S(2)}) async-start(bf16[4,354,288]{1,2,0:T(8,128)(2,1)} %copy.141), calls=%async_computation | async-start | bytes 1769472 | tf_op jit(solution)/shard_map/all_to_all | solution.py:111
  48.3 139.0 %copy-start.13 = (bf16[192,1152]{1,0:T(8,128)(2,1)}, bf16[192,1152]{1,0:T(8,128)(2,1)S(1)}, u32[]{:S(2)}) copy-start(bf16[192,1152]{1,0:T(8,128)(2,1)S(1)} %concatenate.150) | copy-start | bytes 1327108
  48.3 12.9 %collective-permute-start = (bf16[192,1152]{1,0:T(8,128)(2,1)S(1)}, bf16[192,1152]{1,0:T(8,128)(2,1)}, u32[]{:S(2)}, u32[]{:S(2)}) collective-permute-start(bf16[192,1152]{1,0:T(8,128)(2,1)S(1)} %concatenate.150), channel_id=1, source_target_pairs={{0,2},{1,3},{2,0},{3,1},{4,6},{5,7},{6,4},{7,5},{8,10},{9,11},{10,... | collective-permute-start | bytes 1327112 | tf_op jit(solution)/shard_map/ppermute | solution.py:105
  49.9 19.4 %collective-permute-start.1 = (bf16[192,1152]{1,0:T(8,128)(2,1)S(1)}, bf16[192,1152]{1,0:T(8,128)(2,1)}, u32[]{:S(2)}, u32[]{:S(2)}) collective-permute-start(bf16[192,1152]{1,0:T(8,128)(2,1)S(1)} %concatenate.150), channel_id=1, source_target_pairs={{0,1},{1,0},{2,3},{3,2},{4,5},{5,4},{6,7},{7,6},{8,9},{9,8},{10,11... | collective-permute-start | bytes 1327112 | tf_op jit(solution)/shard_map/ppermute | solution.py:105
  52.4 39.8 %all-to-all-start.1 = ((bf16[4,624,288]{1,2,0:T(8,128)(2,1)}), bf16[4,624,288]{1,2,0:T(8,128)(2,1)S(1)}, u32[]{:S(2)}, u32[]{:S(2)}) async-start(bf16[4,624,288]{1,2,0:T(8,128)(2,1)} %copy.152), calls=%async_computation.1 | async-start | bytes 2949120 | tf_op jit(solution)/shard_map/all_to_all | solution.py:111
  59.7 9.5 %collective-permute-start.3 = (bf16[4,144,216]{2,1,0:T(8,128)(2,1)S(1)}, bf16[4,144,216]{2,1,0:T(8,128)(2,1)S(1)}, u32[]{:S(2)}, u32[]{:S(2)}) collective-permute-start(bf16[4,144,216]{2,1,0:T(8,128)(2,1)S(1)} %copy.184), channel_id=1, source_target_pairs={{0,16},{16,0},{1,17},{17,1},{2,18},{18,2},{3,19},{19,3},{4,20},{20... | collective-permute-start | bytes 746504 | tf_op jit(solution)/shard_map/ppermute | solution.py:108
  61.2 8.1 %collective-permute-start.2 = (bf16[192,1152]{1,0:T(8,128)(2,1)}, bf16[192,1152]{1,0:T(8,128)(2,1)S(1)}, u32[]{:S(2)}, u32[]{:S(2)}) collective-permute-start(bf16[192,1152]{1,0:T(8,128)(2,1)} %collective-permute-done), channel_id=1, source_target_pairs={{0,1},{1,0},{2,3},{3,2},{4,5},{5,4},{6,7},{7,6},{8,9},{9,8},{10,11... | collective-permute-start | bytes 1327112 | tf_op jit(solution)/shard_map/ppermute | solution.py:105
  61.6 100.0 %copy-start.54 = (f32[1152]{0:T(1024)}, f32[1152]{0:T(1024)S(1)}, u32[]{:S(2)}) copy-start(f32[1152]{0:T(1024)S(1)} %get-tuple-element.109) | copy-start | bytes 13828
  71.5 115.8 %copy-start.47 = (f32[768]{0:T(1024)}, f32[768]{0:T(1024)S(1)}, u32[]{:S(2)}) copy-start(f32[768]{0:T(1024)S(1)} %get-tuple-element.222) | copy-start | bytes 9220
  71.5 115.8 %copy-start.49 = (f32[768]{0:T(1024)}, f32[768]{0:T(1024)S(1)}, u32[]{:S(2)}) copy-start(f32[768]{0:T(1024)S(1)} %get-tuple-element.223) | copy-start | bytes 9220
  76.4 40.0 %copy-start.27 = (bf16[72,768]{1,0:T(8,128)(2,1)}, bf16[72,768]{1,0:T(8,128)(2,1)S(1)}, u32[]{:S(2)}) copy-start(bf16[72,768]{1,0:T(8,128)(2,1)S(1)} %convolution_convert_fusion.7) | copy-start | bytes 331780
  95.8 25.7 %collective-permute-start.15 = (bf16[4,144,269]{2,1,0:T(8,128)(2,1)}, bf16[4,144,269]{2,1,0:T(8,128)(2,1)}, u32[]{:S(2)}, u32[]{:S(2)}) collective-permute-start(bf16[4,144,269]{2,1,0:T(8,128)(2,1)} %copy.194), channel_id=1, source_target_pairs={{0,16},{16,0},{1,17},{17,1},{2,18},{18,2},{3,19},{19,3},{4,20},{20... | collective-permute-start | bytes 929672 | tf_op jit(solution)/shard_map/ppermute | solution.py:108
  106.0 17.5 %collective-permute-start.7 = (bf16[144,1152]{1,0:T(8,128)(2,1)}, bf16[144,1152]{1,0:T(8,128)(2,1)}, u32[]{:S(2)}, u32[]{:S(2)}) collective-permute-start(bf16[144,1152]{1,0:T(8,128)(2,1)} %concatenate.164), channel_id=1, source_target_pairs={{0,16},{16,0},{1,17},{17,1},{2,18},{18,2},{3,19},{19,3},{4,20},{20... | collective-permute-start | bytes 995336 | tf_op jit(solution)/shard_map/ppermute | solution.py:108
  113.3 13.9 %collective-permute-start.12 = (bf16[192,1152]{1,0:T(8,128)(2,1)}, bf16[192,1152]{1,0:T(8,128)(2,1)}, u32[]{:S(2)}, u32[]{:S(2)}) collective-permute-start(bf16[192,1152]{1,0:T(8,128)(2,1)} %concatenate.168), channel_id=1, source_target_pairs={{0,2},{1,3},{2,0},{3,1},{4,6},{5,7},{6,4},{7,5},{8,10},{9,11},{10,... | collective-permute-start | bytes 1327112 | tf_op jit(solution)/shard_map/ppermute | solution.py:105
  113.8 25.1 %collective-permute-start.13 = (bf16[192,1152]{1,0:T(8,128)(2,1)}, bf16[192,1152]{1,0:T(8,128)(2,1)}, u32[]{:S(2)}, u32[]{:S(2)}) collective-permute-start(bf16[192,1152]{1,0:T(8,128)(2,1)} %concatenate.168), channel_id=1, source_target_pairs={{0,1},{1,0},{2,3},{3,2},{4,5},{5,4},{6,7},{7,6},{8,9},{9,8},{10,11... | collective-permute-start | bytes 1327112 | tf_op jit(solution)/shard_map/ppermute | solution.py:105
  114.9 12.8 %collective-permute-start.11 = (bf16[4,144,269]{2,1,0:T(8,128)(2,1)}, bf16[4,144,269]{2,1,0:T(8,128)(2,1)S(1)}, u32[]{:S(2)}, u32[]{:S(2)}) collective-permute-start(bf16[4,144,269]{2,1,0:T(8,128)(2,1)} %copy.189), channel_id=1, source_target_pairs={{0,16},{16,0},{1,17},{17,1},{2,18},{18,2},{3,19},{19,3},{4,20},{20... | collective-permute-start | bytes 929672 | tf_op jit(solution)/shard_map/ppermute | solution.py:108
  117.2 17.8 %all-to-all-start.2 = ((bf16[4,72,768]{2,1,0:T(8,128)(2,1)}), bf16[4,72,768]{2,1,0:T(8,128)(2,1)}, u32[]{:S(2)}, u32[]{:S(2)}) async-start(bf16[4,72,768]{2,1,0:T(8,128)(2,1)} %broadcast_in_dim.9), calls=%async_computation.2 | async-start | bytes 884736 | tf_op jit(solution)/shard_map/all_to_all | solution.py:111
  124.7 29.7 %copy-start.17 = (bf16[144,1152]{1,0:T(8,128)(2,1)}, bf16[144,1152]{1,0:T(8,128)(2,1)S(1)}, u32[]{:S(2)}) copy-start(bf16[144,1152]{1,0:T(8,128)(2,1)S(1)} %get-tuple-element.160) | copy-start | bytes 995332
  124.7 29.7 %copy-start.19 = (bf16[144,1152]{1,0:T(8,128)(2,1)}, bf16[144,1152]{1,0:T(8,128)(2,1)S(1)}, u32[]{:S(2)}) copy-start(bf16[144,1152]{1,0:T(8,128)(2,1)S(1)} %get-tuple-element.161) | copy-start | bytes 995332
  125.7 18.1 %collective-permute-start.8 = (bf16[288,1152]{1,0:T(8,128)(2,1)}, bf16[288,1152]{1,0:T(8,128)(2,1)}, u32[]{:S(2)}, u32[]{:S(2)}) collective-permute-start(bf16[288,1152]{1,0:T(8,128)(2,1)} %pad_maximum_fusion.9), channel_id=1, source_target_pairs={{0,2},{1,3},{2,0},{3,1},{4,6},{5,7},{6,4},{7,5},{8,10},{9,11},{10,... | collective-permute-start | bytes 1990664 | tf_op jit(solution)/shard_map/ppermute | solution.py:105
  127.2 12.3 %collective-permute-start.14 = (bf16[192,1152]{1,0:T(8,128)(2,1)}, bf16[192,1152]{1,0:T(8,128)(2,1)}, u32[]{:S(2)}, u32[]{:S(2)}) collective-permute-start(bf16[192,1152]{1,0:T(8,128)(2,1)} %collective-permute-done.12), channel_id=1, source_target_pairs={{0,1},{1,0},{2,3},{3,2},{4,5},{5,4},{6,7},{7,6},{8,9},{9,8},{10,11... | collective-permute-start | bytes 1327112 | tf_op jit(solution)/shard_map/ppermute | solution.py:105
  134.9 17.5 %collective-permute-start.4 = (bf16[288,768]{1,0:T(8,128)(2,1)}, bf16[288,768]{1,0:T(8,128)(2,1)S(1)}, u32[]{:S(2)}, u32[]{:S(2)}) collective-permute-start(bf16[288,768]{1,0:T(8,128)(2,1)} %bitcast.23), channel_id=1, source_target_pairs={{0,2},{1,3},{2,0},{3,1},{4,6},{5,7},{6,4},{7,5},{8,10},{9,11},{10,... | collective-permute-start | bytes 1327112 | tf_op jit(solution)/shard_map/ppermute | solution.py:105
  136.4 16.0 %collective-permute-start.5 = (bf16[288,768]{1,0:T(8,128)(2,1)}, bf16[288,768]{1,0:T(8,128)(2,1)S(1)}, u32[]{:S(2)}, u32[]{:S(2)}) collective-permute-start(bf16[288,768]{1,0:T(8,128)(2,1)} %bitcast.23), channel_id=1, source_target_pairs={{0,1},{1,0},{2,3},{3,2},{4,5},{5,4},{6,7},{7,6},{8,9},{9,8},{10,11... | collective-permute-start | bytes 1327112 | tf_op jit(solution)/shard_map/ppermute | solution.py:105
  139.0 15.4 %collective-permute-start.9 = (bf16[288,1152]{1,0:T(8,128)(2,1)}, bf16[288,1152]{1,0:T(8,128)(2,1)S(1)}, u32[]{:S(2)}, u32[]{:S(2)}) collective-permute-start(bf16[288,1152]{1,0:T(8,128)(2,1)} %pad_maximum_fusion.9), channel_id=1, source_target_pairs={{0,1},{1,0},{2,3},{3,2},{4,5},{5,4},{6,7},{7,6},{8,9},{9,8},{10,11... | collective-permute-start | bytes 1990664 | tf_op jit(solution)/shard_map/ppermute | solution.py:105
  143.8 10.6 %collective-permute-start.10 = (bf16[288,1152]{1,0:T(8,128)(2,1)}, bf16[288,1152]{1,0:T(8,128)(2,1)S(1)}, u32[]{:S(2)}, u32[]{:S(2)}) collective-permute-start(bf16[288,1152]{1,0:T(8,128)(2,1)} %collective-permute-done.8), channel_id=1, source_target_pairs={{0,1},{1,0},{2,3},{3,2},{4,5},{5,4},{6,7},{7,6},{8,9},{9,8},{10,11... | collective-permute-start | bytes 1990664 | tf_op jit(solution)/shard_map/ppermute | solution.py:105
  152.4 1.8 collective-permute-start.6
  164.8 65.1 %copy-start.56 = (f32[269]{0:T(512)}, f32[269]{0:T(512)S(1)}, u32[]{:S(2)}) copy-start(f32[269]{0:T(512)S(1)} %get-tuple-element.237) | copy-start | bytes 3232
  165.6 2.5 collective-permute-start.16
  168.8 12.3 %collective-permute-start.17 = (bf16[192,1152]{1,0:T(8,128)(2,1)S(1)}, bf16[192,1152]{1,0:T(8,128)(2,1)S(1)}, u32[]{:S(2)}, u32[]{:S(2)}) collective-permute-start(bf16[192,1152]{1,0:T(8,128)(2,1)S(1)} %slice.775), channel_id=1, source_target_pairs={{0,2},{1,3},{2,0},{3,1},{4,6},{5,7},{6,4},{7,5},{8,10},{9,11},{10,... | collective-permute-start | bytes 1327112 | tf_op jit(solution)/shard_map/ppermute | solution.py:105
  182.0 17.0 %all-to-all-start.3 = ((bf16[4,48,1152]{2,1,0:T(8,128)(2,1)}), bf16[4,48,1152]{2,1,0:T(8,128)(2,1)S(1)}, u32[]{:S(2)}, u32[]{:S(2)}) async-start(bf16[4,48,1152]{2,1,0:T(8,128)(2,1)} %bitcast.34), calls=%async_computation.3 | async-start | bytes 884736 | tf_op jit(solution)/shard_map/all_to_all | solution.py:111
  202.8 21.6 %collective-permute-start.18 = (bf16[384,1152]{1,0:T(8,128)(2,1)}, bf16[384,1152]{1,0:T(8,128)(2,1)}, u32[]{:S(2)}, u32[]{:S(2)}) collective-permute-start(bf16[384,1152]{1,0:T(8,128)(2,1)} %convolution_convert_fusion), channel_id=1, source_target_pairs={{0,1},{1,0},{2,3},{3,2},{4,5},{5,4},{6,7},{7,6},{8,9},{9,8},{10,11... | collective-permute-start | bytes 2654216 | tf_op jit(solution)/shard_map/ppermute | solution.py:105
  204.8 18.1 %all-to-all-start.4 = ((bf16[4,48,1152]{2,1,0:T(8,128)(2,1)}), bf16[4,48,1152]{2,1,0:T(8,128)(2,1)}, u32[]{:S(2)}, u32[]{:S(2)}) async-start(bf16[4,48,1152]{2,1,0:T(8,128)(2,1)} %broadcast_in_dim.10), calls=%async_computation.4 | async-start | bytes 884736 | tf_op jit(solution)/shard_map/all_to_all | solution.py:111
  222.1 37.5 %collective-permute-start.29 = (bf16[4,144,538]{2,1,0:T(8,128)(2,1)}, bf16[4,144,538]{2,1,0:T(8,128)(2,1)}, u32[]{:S(2)}, u32[]{:S(2)}) collective-permute-start(bf16[4,144,538]{2,1,0:T(8,128)(2,1)} %fusion.41), channel_id=1, source_target_pairs={{0,16},{16,0},{1,17},{17,1},{2,18},{18,2},{3,19},{19,3},{4,20},{20... | collective-permute-start | bytes 1859336 | tf_op jit(solution)/shard_map/ppermute | solution.py:108
  222.9 13.4 %collective-permute-start.20 = (bf16[192,1152]{1,0:T(8,128)(2,1)}, bf16[192,1152]{1,0:T(8,128)(2,1)}, u32[]{:S(2)}, u32[]{:S(2)}) collective-permute-start(bf16[192,1152]{1,0:T(8,128)(2,1)} %bitcast.35), channel_id=1, source_target_pairs={{0,2},{1,3},{2,0},{3,1},{4,6},{5,7},{6,4},{7,5},{8,10},{9,11},{10,... | collective-permute-start | bytes 1327112 | tf_op jit(solution)/shard_map/ppermute | solution.py:105
  226.5 18.2 %collective-permute-start.19 = (bf16[192,1152]{1,0:T(8,128)(2,1)S(1)}, bf16[192,1152]{1,0:T(8,128)(2,1)S(1)}, u32[]{:S(2)}, u32[]{:S(2)}) collective-permute-start(bf16[192,1152]{1,0:T(8,128)(2,1)S(1)} %slice.774), channel_id=1, source_target_pairs={{0,2},{1,3},{2,0},{3,1},{4,6},{5,7},{6,4},{7,5},{8,10},{9,11},{10,... | collective-permute-start | bytes 1327112 | tf_op jit(solution)/shard_map/ppermute | solution.py:105
  230.5 19.9 %collective-permute-start.21 = (bf16[192,1152]{1,0:T(8,128)(2,1)}, bf16[192,1152]{1,0:T(8,128)(2,1)S(1)}, u32[]{:S(2)}, u32[]{:S(2)}) collective-permute-start(bf16[192,1152]{1,0:T(8,128)(2,1)} %bitcast.35), channel_id=1, source_target_pairs={{0,1},{1,0},{2,3},{3,2},{4,5},{5,4},{6,7},{7,6},{8,9},{9,8},{10,11... | collective-permute-start | bytes 1327112 | tf_op jit(solution)/shard_map/ppermute | solution.py:105
  236.2 14.9 %collective-permute-start.22 = (bf16[192,1152]{1,0:T(8,128)(2,1)}, bf16[192,1152]{1,0:T(8,128)(2,1)}, u32[]{:S(2)}, u32[]{:S(2)}) collective-permute-start(bf16[192,1152]{1,0:T(8,128)(2,1)} %collective-permute-done.20), channel_id=1, source_target_pairs={{0,1},{1,0},{2,3},{3,2},{4,5},{5,4},{6,7},{7,6},{8,9},{9,8},{10,11... | collective-permute-start | bytes 1327112 | tf_op jit(solution)/shard_map/ppermute | solution.py:105
  245.5 17.1 %all-to-all-start.5 = ((bf16[4,48,1152]{2,1,0:T(8,128)(2,1)}), bf16[4,48,1152]{2,1,0:T(8,128)(2,1)}, u32[]{:S(2)}, u32[]{:S(2)}) async-start(bf16[4,48,1152]{2,1,0:T(8,128)(2,1)} %bitcast.36), calls=%async_computation.5 | async-start | bytes 884736 | tf_op jit(solution)/shard_map/all_to_all | solution.py:111
  259.5 10.3 %collective-permute-start.23 = (bf16[384,1152]{1,0:T(8,128)(2,1)}, bf16[384,1152]{1,0:T(8,128)(2,1)}, u32[]{:S(2)}, u32[]{:S(2)}) collective-permute-start(bf16[384,1152]{1,0:T(8,128)(2,1)} %convolution_convert_fusion.2), channel_id=1, source_target_pairs={{0,1},{1,0},{2,3},{3,2},{4,5},{5,4},{6,7},{7,6},{8,9},{9,8},{10,11... | collective-permute-start | bytes 2654216 | tf_op jit(solution)/shard_map/ppermute | solution.py:105
  264.6 24.9 %all-to-all-start.8 = ((bf16[4,144,538]{2,1,0:T(8,128)(2,1)}), bf16[4,144,538]{2,1,0:T(8,128)(2,1)}, u32[]{:S(2)}, u32[]{:S(2)}) async-start(bf16[4,144,538]{2,1,0:T(8,128)(2,1)} %add_convert_fusion.2), calls=%async_computation.8 | async-start | bytes 1474560 | tf_op jit(solution)/shard_map/all_to_all | solution.py:111
  273.6 12.6 %collective-permute-start.24 = (bf16[192,1152]{1,0:T(8,128)(2,1)}, bf16[192,1152]{1,0:T(8,128)(2,1)}, u32[]{:S(2)}, u32[]{:S(2)}) collective-permute-start(bf16[192,1152]{1,0:T(8,128)(2,1)} %slice.773), channel_id=1, source_target_pairs={{0,2},{1,3},{2,0},{3,1},{4,6},{5,7},{6,4},{7,5},{8,10},{9,11},{10,... | collective-permute-start | bytes 1327112 | tf_op jit(solution)/shard_map/ppermute | solution.py:105
  280.1 13.2 %collective-permute-start.25 = (bf16[4,144,216]{2,1,0:T(8,128)(2,1)}, bf16[4,144,216]{2,1,0:T(8,128)(2,1)S(1)}, u32[]{:S(2)}, u32[]{:S(2)}) collective-permute-start(bf16[4,144,216]{2,1,0:T(8,128)(2,1)} %constant_dynamic-slice_fusion), channel_id=1, source_target_pairs={{0,16},{16,0},{1,17},{17,1},{2,18},{18,2},{3,19},{19,3},{4,20},{20... | collective-permute-start | bytes 746504 | tf_op jit(solution)/shard_map/ppermute | solution.py:108
  289.5 16.0 %all-to-all-start.6 = ((bf16[4,48,1152]{2,1,0:T(8,128)(2,1)}), bf16[4,48,1152]{2,1,0:T(8,128)(2,1)S(1)}, u32[]{:S(2)}, u32[]{:S(2)}) async-start(bf16[4,48,1152]{2,1,0:T(8,128)(2,1)} %bitcast.38), calls=%async_computation.6 | async-start | bytes 884736 | tf_op jit(solution)/shard_map/all_to_all | solution.py:111
  293.6 30.8 %collective-permute-start.30 = (bf16[4,144,538]{2,1,0:T(8,128)(2,1)}, bf16[4,144,538]{2,1,0:T(8,128)(2,1)}, u32[]{:S(2)}, u32[]{:S(2)}) collective-permute-start(bf16[4,144,538]{2,1,0:T(8,128)(2,1)} %all-to-all-done.8), channel_id=1, source_target_pairs={{0,16},{16,0},{1,17},{17,1},{2,18},{18,2},{3,19},{19,3},{4,20},{20... | collective-permute-start | bytes 1859336 | tf_op jit(solution)/shard_map/ppermute | solution.py:108
  311.7 23.9 %all-to-all-start.7 = ((bf16[4,258,288]{2,1,0:T(8,128)(2,1)}), bf16[4,258,288]{2,1,0:T(8,128)(2,1)S(1)}, u32[]{:S(2)}, u32[]{:S(2)}) async-start(bf16[4,258,288]{2,1,0:T(8,128)(2,1)} %pad_maximum_fusion.8), calls=%async_computation.7 | async-start | bytes 1622016 | tf_op jit(solution)/shard_map/all_to_all | solution.py:111
  317.0 6.5 %collective-permute-start.28 = (bf16[288,288]{1,0:T(8,128)(2,1)S(1)}, bf16[288,288]{1,0:T(8,128)(2,1)S(1)}, u32[]{:S(2)}, u32[]{:S(2)}) collective-permute-start(bf16[288,288]{1,0:T(8,128)(2,1)S(1)} %convolution_convert_fusion.6), channel_id=1, source_target_pairs={{0,16},{16,0},{1,17},{17,1},{2,18},{18,2},{3,19},{19,3},{4,20},{20... | collective-permute-start | bytes 497672 | tf_op jit(solution)/shard_map/ppermute | solution.py:108
  349.4 4.6 %collective-permute-start.26 = (f32[11,288]{1,0:T(8,128)S(1)}, f32[11,288]{1,0:T(8,128)S(1)}, u32[]{:S(2)}, u32[]{:S(2)}) collective-permute-start(f32[11,288]{1,0:T(8,128)S(1)} %pad_maximum_fusion.17), channel_id=1, source_target_pairs={{0,16},{16,0},{1,17},{17,1},{2,18},{18,2},{3,19},{19,3},{4,20},{20... | collective-permute-start | bytes 38024 | tf_op jit(solution)/shard_map/ppermute | solution.py:108
  353.5 9.1 %collective-permute-start.27 = (bf16[4,144,216]{2,1,0:T(8,128)(2,1)S(1)}, bf16[4,144,216]{2,1,0:T(8,128)(2,1)S(1)}, u32[]{:S(2)}, u32[]{:S(2)}) collective-permute-start(bf16[4,144,216]{2,1,0:T(8,128)(2,1)S(1)} %slice.586), channel_id=1, source_target_pairs={{0,16},{16,0},{1,17},{17,1},{2,18},{18,2},{3,19},{19,3},{4,20},{20... | collective-permute-start | bytes 746504 | tf_op jit(solution)/shard_map/ppermute | solution.py:108
  (58 other events, 390.4 us)
where the time goes:
time: 371 us; the launch traced here: 364 us
  waiting for transfers between devices  130 us (35%)
  local copies, waits for them, and re-layouts  69.2 us (19%)
  starting transfers between devices  65.1 us (18%)
  other arithmetic  48.6 us (13%)
  matrix products  37.6 us (10%)
  blocking collectives  10.8 us (3%)
    all_to_all x9, waiting for transfers between devices, row_exchange(): return lax.all_to_all(blocks, 'row', 0, 0, tiled=True)  66.9 us
    ppermute x21, waiting for transfers between devices, col_swap(): return lax.ppermute(value, 'col', [(i, i ^ mask) for i in range(n_col)])  44.6 us
    all_to_all x9, starting transfers between devices, row_exchange(): return lax.all_to_all(blocks, 'row', 0, 0, tiled=True)  41.3 us
    dot_general x21, matrix products, dot(): lax.dot_general(left, right, (((left_dim,), (right_dim,)), ((), ())), pre...  37.6 us
    unnamed x154, local copies, waits for them, and re-layouts  26.7 us
    ppermute x10, waiting for transfers between devices, dp_swap(): return lax.ppermute(value, 'dp', [(0, 1), (1, 0)])  18.9 us
    ppermute x10, starting transfers between devices, dp_swap(): return lax.ppermute(value, 'dp', [(0, 1), (1, 0)])  12.4 us
    ppermute x21, starting transfers between devices, col_swap(): return lax.ppermute(value, 'col', [(i, i ^ mask) for i in range(n_col)])  11.4 us
  transfers between devices with their start and end apart: 40, of which 20 were waited for; matrix products, arithmetic and copies ran while one was open for 30% of the time, Pallas kernels for 0%

commit v1 on v0

--- a/solution.py
+++ b/solution.py
@@ -1,7 +1,9 @@
 import jax
 import jax.numpy as jnp
 from jax import lax
+from jax.experimental import pallas as pl
 from jax.experimental.layout import Layout, with_layout_constraint
+from jax.experimental.pallas import tpu as pltpu
 from jax.sharding import PartitionSpec as P
 
 D = 1152
@@ -83,16 +85,212 @@
 
 
 def split_wide(value):
-    high = value.astype(LOW)
-    rest = value - high.astype(WIDE)
-    middle = rest.astype(LOW)
-    last = (rest - middle.astype(WIDE)).astype(LOW)
-    return jnp.concatenate([high, middle, last], axis=0)
+    high = lax.reduce_precision(value, 8, 7)
+    rest = value - high
+    middle = lax.reduce_precision(rest, 8, 7)
+    return jnp.concatenate([high, middle, rest - middle], axis=0).astype(LOW)
 
 
 def merge_wide(rows):
     high, middle, last = jnp.split(rows.astype(WIDE), 3, axis=-2)
     return high + (middle + last)
+
+
+def local_call(kernel, outs, scalars, *arrays, scratch=()):
+    return pl.pallas_call(
+        kernel,
+        out_shape=[jax.ShapeDtypeStruct(shape, kind) for shape, kind in outs],
+        grid_spec=pltpu.PrefetchScalarGridSpec(
+            num_scalar_prefetch=1,
+            grid=(1,),
+            in_specs=[
+                pl.BlockSpec(a.shape, lambda i, _, n=a.ndim: (0,) * n) for a in arrays
+            ],
+            out_specs=[
+                pl.BlockSpec(shape, lambda i, _, n=len(shape): (0,) * n) for shape, _ in outs
+            ],
+            scratch_shapes=list(scratch),
+        ),
+    )(scalars, *arrays)
+
+
+def split_blocks(moved, plan):
+    sources = moved.shape[0]
+    outs = []
+    for _, rows, used, side in plan:
+        shape = (rows, sources * used) if side else (sources * rows, used)
+        outs.append((shape, moved.dtype))
+
+    def kernel(_, moved_ref, *out_refs):
+        for (start, rows, used, side), out_ref in zip(plan, out_refs):
+            for i in range(sources):
+                piece = moved_ref[i, start : start + rows, :used]
+                if side:
+                    out_ref[:, i * used : (i + 1) * used] = piece
+                else:
+                    out_ref[i * rows : (i + 1) * rows, :] = piece
+
+    return local_call(kernel, outs, jnp.zeros((1,), jnp.int32), moved)
+
+
+def pack_first(inputs, joint_weight, vectors, col, rank, block, padded, parts, halves):
+    tokens, feats = inputs.shape
+    count = len(vectors)
+    small = -(-3 * count // 16) * 16
+    half = feats // halves
+    rows = block + small + half
+
+    def kernel(place_ref, input_ref, joint_ref, *refs):
+        vector_refs, (out_ref, wide_ref, token_ref) = refs[:count], refs[count:]
+        token_ref[...] = jnp.zeros_like(token_ref)
+        token_ref[:tokens, :] = input_ref[...]
+        wide_ref[...] = jnp.zeros_like(wide_ref)
+        for i, vector_ref in enumerate(vector_refs):
+            value = vector_ref[...].reshape(1, feats)
+            high = value.astype(LOW).astype(WIDE)
+            middle = (value - high).astype(LOW).astype(WIDE)
+            wide_ref[i : i + 1, :] = high
+            wide_ref[count + i : count + i + 1, :] = middle
+            wide_ref[2 * count + i : 2 * count + i + 1, :] = value - high - middle
+        start = pl.multiple_of(place_ref[0] * block, 16)
+        mine = token_ref[pl.ds(start, block), :]
+        low = wide_ref[...].astype(LOW)
+        joint = joint_ref[pl.ds(pl.multiple_of(place_ref[1] * half, 16), half), :]
+        for j in range(out_ref.shape[0]):
+            out_ref[j, :block, :] = mine
+            out_ref[j, block : block + small, :] = low
+            out_ref[j, block + small :, :parts] = joint[:, j * parts : (j + 1) * parts]
+            out_ref[j, block + small :, parts:] = jnp.zeros((half, feats - parts), LOW)
+
+    count_out = joint_weight.shape[1] // parts
+    place_at = jnp.stack([col, rank if halves == 2 else 0 * rank]).astype(jnp.int32)
+    return local_call(
+        kernel,
+        [((count_out, rows, feats), LOW)],
+        place_at,
+        inputs,
+        joint_weight,
+        *vectors,
+        scratch=(pltpu.VMEM((small, feats), WIDE), pltpu.VMEM((padded, feats), LOW)),
+    )[0]
+
+
+def join_halves(mine, other, rank, groups):
+    rows = mine.shape[0] // groups
+    outs = [((2 * mine.shape[0], mine.shape[1]), mine.dtype)]
+
+    def kernel(rank_ref, mine_ref, other_ref, out_ref):
+        for i in range(groups):
+            first = pl.multiple_of((2 * i + rank_ref[0]) * rows, 16)
+            second = pl.multiple_of((2 * i + 1 - rank_ref[0]) * rows, 16)
+            out_ref[pl.ds(first, rows), :] = mine_ref[i * rows : (i + 1) * rows, :]
+            out_ref[pl.ds(second, rows), :] = other_ref[i * rows : (i + 1) * rows, :]
+
+    return local_call(kernel, outs, rank.reshape(1).astype(jnp.int32), mine, other)[0]
+
+
+def mlp_blocks(moved, rows, used):
+    sources = moved.shape[0]
+
+    def kernel(_, moved_ref, out_ref):
+        for i in range(sources):
+            at = slice(i * rows, (i + 1) * rows)
+            out_ref[at, :used] = moved_ref[i, :rows, :used]
+            out_ref[at, used : 2 * used] = moved_ref[i, rows:, :used]
+            out_ref[at, 2 * used :] = jnp.zeros((rows, out_ref.shape[1] - 2 * used), LOW)
+
+    outs = [((sources * rows, -(-2 * used // 128) * 128), moved.dtype)]
+    return local_call(kernel, outs, jnp.zeros((1,), jnp.int32), moved)[0]
+
+
+def mlp_join(mine, other, rank, groups, used, paired):
+    if not paired:
+        return mine[:, :used], mine[:, used : 2 * used]
+    rows = mine.shape[0] // groups
+
+    def kernel(rank_ref, mine_ref, other_ref, *out_refs):
+        for i in range(groups):
+            at = slice(i * rows, (i + 1) * rows)
+            first = pl.multiple_of((2 * i + rank_ref[0]) * rows, 16)
+            second = pl.multiple_of((2 * i + 1 - rank_ref[0]) * rows, 16)
+            for k, out_ref in enumerate(out_refs):
+                lanes = slice(k * used, (k + 1) * used)
+                out_ref[pl.ds(first, rows), :] = mine_ref[at, lanes]
+                out_ref[pl.ds(second, rows), :] = other_ref[at, lanes]
+
+    outs = [((2 * mine.shape[0], used), mine.dtype)] * 2
+    return local_call(kernel, outs, rank.reshape(1).astype(jnp.int32), mine, other)
+
+
+def rows_backward(part_ref, unit_ref, inv_ref, gain_ref):
+    total = part_ref[0].astype(WIDE)
+    for i in range(1, part_ref.shape[0]):
+        total = total + part_ref[i].astype(WIDE)
+    unit = unit_ref[...]
+    return total, unit, norm_backward(total, unit, inv_ref[...], gain_ref[...])
+
+
+def middle_rows(parts, unit, inv_scale, gain, cotangent):
+    sources, span, width = parts.shape
+
+    def kernel(_, part_ref, unit_ref, inv_ref, gain_ref, cot_ref, grad_ref, low_ref, sum_ref):
+        total, unit_rows, delta = rows_backward(part_ref, unit_ref, inv_ref, gain_ref)
+        grad = cot_ref[...].astype(WIDE) + delta
+        grad_ref[...] = grad
+        low = grad.astype(LOW)
+        for i in range(sources):
+            low_ref[i] = low
+        sum_ref[...] = jnp.zeros_like(sum_ref)
+        sum_ref[0:1, :] = jnp.sum(total * unit_rows, axis=0, keepdims=True)
+        sum_ref[1:2, :] = jnp.sum(total, axis=0, keepdims=True)
+        sum_ref[2:3, :] = jnp.sum(grad, axis=0, keepdims=True)
+
+    outs = [((span, width), WIDE), ((sources, span, width), LOW), ((8, width), WIDE)]
+    return local_call(
+        kernel, outs, jnp.zeros((1,), jnp.int32), parts, unit, inv_scale, gain, cotangent
+    )
+
+
+def final_rows(parts, unit, inv_scale, gain, grad, sums, hidden, outputs, joint):
+    sources, span, width = parts.shape
+    feats = width // sources
+    count = 5
+    extra = hidden.shape[0]
+    small = -(-3 * (count + extra) // 16) * 16
+    half, trio = joint.shape[1:]
+
+    def kernel(
+        _, part_ref, unit_ref, inv_ref, gain_ref, grad_ref, sum_ref, hidden_ref, out_rows_ref,
+        joint_ref, out_ref, all_ref, wide_ref
+    ):
+        total, unit_rows, delta = rows_backward(part_ref, unit_ref, inv_ref, gain_ref)
+        low = (grad_ref[...] + delta).astype(LOW)
+        out_rows = out_rows_ref[...]
+        all_ref[...] = sum_ref[...]
+        all_ref[3:4, :] = jnp.sum(total * unit_rows, axis=0, keepdims=True)
+        all_ref[4:5, :] = jnp.sum(total, axis=0, keepdims=True)
+        for j in range(sources):
+            lanes = slice(j * feats, (j + 1) * feats)
+            out_ref[j, :span, :] = out_rows[:, lanes]
+            out_ref[j, span : 2 * span, :] = low[:, lanes]
+            wide_ref[...] = jnp.zeros_like(wide_ref)
+            start = 0
+            for value in (all_ref[:count, lanes], hidden_ref[...]):
+                size = value.shape[0]
+                high = value.astype(LOW).astype(WIDE)
+                middle = (value - high).astype(LOW).astype(WIDE)
+                for piece in (high, middle, value - high - middle):
+                    wide_ref[start : start + size, :] = piece
+                    start += size
+            out_ref[j, 2 * span : 2 * span + small, :] = wide_ref[...].astype(LOW)
+            out_ref[j, 2 * span + small :, :trio] = joint_ref[j]
+            out_ref[j, 2 * span + small :, trio:] = jnp.zeros((half, feats - trio), LOW)
+
+    outs = [((sources, 2 * span + small + half, feats), LOW)]
+    arrays = (parts, unit, inv_scale, gain, grad, sums, hidden, outputs, joint)
+    scratch = (pltpu.VMEM((8, width), WIDE), pltpu.VMEM((small, feats), WIDE))
+    packed = local_call(kernel, outs, jnp.zeros((1,), jnp.int32), *arrays, scratch=scratch)[0]
+    return packed, 2 * span + small
 
 
 def make_body(n_dp, n_row, n_col):
@@ -200,10 +398,8 @@
             mine = half_of(value, rank, 1) if paired else value
             return [mine[j * parts : (j + 1) * parts].T for j in range(n_row)]
 
-        def weight_join(moved):
-            if paired:
-                moved = join(moved, dp_swap(moved), rank, 1)
-            return moved.reshape(-1, moved.shape[-1])
+        def dp_rows(moved, groups):
+            return join_halves(moved, dp_swap(moved), rank, groups) if paired else moved
 
         def grad_start(blocks):
             low = blocks.astype(LOW)
@@ -218,45 +414,51 @@
         def grad_join(moved):
             return join(moved, dp_swap(moved), rank, 1) if paired else moved
 
-        def sum_rows(product, rows, late=None):
+        def sum_start(product, rows):
             size = padded // 2
             got = col_swap(product(rows[size:]).astype(LOW), masks[0])
             total = product(rows[:size]) + got.astype(WIDE)
             for mask in masks[1:]:
                 size //= 2
                 total = total[:size] + col_swap(total[size:].astype(LOW), mask).astype(WIDE)
-            total = total.astype(LOW)
-            if late is not None:
-                total = after(total, late)
-            parts = row_exchange(total.reshape(n_row, span, width))
-            return jnp.sum(parts.astype(WIDE), axis=0)
-
-        def feature_blocks(rows):
-            return [rows[:, j * feats : (j + 1) * feats] for j in range(n_row)]
-
-        small = split_wide(
-            jnp.stack([pre_gain, pre_shift, merge_bias, mid_gain, mid_shift, reduce_bias])
-        )
-        joint_wide = weight_move(joint_weight, trio)
-        first = row_exchange(
-            pack(everywhere(own_block(inputs)), everywhere(small), fit_lanes(joint_wide))
-        )
-        pieces = [
-            everywhere(own_block(cotangent)),
-            everywhere(half_of(merge_weight, rank, 0) if paired else merge_weight),
-            fit_lanes(weight_move(expand_weight, units)),
-            fit_lanes(weight_move_rows(reduce_weight, units)),
-        ]
-        second = row_exchange(after(pack(*pieces), first))
-        ends = [sum(height(piece) for piece in pieces[:i]) for i in range(5)]
-        cot_moved, merge_moved, expand_moved, reduce_moved = [
-            second[:, low:high] for low, high in zip(ends, ends[1:])
-        ]
-        inner = block + small.shape[0]
-        small_full = merge_wide(lanes(first[:, block:inner]))
+            return total.astype(LOW).reshape(n_row, span, width)
+
+        vectors = (pre_gain, pre_shift, merge_bias, mid_gain, mid_shift, reduce_bias)
+        small = -(-3 * len(vectors) // 16) * 16
+        first_out = pack_first(
+            inputs, joint_weight, vectors, col, rank, block, padded, trio, 2 if paired else 1
+        )
+        first = row_exchange(first_out)
+        cot_in, merge_in, expand_in, reduce_in = lax.optimization_barrier(
+            (cotangent, merge_weight, expand_weight, reduce_weight, first_out)
+        )[:4]
+        second_out = pack(
+            everywhere(own_block(cot_in)),
+            everywhere(half_of(merge_in, rank, 0) if paired else merge_in),
+        )
+        third_out = pack(
+            fit_lanes(weight_move(expand_in, units)), fit_lanes(weight_move_rows(reduce_in, units))
+        )
+        second = row_exchange(after(second_out, first))
+        third = row_exchange(after(third_out, second))
+        inner = block + small
+        half = feats // 2 if paired else feats
+        x_rows, small_full, joint_own = split_blocks(
+            first,
+            (
+                (0, block, feats, True),
+                (block, small, feats, True),
+                (inner, half, trio, False),
+            ),
+        )
+        small_full = merge_wide(small_full[:18])
         gain1, shift1, bias1, gain2, shift2, bias2 = [small_full[i : i + 1] for i in range(6)]
-        x_full = col_gather(lanes(first[:, :block]))
-        joint_own = weight_join(first[:, inner:, :trio])
+        x_full = col_gather(x_rows)
+        joint_own = dp_rows(joint_own, n_row)
+        cot_rows, merge_rows = split_blocks(
+            second, ((0, block, feats, True), (block, half, feats, True))
+        )
+        mlp_part = mlp_blocks(third, half, units)
 
         residual = x_full.astype(WIDE)
         unit1, inv1 = norm_forward(residual)
@@ -277,15 +479,16 @@
             keep = keep * (order[:, None] // SEQ == order[None] // SEQ).astype(WIDE)
         own_context, totals = attend(query_rows, key_rows, value_rows, factor, keep)
 
-        cot_full = col_gather(lanes(cot_moved))
-        merge_rows = lanes(merge_moved)
-        if paired:
-            merge_rows = join(merge_rows, dp_swap(merge_rows), rank, 0)
-        merge_full = col_gather(merge_rows)
-        expand_own = weight_join(expand_moved[..., :units])
-        reduce_own = weight_join(reduce_moved[..., :units])
-
-        group_context = row_gather(after(own_context, second)).reshape(n_row * head_size, padded)
+        merge_other = dp_swap(merge_rows) if paired else merge_rows
+        merge_own = join_halves(merge_rows, merge_other, rank, 1) if paired else merge_rows
+        merge_full = col_gather(merge_own)
+        cot_full = col_gather(cot_rows)
+        mlp_other = dp_swap(mlp_part) if paired else mlp_part
+
+        group_context = row_gather(after(own_context, third, merge_other)).reshape(n_row * head_size, padded)
+        expand_own, reduce_own = mlp_join(
+            mlp_part, after(mlp_other, group_context), rank, n_row, units, paired
+        )
         context_full = jnp.concatenate(
             [
                 align_lanes(part, offset, near) if offset else part
@@ -302,16 +505,22 @@
         value, slope = gelu_pair(hidden_pre)
         active = value.astype(LOW)
         hidden_grad = (dot(cot_full, reduce_own, 1, 0) * slope).astype(LOW)
-        normed2_grad = sum_rows(lambda rows: dot(rows, expand_own, 1, 1), hidden_grad)
-
-        unit2_own = own_rows(unit2)
-        cot_own = own_rows(cot_full).astype(WIDE)
-        mixed_grad = cot_own + norm_backward(normed2_grad, unit2_own, own_rows(inv2), gain2)
-        mixed_block = row_gather(mixed_grad.astype(LOW)).reshape(block, width)
+        normed2_total = sum_start(lambda rows: dot(rows, expand_own, 1, 1), hidden_grad)
+        out_total = sum_start(
+            lambda rows: dot(rows, reduce_own, 1, 1), after(active, normed2_total)
+        )
+
+        mixed_grad, mixed_low, sums = middle_rows(
+            row_exchange(normed2_total),
+            own_rows(unit2),
+            own_rows(inv2),
+            gain2,
+            own_rows(cot_full),
+        )
+        mixed_block = row_exchange(mixed_low).reshape(block, width)
         mixed_low = col_gather(mixed_block)
-        out_rows = sum_rows(
-            lambda rows: dot(rows, reduce_own, 1, 1), after(active, normed2_grad), mixed_block
-        )
+        out_parts = row_exchange(after(out_total, mixed_block))
+        out_rows = jnp.sum(out_parts.astype(WIDE), axis=0)
         out_rows = (own_rows(mixed1) + out_rows + bias2).astype(LOW)
 
         expand_grad = dot(normed2, hidden_grad, 0, 0).reshape(n_row, feats, units)
@@ -319,7 +528,10 @@
         mlp_grad = grad_start(
             jnp.concatenate([expand_grad.astype(LOW), reduce_grad.astype(LOW)], axis=2)
         )
-        mlp_grad = grad_join(row_exchange(after(mlp_grad, out_rows)))
+        head_rows = lax.dynamic_slice_in_dim(merge_own, row * head_size, head_size, 0)
+        context_grad = dot(mixed_low, head_rows, 1, 1).astype(LOW)
+        mlp_moved = row_exchange(after(mlp_grad, context_grad, out_parts))
+        mlp_grad = grad_join(mlp_moved)
         expand_weight_grad = (
             lanes(mlp_grad[..., :units]).astype(WIDE)
         )
@@ -327,8 +539,6 @@
             jnp.concatenate([mlp_grad[j, :, units:].T for j in range(n_row)]).astype(WIDE)
         )
 
-        head_rows = lax.dynamic_slice_in_dim(merge_full, row * head_size, head_size, 0)
-        context_grad = dot(mixed_low, head_rows, 1, 1).astype(LOW)
         query_grad, key_grad, value_grad = attend_back(
             query_rows, key_rows, value_rows, own_context, totals, context_grad, factor, keep
         )
@@ -336,9 +546,7 @@
         joint_bias_grad = jnp.concatenate(
             [jnp.sum(query_grad, axis=0), jnp.sum(value_grad, axis=0)]
         )
-        normed1_grad = sum_rows(lambda rows: dot(rows, joint_own, 1, 1), joint_grad)
-        unit1_own = own_rows(unit1)
-        inputs_rows = mixed_grad + norm_backward(normed1_grad, unit1_own, own_rows(inv1), gain1)
+        normed1_parts = row_exchange(sum_start(lambda rows: dot(rows, joint_own, 1, 1), joint_grad))
 
         joint_blocks = grad_start(dot(normed1, joint_grad, 0, 0).reshape(n_row, feats, trio))
         own_mixed = lax.dynamic_slice_in_dim(mixed_low, row * feats, feats, 1)
@@ -349,35 +557,26 @@
         elif n_dp > 1:
             merge_weight_grad = lax.psum(merge_weight_grad, "dp")
 
-        sums = jnp.stack(
-            [
-                jnp.sum(normed2_grad * unit2_own, axis=0),
-                jnp.sum(normed2_grad, axis=0),
-                jnp.sum(mixed_grad, axis=0),
-                jnp.sum(normed1_grad * unit1_own, axis=0),
-                jnp.sum(normed1_grad, axis=0),
-            ]
-        )
         hidden_sum = jnp.pad(
-            jnp.sum(hidden_grad, axis=0, dtype=WIDE), (0, -(-units // feats) * feats - units)
+            jnp.sum(hidden_grad, axis=0, dtype=WIDE), (0, -units % feats)
         ).reshape(-1, feats)
-        hidden_rows = hidden_sum.shape[0]
-        hidden_low = split_wide(hidden_sum)
-        sums_low = [jnp.concatenate([p, hidden_low]) for p in feature_blocks(split_wide(sums))]
-        final = row_exchange(
-            pack(
-                feature_blocks(out_rows),
-                feature_blocks(inputs_rows.astype(LOW)),
-                sums_low,
-                fit_lanes([joint_blocks[j] for j in range(n_row)]),
-            )
-        )
-        ends = 2 * span + height(sums_low)
+        packed, ends = final_rows(
+            normed1_parts,
+            own_rows(unit1),
+            own_rows(inv1),
+            gain1,
+            mixed_grad,
+            sums,
+            hidden_sum,
+            out_rows,
+            joint_blocks,
+        )
+        final = row_exchange(packed)
         vectors = final[:, 2 * span : ends]
         joint_blocks = grad_join(final[:, ends:, :trio])
         joint_weight_grad = lanes(joint_blocks).astype(WIDE)
         partial = jnp.sum(merge_wide(vectors[:, :15]), axis=0)
-        hidden_all = merge_wide(vectors[:, 15:]).reshape(n_row, -1)[:, :units].reshape(-1)
+        hidden_all = merge_wide(vectors[:, 15 : 15 + 3 * hidden_sum.shape[0]]).reshape(n_row, -1)[:, :units].reshape(-1)
         local = jnp.concatenate([hidden_all, joint_bias_grad])
         local = jnp.pad(local, (0, -local.shape[0] % feats)).reshape(-1, feats)
         local = jnp.concatenate(

time: 371 us -> 340 us (0.916); the launches traced: 364 us -> 338 us
  Pallas kernels: 0 us -> 21.9 us
  local copies, waits for them, and re-layouts: 69.2 us -> 49.6 us
  other arithmetic: 48.6 us -> 32.1 us
  starting transfers between devices: 65.1 us -> 58.4 us
  matrix products: 37.6 us -> 33.8 us
    pallas_call x0 -> x9, Pallas kernels: none -> 21.9 us  [local_call(): pl.pallas_call(kernel, out_shape=[jax.ShapeDtypeStruct(shape, kind) for s...]
    unnamed x154 -> x167, local copies, waits for them, and re-layouts: 26.7 us -> 18.1 us
    dynamic_slice x0 -> x7, local copies, waits for them, and re-layouts: none -> 6.34 us  [own_rows(): return lax.dynamic_slice_in_dim(value, row * span, span, 0)]
    concatenate x8 -> x1, local copies, waits for them, and re-layouts: 5.91 us -> 0.2 us  [pack(): jnp.concatenate(group, axis=0)]
    another operation x14 -> x4, local copies, waits for them, and re-layouts: 6.14 us -> 0.52 us  [the longest x7 4.13 us: body(): jnp.stack([pre_gain, pre_shift, merge_bias, mid_gain, mid_shift, reduce_b...]
    concatenate x5 -> x1, local copies, waits for them, and re-layouts: 6.08 us -> 0.57 us  [lanes(): return jnp.concatenate([blocks[i] for i in range(n_row)], axis=-1)]
    ppermute x21, starting transfers between devices: 11.4 us -> 6.23 us  [col_swap(): return lax.ppermute(value, 'col', [(i, i ^ mask) for i in range(n_col)])]
    concatenate x3 -> x1, other arithmetic: 5.95 us -> 1.42 us  [col_gather(): return jnp.concatenate(col_parts(value), axis=0)]
  transfers between devices with their start and end apart: 40 -> 40, of which waited for: 20 -> 20; matrix products, arithmetic and copies ran while one was open for 30% -> 25% of each run, Pallas kernels for 0% -> 5%
where the time goes in v1:
time: 340 us; the launch traced here: 338 us
  waiting for transfers between devices  130 us (38%)
  starting transfers between devices  58.4 us (17%)
  local copies, waits for them, and re-layouts  49.6 us (15%)
  matrix products  33.8 us (10%)
  other arithmetic  32.1 us (9%)
  Pallas kernels  21.9 us (6%)
  blocking collectives  9.75 us (3%)
    all_to_all x10, waiting for transfers between devices, row_exchange(): return lax.all_to_all(blocks, 'row', 0, 0, tiled=True)  66.7 us
    ppermute x21, waiting for transfers between devices, col_swap(): return lax.ppermute(value, 'col', [(i, i ^ mask) for i in range(n_col)])  48.8 us
    all_to_all x10, starting transfers between devices, row_exchange(): return lax.all_to_all(blocks, 'row', 0, 0, tiled=True)  43.3 us
    dot_general x21, matrix products, dot(): lax.dot_general(left, right, (((left_dim,), (right_dim,)), ((), ())), pre...  33.8 us
    pallas_call x9, Pallas kernels, local_call(): pl.pallas_call(kernel, out_shape=[jax.ShapeDtypeStruct(shape, kind) for s...  21.9 us
    unnamed x167, local copies, waits for them, and re-layouts  18.1 us
    ppermute x9, waiting for transfers between devices, dp_swap(): return lax.ppermute(value, 'dp', [(0, 1), (1, 0)])  14.8 us
    all_gather x1, blocking collectives, body(): lax.all_gather(jnp.concatenate([final[:, :2 * span].reshape(2 * block, fe...  9.75 us
  transfers between devices with their start and end apart: 40, of which 20 were waited for; matrix products, arithmetic and copies ran while one was open for 25% of the time, Pallas kernels for 5%

profile of v1, /device:TPU:0, one launch (start us, length us, event | category | flops | bytes accessed | tf_op | source)
XLA Modules:
  0.0 337.9 jit_solution(7962931694141192471)
XLA Ops:
  0.7 2.1 copy.112.input_ref
  3.3 3.2 shard_map.245
  6.5 2.3 copy.113
  8.8 6.5 %all-to-all-start = ((bf16[4,368,288]{1,2,0:T(8,128)(2,1)}), bf16[4,368,288]{1,2,0:T(8,128)(2,1)S(1)}, u32[]{:S(2)}, u32[]{:S(2)}) async-start(bf16[4,368,288]{1,2,0:T(8,128)(2,1)} %copy.113), calls=%async_computation | async-start | bytes 1769472 | tf_op jit(solution)/shard_map/all_to_all | solution.py:309
  18.6 18.9 %all-to-all-done = bf16[4,368,288]{1,2,0:T(8,128)(2,1)S(1)} async-done(((bf16[4,368,288]{1,2,0:T(8,128)(2,1)}), bf16[4,368,288]{1,2,0:T(8,128)(2,1)S(1)}, u32[]{:S(2)}, u32[]{:S(2)}) %all-to-all-start) | async-done | bytes 847904 | tf_op jit(solution)/shard_map/all_to_all | solution.py:309
  38.9 2.4 shard_map.246
  44.3 3.5 %all-to-all-start.1 = ((bf16[4,336,288]{1,2,0:T(8,128)(2,1)}), bf16[4,336,288]{1,2,0:T(8,128)(2,1)S(1)}, u32[]{:S(2)}, u32[]{:S(2)}) async-start(bf16[4,336,288]{1,2,0:T(8,128)(2,1)} %copy.117), calls=%async_computation.1 | async-start | bytes 1769472 | tf_op jit(solution)/shard_map/all_to_all | solution.py:309
  49.4 4.7 %collective-permute-done = bf16[192,1152]{1,0:T(8,128)(2,1)S(1)} collective-permute-done((bf16[192,1152]{1,0:T(8,128)(2,1)}, bf16[192,1152]{1,0:T(8,128)(2,1)S(1)}, u32[]{:S(2)}, u32[]{:S(2)}) %collective-permute-start) | collective-permute-done | bytes 442400 | tf_op jit(solution)/shard_map/ppermute | solution.py:303
  57.7 2.0 shard_map.247
  60.4 10.2 %all-to-all-done.1 = bf16[4,336,288]{1,2,0:T(8,128)(2,1)S(1)} async-done(((bf16[4,336,288]{1,2,0:T(8,128)(2,1)}), bf16[4,336,288]{1,2,0:T(8,128)(2,1)S(1)}, u32[]{:S(2)}, u32[]{:S(2)}) %all-to-all-start.1) | async-done | bytes 774176 | tf_op jit(solution)/shard_map/all_to_all | solution.py:309
  70.6 4.2 %all-to-all-start.2 = ((bf16[4,288,288]{2,1,0:T(8,128)(2,1)}), bf16[4,288,288]{2,1,0:T(8,128)(2,1)}, u32[]{:S(2)}, u32[]{:S(2)}) async-start(bf16[4,288,288]{2,1,0:T(8,128)(2,1)} %pad_maximum_fusion.2), calls=%async_computation.2 | async-start | bytes 1769472 | tf_op jit(solution)/shard_map/all_to_all | solution.py:309
  79.4 2.4 shard_map.248
  86.2 4.9 %collective-permute-done.8.other_ref = bf16[144,1152]{1,0:T(8,128)(2,1)} collective-permute-done((bf16[144,1152]{1,0:T(8,128)(2,1)}, bf16[144,1152]{1,0:T(8,128)(2,1)}, u32[]{:S(2)}, u32[]{:S(2)}) %collective-permute-start.8) | collective-permute-done | bytes 331808 | tf_op jit(solution)/shard_map/ppermute | solution.py:306
  91.1 5.7 %all-to-all-done.2.moved_ref = bf16[4,288,288]{2,1,0:T(8,128)(2,1)} async-done(((bf16[4,288,288]{2,1,0:T(8,128)(2,1)}), bf16[4,288,288]{2,1,0:T(8,128)(2,1)}, u32[]{:S(2)}, u32[]{:S(2)}) %all-to-all-start.2) | async-done | bytes 663584 | tf_op jit(solution)/shard_map/all_to_all | solution.py:309
  97.6 3.6 %all-to-all-start.3 = ((bf16[4,72,768]{2,1,0:T(8,128)(2,1)}), bf16[4,72,768]{2,1,0:T(8,128)(2,1)S(1)}, u32[]{:S(2)}, u32[]{:S(2)}) async-start(bf16[4,72,768]{2,1,0:T(8,128)(2,1)} %broadcast_in_dim.7), calls=%async_computation.3 | async-start | bytes 884736 | tf_op jit(solution)/shard_map/all_to_all | solution.py:309
  102.1 2.2 shard_map.249.mine_ref
  107.6 2.0 shard_map.251
  111.0 2.4 all-to-all-done.3
  115.7 12.0 %collective-permute-done.12 = bf16[288,1152]{1,0:T(8,128)(2,1)} collective-permute-done((bf16[288,1152]{1,0:T(8,128)(2,1)}, bf16[288,1152]{1,0:T(8,128)(2,1)}, u32[]{:S(2)}, u32[]{:S(2)}) %collective-permute-start.12) | collective-permute-done | bytes 663584 | tf_op jit(solution)/shard_map/ppermute | solution.py:303
  127.7 2.9 shard_map.250
  130.6 5.8 %collective-permute-done.9 = bf16[288,768]{1,0:T(8,128)(2,1)} collective-permute-done((bf16[288,768]{1,0:T(8,128)(2,1)S(1)}, bf16[288,768]{1,0:T(8,128)(2,1)}, u32[]{:S(2)}, u32[]{:S(2)}) %collective-permute-start.9) | collective-permute-done | bytes 442400 | tf_op jit(solution)/shard_map/ppermute | solution.py:303
  139.1 4.8 %fusion.116 = (f32[768]{0:T(1024)S(1)}, f32[768]{0:T(1024)S(1)}, f32[768,1152]{1,0:T(8,128)S(1)}) fusion(f32[1152]{0:T(1024)S(1)} %copy-done.73, bf16[288,1152]{1,0:T(8,128)(2,1)} %collective-permute-done.14, bf16[288,1152]{1,0:T(8,128)(2,1)} %collective-permute-done.13, bf16[288,1152]{1,0:T(8,128)(2,1)} %collective-permute-done.12, ...), kind=kOutput, calls=%fused_computation.255 | convolution fusion | flops 2080012800 | bytes 9742848 | tf_op jit(solution)/shard_map/dot_general | solution.py:30
  151.7 2.1 collective-permute-done.15
  155.8 12.1 %collective-permute-done.16 = bf16[192,1152]{1,0:T(8,128)(2,1)S(1)} collective-permute-done((bf16[192,1152]{1,0:T(8,128)(2,1)}, bf16[192,1152]{1,0:T(8,128)(2,1)S(1)}, u32[]{:S(2)}, u32[]{:S(2)}) %collective-permute-start.16) | collective-permute-done | bytes 442400 | tf_op jit(solution)/shard_map/ppermute | solution.py:303
  168.8 4.9 %all-to-all-start.4 = ((bf16[4,48,1152]{2,1,0:T(8,128)(2,1)}), bf16[4,48,1152]{2,1,0:T(8,128)(2,1)S(1)}, u32[]{:S(2)}, u32[]{:S(2)}) async-start(bf16[4,48,1152]{2,1,0:T(8,128)(2,1)} %bitcast.13), calls=%async_computation.4 | async-start | bytes 884736 | tf_op jit(solution)/shard_map/all_to_all | solution.py:309
  173.7 3.0 convolution_convert_fusion
  180.7 5.5 %all-to-all-done.4.part_ref = bf16[4,48,1152]{2,1,0:T(8,128)(2,1)S(1)} async-done(((bf16[4,48,1152]{2,1,0:T(8,128)(2,1)}), bf16[4,48,1152]{2,1,0:T(8,128)(2,1)S(1)}, u32[]{:S(2)}, u32[]{:S(2)}) %all-to-all-start.4) | async-done | bytes 442400 | tf_op jit(solution)/shard_map/all_to_all | solution.py:309
  186.9 2.3 shard_map.252
  189.1 3.7 %all-to-all-start.5 = ((bf16[4,48,1152]{2,1,0:T(8,128)(2,1)}), bf16[4,48,1152]{2,1,0:T(8,128)(2,1)S(1)}, u32[]{:S(2)}, u32[]{:S(2)}) async-start(bf16[4,48,1152]{2,1,0:T(8,128)(2,1)} %get-tuple-element.50), calls=%async_computation.5 | async-start | bytes 884736 | tf_op jit(solution)/shard_map/all_to_all | solution.py:309
  192.9 1.9 convert_add_fusion.1
  197.3 7.5 %all-to-all-done.5 = bf16[4,48,1152]{2,1,0:T(8,128)(2,1)S(1)} async-done(((bf16[4,48,1152]{2,1,0:T(8,128)(2,1)}), bf16[4,48,1152]{2,1,0:T(8,128)(2,1)S(1)}, u32[]{:S(2)}, u32[]{:S(2)}) %all-to-all-start.5) | async-done | bytes 442400 | tf_op jit(solution)/shard_map/all_to_all | solution.py:309
  205.4 2.7 convolution_convert_fusion.4
  208.6 3.4 %convolution_convert_fusion.3 = bf16[1152,269]{0,1:T(8,128)(2,1)} fusion(bf16[768,1152]{1,0:T(8,128)(2,1)} %constant_dynamic-update-slice_fusion, bf16[768,269]{0,1:T(8,128)(2,1)} %get-tuple-element.53), kind=kOutput, calls=%fused_computation.36 | convolution fusion | flops 476297856 | bytes 2802432 | tf_op jit(solution)/shard_map/dot_general | solution.py:30
  215.2 2.6 collective-permute-done.17
  219.7 4.5 %all-to-all-start.7 = ((bf16[4,48,1152]{2,1,0:T(8,128)(2,1)}), bf16[4,48,1152]{2,1,0:T(8,128)(2,1)}, u32[]{:S(2)}, u32[]{:S(2)}) async-start(bf16[4,48,1152]{2,1,0:T(8,128)(2,1)} %bitcast.19), calls=%async_computation.7 | async-start | bytes 884736 | tf_op jit(solution)/shard_map/all_to_all | solution.py:309
  234.8 3.0 fusion.1
  240.7 2.5 add_convert_fusion.2
  245.0 4.9 %all-to-all-start.9 = ((bf16[4,144,538]{2,1,0:T(8,128)(2,1)}), bf16[4,144,538]{2,1,0:T(8,128)(2,1)}, u32[]{:S(2)}, u32[]{:S(2)}) async-start(bf16[4,144,538]{2,1,0:T(8,128)(2,1)} %add_convert_fusion.2), calls=%async_computation.9 | async-start | bytes 1474560 | tf_op jit(solution)/shard_map/all_to_all | solution.py:309
  257.0 9.5 %collective-permute-done.21 = bf16[192,1152]{1,0:T(8,128)(2,1)} collective-permute-done((bf16[192,1152]{1,0:T(8,128)(2,1)}, bf16[192,1152]{1,0:T(8,128)(2,1)}, u32[]{:S(2)}, u32[]{:S(2)}) %collective-permute-start.21) | collective-permute-done | bytes 442400 | tf_op jit(solution)/shard_map/ppermute | solution.py:303
  266.5 2.1 fusion.36
  269.7 3.7 %all-to-all-start.6 = ((bf16[4,48,1152]{2,1,0:T(8,128)(2,1)}), bf16[4,48,1152]{2,1,0:T(8,128)(2,1)S(1)}, u32[]{:S(2)}, u32[]{:S(2)}) async-start(bf16[4,48,1152]{2,1,0:T(8,128)(2,1)} %bitcast.17), calls=%async_computation.6 | async-start | bytes 884736 | tf_op jit(solution)/shard_map/all_to_all | solution.py:309
  277.4 8.3 %all-to-all-done.6.part_ref = bf16[4,48,1152]{2,1,0:T(8,128)(2,1)S(1)} async-done(((bf16[4,48,1152]{2,1,0:T(8,128)(2,1)}), bf16[4,48,1152]{2,1,0:T(8,128)(2,1)S(1)}, u32[]{:S(2)}, u32[]{:S(2)}) %all-to-all-start.6) | async-done | bytes 442400 | tf_op jit(solution)/shard_map/all_to_all | solution.py:309
  286.4 2.6 shard_map.253
  289.0 3.8 %all-to-all-start.8 = ((bf16[4,272,288]{2,1,0:T(8,128)(2,1)}), bf16[4,272,288]{2,1,0:T(8,128)(2,1)S(1)}, u32[]{:S(2)}, u32[]{:S(2)}) async-start(bf16[4,272,288]{2,1,0:T(8,128)(2,1)} %shard_map.253), calls=%async_computation.8 | async-start | bytes 1671168 | tf_op jit(solution)/shard_map/all_to_all | solution.py:309
  295.1 4.7 %collective-permute-done.27 = bf16[288,288]{1,0:T(8,128)(2,1)S(1)} collective-permute-done((bf16[288,288]{1,0:T(8,128)(2,1)S(1)}, bf16[288,288]{1,0:T(8,128)(2,1)S(1)}, u32[]{:S(2)}, u32[]{:S(2)}) %collective-permute-start.27) | collective-permute-done | bytes 165920 | tf_op jit(solution)/shard_map/ppermute | solution.py:306
  306.1 7.1 %all-to-all-done.8 = bf16[4,272,288]{2,1,0:T(8,128)(2,1)S(1)} async-done(((bf16[4,272,288]{2,1,0:T(8,128)(2,1)}), bf16[4,272,288]{2,1,0:T(8,128)(2,1)S(1)}, u32[]{:S(2)}, u32[]{:S(2)}) %all-to-all-start.8) | async-done | bytes 626720 | tf_op jit(solution)/shard_map/all_to_all | solution.py:309
  314.4 9.8 %all-gather.1 = bf16[4,417,288]{1,2,0:T(8,128)(2,1)S(1)} all-gather(bf16[1,417,288]{1,2,0:T(8,128)(2,1)S(1)} %maximum_bitcast_fusion), channel_id=2, replica_groups=mesh['dp'=2,'row'=4,'col'=4] {'col'}, dimensions={0}, use_global_device_ids=true | all-gather | bytes 1200960 | tf_op jit(solution)/shard_map/all_gather | solution.py:585
  330.6 3.6 %collective-permute-done.25 = f32[11,288]{1,0:T(8,128)S(1)} collective-permute-done((f32[11,288]{1,0:T(8,128)S(1)}, f32[11,288]{1,0:T(8,128)S(1)}, u32[]{:S(2)}, u32[]{:S(2)}) %collective-permute-start.25) | collective-permute-done | bytes 12704 | tf_op jit(solution)/shard_map/ppermute | solution.py:306
  (341 shorter events, 105.6 us)
Async XLA Ops:
  8.8 28.7 %all-to-all-start = ((bf16[4,368,288]{1,2,0:T(8,128)(2,1)}), bf16[4,368,288]{1,2,0:T(8,128)(2,1)S(1)}, u32[]{:S(2)}, u32[]{:S(2)}) async-start(bf16[4,368,288]{1,2,0:T(8,128)(2,1)} %copy.113), calls=%async_computation | async-start | bytes 1769472 | tf_op jit(solution)/shard_map/all_to_all | solution.py:309
  41.3 18.4 %collective-permute-start.1 = (bf16[192,1152]{1,0:T(8,128)(2,1)}, bf16[192,1152]{1,0:T(8,128)(2,1)S(1)}, u32[]{:S(2)}, u32[]{:S(2)}) collective-permute-start(bf16[192,1152]{1,0:T(8,128)(2,1)} %get-tuple-element.35), channel_id=1, source_target_pairs={{0,1},{1,0},{2,3},{3,2},{4,5},{5,4},{6,7},{7,6},{8,9},{9,8},{10,11... | collective-permute-start | bytes 1327112 | tf_op jit(solution)/shard_map/ppermute | solution.py:303
  41.3 12.8 %collective-permute-start = (bf16[192,1152]{1,0:T(8,128)(2,1)}, bf16[192,1152]{1,0:T(8,128)(2,1)S(1)}, u32[]{:S(2)}, u32[]{:S(2)}) collective-permute-start(bf16[192,1152]{1,0:T(8,128)(2,1)} %get-tuple-element.35), channel_id=1, source_target_pairs={{0,2},{1,3},{2,0},{3,1},{4,6},{5,7},{6,4},{7,5},{8,10},{9,11},{10,... | collective-permute-start | bytes 1327112 | tf_op jit(solution)/shard_map/ppermute | solution.py:303
  44.3 26.3 %all-to-all-start.1 = ((bf16[4,336,288]{1,2,0:T(8,128)(2,1)}), bf16[4,336,288]{1,2,0:T(8,128)(2,1)S(1)}, u32[]{:S(2)}, u32[]{:S(2)}) async-start(bf16[4,336,288]{1,2,0:T(8,128)(2,1)} %copy.117), calls=%async_computation.1 | async-start | bytes 1769472 | tf_op jit(solution)/shard_map/all_to_all | solution.py:309
  47.9 9.1 %collective-permute-start.3 = (bf16[576,216]{1,0:T(8,128)(2,1)S(1)}, bf16[576,216]{1,0:T(8,128)(2,1)S(1)}, u32[]{:S(2)}, u32[]{:S(2)}) collective-permute-start(bf16[576,216]{1,0:T(8,128)(2,1)S(1)} %copy-done.56), channel_id=1, source_target_pairs={{0,16},{16,0},{1,17},{17,1},{2,18},{18,2},{3,19},{19,3},{4,20},{20... | collective-permute-start | bytes 746504 | tf_op jit(solution)/shard_map/ppermute | solution.py:306
  54.1 20.8 %copy-start.30 = (bf16[192,1152]{1,0:T(8,128)(2,1)}, bf16[192,1152]{1,0:T(8,128)(2,1)S(1)}, u32[]{:S(2)}) copy-start(bf16[192,1152]{1,0:T(8,128)(2,1)S(1)} %collective-permute-done) | copy-start | bytes 1327108
  54.1 5.6 %collective-permute-start.2 = (bf16[192,1152]{1,0:T(8,128)(2,1)S(1)}, bf16[192,1152]{1,0:T(8,128)(2,1)S(1)}, u32[]{:S(2)}, u32[]{:S(2)}) collective-permute-start(bf16[192,1152]{1,0:T(8,128)(2,1)S(1)} %collective-permute-done), channel_id=1, source_target_pairs={{0,1},{1,0},{2,3},{3,2},{4,5},{5,4},{6,7},{7,6},{8,9},{9,8},{10,11... | collective-permute-start | bytes 1327112 | tf_op jit(solution)/shard_map/ppermute | solution.py:303
  70.6 26.2 %all-to-all-start.2 = ((bf16[4,288,288]{2,1,0:T(8,128)(2,1)}), bf16[4,288,288]{2,1,0:T(8,128)(2,1)}, u32[]{:S(2)}, u32[]{:S(2)}) async-start(bf16[4,288,288]{2,1,0:T(8,128)(2,1)} %pad_maximum_fusion.2), calls=%async_computation.2 | async-start | bytes 1769472 | tf_op jit(solution)/shard_map/all_to_all | solution.py:309
  81.8 9.3 %collective-permute-start.8 = (bf16[144,1152]{1,0:T(8,128)(2,1)}, bf16[144,1152]{1,0:T(8,128)(2,1)}, u32[]{:S(2)}, u32[]{:S(2)}) collective-permute-start(bf16[144,1152]{1,0:T(8,128)(2,1)} %get-tuple-element.45.mine_ref), channel_id=1, source_target_pairs={{0,16},{16,0},{1,17},{17,1},{2,18},{18,2},{3,19},{19,3},{4,20},{20... | collective-permute-start | bytes 995336 | tf_op jit(solution)/shard_map/ppermute | solution.py:306
  84.4 25.7 %collective-permute-start.4 = (bf16[192,1152]{1,0:T(8,128)(2,1)}, bf16[192,1152]{1,0:T(8,128)(2,1)S(1)}, u32[]{:S(2)}, u32[]{:S(2)}) collective-permute-start(bf16[192,1152]{1,0:T(8,128)(2,1)} %get-tuple-element.41), channel_id=1, source_target_pairs={{0,2},{1,3},{2,0},{3,1},{4,6},{5,7},{6,4},{7,5},{8,10},{9,11},{10,... | collective-permute-start | bytes 1327112 | tf_op jit(solution)/shard_map/ppermute | solution.py:303
  97.6 15.7 %all-to-all-start.3 = ((bf16[4,72,768]{2,1,0:T(8,128)(2,1)}), bf16[4,72,768]{2,1,0:T(8,128)(2,1)S(1)}, u32[]{:S(2)}, u32[]{:S(2)}) async-start(bf16[4,72,768]{2,1,0:T(8,128)(2,1)} %broadcast_in_dim.7), calls=%async_computation.3 | async-start | bytes 884736 | tf_op jit(solution)/shard_map/all_to_all | solution.py:309
  102.1 11.3 %collective-permute-start.5 = (bf16[192,1152]{1,0:T(8,128)(2,1)}, bf16[192,1152]{1,0:T(8,128)(2,1)S(1)}, u32[]{:S(2)}, u32[]{:S(2)}) collective-permute-start(bf16[192,1152]{1,0:T(8,128)(2,1)} %get-tuple-element.41), channel_id=1, source_target_pairs={{0,1},{1,0},{2,3},{3,2},{4,5},{5,4},{6,7},{7,6},{8,9},{9,8},{10,11... | collective-permute-start | bytes 1327112 | tf_op jit(solution)/shard_map/ppermute | solution.py:303
  104.3 23.4 %collective-permute-start.7 = (bf16[576,640]{1,0:T(8,128)(2,1)}, bf16[576,640]{1,0:T(8,128)(2,1)}, u32[]{:S(2)}, u32[]{:S(2)}) collective-permute-start(bf16[576,640]{1,0:T(8,128)(2,1)} %shard_map.249.mine_ref), channel_id=1, source_target_pairs={{0,16},{16,0},{1,17},{17,1},{2,18},{18,2},{3,19},{19,3},{4,20},{20... | collective-permute-start | bytes 2211848 | tf_op jit(solution)/shard_map/ppermute | solution.py:306
  109.6 18.1 %collective-permute-start.12 = (bf16[288,1152]{1,0:T(8,128)(2,1)}, bf16[288,1152]{1,0:T(8,128)(2,1)}, u32[]{:S(2)}, u32[]{:S(2)}) collective-permute-start(bf16[288,1152]{1,0:T(8,128)(2,1)} %shard_map.251), channel_id=1, source_target_pairs={{0,2},{1,3},{2,0},{3,1},{4,6},{5,7},{6,4},{7,5},{8,10},{9,11},{10,... | collective-permute-start | bytes 1990664 | tf_op jit(solution)/shard_map/ppermute | solution.py:303
  110.1 4.6 %collective-permute-start.6 = (bf16[192,1152]{1,0:T(8,128)(2,1)S(1)}, bf16[192,1152]{1,0:T(8,128)(2,1)S(1)}, u32[]{:S(2)}, u32[]{:S(2)}) collective-permute-start(bf16[192,1152]{1,0:T(8,128)(2,1)S(1)} %collective-permute-done.4), channel_id=1, source_target_pairs={{0,1},{1,0},{2,3},{3,2},{4,5},{5,4},{6,7},{7,6},{8,9},{9,8},{10,11... | collective-permute-start | bytes 1327112 | tf_op jit(solution)/shard_map/ppermute | solution.py:303
  113.4 25.7 %copy-start.18 = (bf16[4,72,768]{2,1,0:T(8,128)(2,1)}, bf16[4,72,768]{2,1,0:T(8,128)(2,1)S(1)}, u32[]{:S(2)}) copy-start(bf16[4,72,768]{2,1,0:T(8,128)(2,1)S(1)} %all-to-all-done.3) | copy-start | bytes 1327108
  113.4 23.1 %collective-permute-start.10 = (bf16[288,768]{1,0:T(8,128)(2,1)S(1)}, bf16[288,768]{1,0:T(8,128)(2,1)}, u32[]{:S(2)}, u32[]{:S(2)}) collective-permute-start(bf16[288,768]{1,0:T(8,128)(2,1)S(1)} %bitcast.114), channel_id=1, source_target_pairs={{0,1},{1,0},{2,3},{3,2},{4,5},{5,4},{6,7},{7,6},{8,9},{9,8},{10,11... | collective-permute-start | bytes 1327112 | tf_op jit(solution)/shard_map/ppermute | solution.py:303
  113.4 23.1 %collective-permute-start.9 = (bf16[288,768]{1,0:T(8,128)(2,1)S(1)}, bf16[288,768]{1,0:T(8,128)(2,1)}, u32[]{:S(2)}, u32[]{:S(2)}) collective-permute-start(bf16[288,768]{1,0:T(8,128)(2,1)S(1)} %bitcast.115), channel_id=1, source_target_pairs={{0,2},{1,3},{2,0},{3,1},{4,6},{5,7},{6,4},{7,5},{8,10},{9,11},{10,... | collective-permute-start | bytes 1327112 | tf_op jit(solution)/shard_map/ppermute | solution.py:303
  114.7 24.3 %collective-permute-start.13 = (bf16[288,1152]{1,0:T(8,128)(2,1)}, bf16[288,1152]{1,0:T(8,128)(2,1)}, u32[]{:S(2)}, u32[]{:S(2)}) collective-permute-start(bf16[288,1152]{1,0:T(8,128)(2,1)} %shard_map.251), channel_id=1, source_target_pairs={{0,1},{1,0},{2,3},{3,2},{4,5},{5,4},{6,7},{7,6},{8,9},{9,8},{10,11... | collective-permute-start | bytes 1990664 | tf_op jit(solution)/shard_map/ppermute | solution.py:303
  115.7 23.4 %copy-start.23 = (bf16[192,1152]{1,0:T(8,128)(2,1)S(1)}, bf16[192,1152]{1,0:T(8,128)(2,1)}, u32[]{:S(2)}) copy-start(bf16[192,1152]{1,0:T(8,128)(2,1)} %get-tuple-element.35) | copy-start | bytes 1327108
  115.7 23.4 %copy-start.27 = (bf16[192,1152]{1,0:T(8,128)(2,1)S(1)}, bf16[192,1152]{1,0:T(8,128)(2,1)}, u32[]{:S(2)}) copy-start(bf16[192,1152]{1,0:T(8,128)(2,1)} %copy-done.26) | copy-start | bytes 1327108
  115.7 23.4 %copy-start.31 = (bf16[192,1152]{1,0:T(8,128)(2,1)S(1)}, bf16[192,1152]{1,0:T(8,128)(2,1)}, u32[]{:S(2)}) copy-start(bf16[192,1152]{1,0:T(8,128)(2,1)} %copy-done.30) | copy-start | bytes 1327108
  115.7 23.4 %copy-start.35 = (bf16[192,1152]{1,0:T(8,128)(2,1)S(1)}, bf16[192,1152]{1,0:T(8,128)(2,1)}, u32[]{:S(2)}) copy-start(bf16[192,1152]{1,0:T(8,128)(2,1)} %copy-done.34) | copy-start | bytes 1327108
  115.7 23.4 %copy-start.73 = (f32[1152]{0:T(1024)S(1)}, f32[1152]{0:T(1024)}, u32[]{:S(2)}) copy-start(f32[1152]{0:T(1024)} %get-tuple-element.134) | copy-start | bytes 13828
  127.7 11.3 %collective-permute-start.14 = (bf16[288,1152]{1,0:T(8,128)(2,1)}, bf16[288,1152]{1,0:T(8,128)(2,1)}, u32[]{:S(2)}, u32[]{:S(2)}) collective-permute-start(bf16[288,1152]{1,0:T(8,128)(2,1)} %collective-permute-done.12), channel_id=1, source_target_pairs={{0,1},{1,0},{2,3},{3,2},{4,5},{5,4},{6,7},{7,6},{8,9},{9,8},{10,11... | collective-permute-start | bytes 1990664 | tf_op jit(solution)/shard_map/ppermute | solution.py:303
  136.5 2.4 collective-permute-start.11
  151.2 2.6 collective-permute-start.15
  155.3 12.7 %collective-permute-start.16 = (bf16[192,1152]{1,0:T(8,128)(2,1)}, bf16[192,1152]{1,0:T(8,128)(2,1)S(1)}, u32[]{:S(2)}, u32[]{:S(2)}) collective-permute-start(bf16[192,1152]{1,0:T(8,128)(2,1)} %slice.560), channel_id=1, source_target_pairs={{0,2},{1,3},{2,0},{3,1},{4,6},{5,7},{6,4},{7,5},{8,10},{9,11},{10,... | collective-permute-start | bytes 1327112 | tf_op jit(solution)/shard_map/ppermute | solution.py:303
  168.8 17.3 %all-to-all-start.4 = ((bf16[4,48,1152]{2,1,0:T(8,128)(2,1)}), bf16[4,48,1152]{2,1,0:T(8,128)(2,1)S(1)}, u32[]{:S(2)}, u32[]{:S(2)}) async-start(bf16[4,48,1152]{2,1,0:T(8,128)(2,1)} %bitcast.13), calls=%async_computation.4 | async-start | bytes 884736 | tf_op jit(solution)/shard_map/all_to_all | solution.py:309
  173.7 19.2 %copy-start.51 = (bf16[768,269]{0,1:T(8,128)(2,1)S(1)}, bf16[768,269]{0,1:T(8,128)(2,1)}, u32[]{:S(2)}) copy-start(bf16[768,269]{0,1:T(8,128)(2,1)} %get-tuple-element.53) | copy-start | bytes 1239556
  176.7 16.1 %collective-permute-start.22 = (bf16[384,1152]{1,0:T(8,128)(2,1)}, bf16[384,1152]{1,0:T(8,128)(2,1)}, u32[]{:S(2)}, u32[]{:S(2)}) collective-permute-start(bf16[384,1152]{1,0:T(8,128)(2,1)} %convolution_convert_fusion), channel_id=1, source_target_pairs={{0,1},{1,0},{2,3},{3,2},{4,5},{5,4},{6,7},{7,6},{8,9},{9,8},{10,11... | collective-permute-start | bytes 2654216 | tf_op jit(solution)/shard_map/ppermute | solution.py:303
  189.1 15.7 %all-to-all-start.5 = ((bf16[4,48,1152]{2,1,0:T(8,128)(2,1)}), bf16[4,48,1152]{2,1,0:T(8,128)(2,1)S(1)}, u32[]{:S(2)}, u32[]{:S(2)}) async-start(bf16[4,48,1152]{2,1,0:T(8,128)(2,1)} %get-tuple-element.50), calls=%async_computation.5 | async-start | bytes 884736 | tf_op jit(solution)/shard_map/all_to_all | solution.py:309
  196.8 21.0 %collective-permute-start.23 = (bf16[192,1152]{1,0:T(8,128)(2,1)}, bf16[192,1152]{1,0:T(8,128)(2,1)}, u32[]{:S(2)}, u32[]{:S(2)}) collective-permute-start(bf16[192,1152]{1,0:T(8,128)(2,1)} %slice.558), channel_id=1, source_target_pairs={{0,2},{1,3},{2,0},{3,1},{4,6},{5,7},{6,4},{7,5},{8,10},{9,11},{10,... | collective-permute-start | bytes 1327112 | tf_op jit(solution)/shard_map/ppermute | solution.py:303
  204.9 12.9 %collective-permute-start.17 = (bf16[192,1152]{1,0:T(8,128)(2,1)S(1)}, bf16[192,1152]{1,0:T(8,128)(2,1)}, u32[]{:S(2)}, u32[]{:S(2)}) collective-permute-start(bf16[192,1152]{1,0:T(8,128)(2,1)S(1)} %bitcast.118), channel_id=1, source_target_pairs={{0,2},{1,3},{2,0},{3,1},{4,6},{5,7},{6,4},{7,5},{8,10},{9,11},{10,... | collective-permute-start | bytes 1327112 | tf_op jit(solution)/shard_map/ppermute | solution.py:303
  214.6 26.1 %collective-permute-start.28 = (bf16[4,144,538]{2,1,0:T(8,128)(2,1)}, bf16[4,144,538]{2,1,0:T(8,128)(2,1)}, u32[]{:S(2)}, u32[]{:S(2)}) collective-permute-start(bf16[4,144,538]{2,1,0:T(8,128)(2,1)} %fusion.43), channel_id=1, source_target_pairs={{0,16},{16,0},{1,17},{17,1},{2,18},{18,2},{3,19},{19,3},{4,20},{20... | collective-permute-start | bytes 1859336 | tf_op jit(solution)/shard_map/ppermute | solution.py:306
  215.2 9.1 %collective-permute-start.18 = (bf16[192,1152]{1,0:T(8,128)(2,1)S(1)}, bf16[192,1152]{1,0:T(8,128)(2,1)S(1)}, u32[]{:S(2)}, u32[]{:S(2)}) collective-permute-start(bf16[192,1152]{1,0:T(8,128)(2,1)S(1)} %bitcast.119), channel_id=1, source_target_pairs={{0,1},{1,0},{2,3},{3,2},{4,5},{5,4},{6,7},{7,6},{8,9},{9,8},{10,11... | collective-permute-start | bytes 1327112 | tf_op jit(solution)/shard_map/ppermute | solution.py:303
  217.8 7.2 %collective-permute-start.19 = (bf16[192,1152]{1,0:T(8,128)(2,1)}, bf16[192,1152]{1,0:T(8,128)(2,1)}, u32[]{:S(2)}, u32[]{:S(2)}) collective-permute-start(bf16[192,1152]{1,0:T(8,128)(2,1)} %collective-permute-done.17), channel_id=1, source_target_pairs={{0,1},{1,0},{2,3},{3,2},{4,5},{5,4},{6,7},{7,6},{8,9},{9,8},{10,11... | collective-permute-start | bytes 1327112 | tf_op jit(solution)/shard_map/ppermute | solution.py:303
  219.7 23.5 %all-to-all-start.7 = ((bf16[4,48,1152]{2,1,0:T(8,128)(2,1)}), bf16[4,48,1152]{2,1,0:T(8,128)(2,1)}, u32[]{:S(2)}, u32[]{:S(2)}) async-start(bf16[4,48,1152]{2,1,0:T(8,128)(2,1)} %bitcast.19), calls=%async_computation.7 | async-start | bytes 884736 | tf_op jit(solution)/shard_map/all_to_all | solution.py:309
  234.6 15.4 %collective-permute-start.20 = (bf16[384,1152]{1,0:T(8,128)(2,1)}, bf16[384,1152]{1,0:T(8,128)(2,1)}, u32[]{:S(2)}, u32[]{:S(2)}) collective-permute-start(bf16[384,1152]{1,0:T(8,128)(2,1)} %convolution_convert_fusion.2), channel_id=1, source_target_pairs={{0,1},{1,0},{2,3},{3,2},{4,5},{5,4},{6,7},{7,6},{8,9},{9,8},{10,11... | collective-permute-start | bytes 2654216 | tf_op jit(solution)/shard_map/ppermute | solution.py:303
  245.0 24.7 %all-to-all-start.9 = ((bf16[4,144,538]{2,1,0:T(8,128)(2,1)}), bf16[4,144,538]{2,1,0:T(8,128)(2,1)}, u32[]{:S(2)}, u32[]{:S(2)}) async-start(bf16[4,144,538]{2,1,0:T(8,128)(2,1)} %add_convert_fusion.2), calls=%async_computation.9 | async-start | bytes 1474560 | tf_op jit(solution)/shard_map/all_to_all | solution.py:309
  253.9 12.6 %collective-permute-start.21 = (bf16[192,1152]{1,0:T(8,128)(2,1)}, bf16[192,1152]{1,0:T(8,128)(2,1)}, u32[]{:S(2)}, u32[]{:S(2)}) collective-permute-start(bf16[192,1152]{1,0:T(8,128)(2,1)} %slice.559), channel_id=1, source_target_pairs={{0,2},{1,3},{2,0},{3,1},{4,6},{5,7},{6,4},{7,5},{8,10},{9,11},{10,... | collective-permute-start | bytes 1327112 | tf_op jit(solution)/shard_map/ppermute | solution.py:303
  256.4 18.6 %collective-permute-start.24 = (bf16[4,144,216]{2,1,0:T(8,128)(2,1)}, bf16[4,144,216]{2,1,0:T(8,128)(2,1)}, u32[]{:S(2)}, u32[]{:S(2)}) collective-permute-start(bf16[4,144,216]{2,1,0:T(8,128)(2,1)} %constant_dynamic-slice_fusion), channel_id=1, source_target_pairs={{0,16},{16,0},{1,17},{17,1},{2,18},{18,2},{3,19},{19,3},{4,20},{20... | collective-permute-start | bytes 746504 | tf_op jit(solution)/shard_map/ppermute | solution.py:306
  269.7 16.0 %all-to-all-start.6 = ((bf16[4,48,1152]{2,1,0:T(8,128)(2,1)}), bf16[4,48,1152]{2,1,0:T(8,128)(2,1)S(1)}, u32[]{:S(2)}, u32[]{:S(2)}) async-start(bf16[4,48,1152]{2,1,0:T(8,128)(2,1)} %bitcast.17), calls=%async_computation.6 | async-start | bytes 884736 | tf_op jit(solution)/shard_map/all_to_all | solution.py:309
  276.8 23.9 %collective-permute-start.29 = (bf16[4,144,538]{2,1,0:T(8,128)(2,1)}, bf16[4,144,538]{2,1,0:T(8,128)(2,1)}, u32[]{:S(2)}, u32[]{:S(2)}) collective-permute-start(bf16[4,144,538]{2,1,0:T(8,128)(2,1)} %all-to-all-done.9), channel_id=1, source_target_pairs={{0,16},{16,0},{1,17},{17,1},{2,18},{18,2},{3,19},{19,3},{4,20},{20... | collective-permute-start | bytes 1859336 | tf_op jit(solution)/shard_map/ppermute | solution.py:306
  289.0 24.2 %all-to-all-start.8 = ((bf16[4,272,288]{2,1,0:T(8,128)(2,1)}), bf16[4,272,288]{2,1,0:T(8,128)(2,1)S(1)}, u32[]{:S(2)}, u32[]{:S(2)}) async-start(bf16[4,272,288]{2,1,0:T(8,128)(2,1)} %shard_map.253), calls=%async_computation.8 | async-start | bytes 1671168 | tf_op jit(solution)/shard_map/all_to_all | solution.py:309
  293.3 6.5 %collective-permute-start.27 = (bf16[288,288]{1,0:T(8,128)(2,1)S(1)}, bf16[288,288]{1,0:T(8,128)(2,1)S(1)}, u32[]{:S(2)}, u32[]{:S(2)}) collective-permute-start(bf16[288,288]{1,0:T(8,128)(2,1)S(1)} %convolution_convert_fusion.6), channel_id=1, source_target_pairs={{0,16},{16,0},{1,17},{17,1},{2,18},{18,2},{3,19},{19,3},{4,20},{20... | collective-permute-start | bytes 497672 | tf_op jit(solution)/shard_map/ppermute | solution.py:306
  324.3 11.2 %collective-permute-start.26 = (bf16[4,144,216]{2,1,0:T(8,128)(2,1)S(1)}, bf16[4,144,216]{2,1,0:T(8,128)(2,1)S(1)}, u32[]{:S(2)}, u32[]{:S(2)}) collective-permute-start(bf16[4,144,216]{2,1,0:T(8,128)(2,1)S(1)} %slice.374), channel_id=1, source_target_pairs={{0,16},{16,0},{1,17},{17,1},{2,18},{18,2},{3,19},{19,3},{4,20},{20... | collective-permute-start | bytes 746504 | tf_op jit(solution)/shard_map/ppermute | solution.py:306
  325.7 8.5 %collective-permute-start.25 = (f32[11,288]{1,0:T(8,128)S(1)}, f32[11,288]{1,0:T(8,128)S(1)}, u32[]{:S(2)}, u32[]{:S(2)}) collective-permute-start(f32[11,288]{1,0:T(8,128)S(1)} %pad_maximum_fusion.8), channel_id=1, source_target_pairs={{0,16},{16,0},{1,17},{17,1},{2,18},{18,2},{3,19},{19,3},{4,20},{20... | collective-permute-start | bytes 38024 | tf_op jit(solution)/shard_map/ppermute | solution.py:306
  (72 other events, 471.1 us)

commit v2 on v1

--- a/solution.py
+++ b/solution.py
@@ -6,7 +6,6 @@
 from jax.experimental.pallas import tpu as pltpu
 from jax.sharding import PartitionSpec as P
 
-D = 1152
 SEQ = 729
 
 
@@ -34,10 +33,6 @@
 
 def pick(blocks, index, axis=0):
     return lax.dynamic_index_in_dim(blocks, index, axis, keepdims=False)
-
-
-def place(blocks, block, index):
-    return lax.dynamic_update_index_in_dim(blocks, block, index, 0)
 
 
 def after(values, *others):
@@ -384,9 +379,6 @@
         def pack(*pieces):
             return straight(jnp.stack([jnp.concatenate(group, axis=0) for group in zip(*pieces)]))
 
-        def height(piece):
-            return piece[0].shape[0]
-
         def lanes(blocks):
             return jnp.concatenate([blocks[i] for i in range(n_row)], axis=-1)
 
@@ -416,11 +408,13 @@
 
         def sum_start(product, rows):
             size = padded // 2
-            got = col_swap(product(rows[size:]).astype(LOW), masks[0])
+            sent = product(rows[size:]).astype(LOW)
+            got = col_swap(sent, masks[0])
             total = product(rows[:size]) + got.astype(WIDE)
             for mask in masks[1:]:
                 size //= 2
-                total = total[:size] + col_swap(total[size:].astype(LOW), mask).astype(WIDE)
+                got = col_swap(total[size:].astype(LOW), mask)
+                total = total[:size] + got.astype(WIDE)
             return total.astype(LOW).reshape(n_row, span, width)
 
         vectors = (pre_gain, pre_shift, merge_bias, mid_gain, mid_shift, reduce_bias)
@@ -486,13 +480,14 @@
         mlp_other = dp_swap(mlp_part) if paired else mlp_part
 
         group_context = row_gather(after(own_context, third, merge_other)).reshape(n_row * head_size, padded)
+        context_parts = col_parts(group_context)
         expand_own, reduce_own = mlp_join(
-            mlp_part, after(mlp_other, group_context), rank, n_row, units, paired
+            mlp_part, after(mlp_other, context_parts[-1]), rank, n_row, units, paired
         )
         context_full = jnp.concatenate(
             [
                 align_lanes(part, offset, near) if offset else part
-                for part, offset in zip(col_parts(group_context), near)
+                for part, offset in zip(context_parts, near)
             ],
             axis=0,
         )
@@ -510,12 +505,15 @@
             lambda rows: dot(rows, reduce_own, 1, 1), after(active, normed2_total)
         )
 
+        unit2_own, inv2_own, cot_own = own_rows(unit2), own_rows(inv2), own_rows(cot_full)
+        normed2_parts = row_exchange(normed2_total)
+
         mixed_grad, mixed_low, sums = middle_rows(
-            row_exchange(normed2_total),
-            own_rows(unit2),
-            own_rows(inv2),
+            normed2_parts,
+            unit2_own,
+            inv2_own,
             gain2,
-            own_rows(cot_full),
+            cot_own,
         )
         mixed_block = row_exchange(mixed_low).reshape(block, width)
         mixed_low = col_gather(mixed_block)
@@ -523,14 +521,14 @@
         out_rows = jnp.sum(out_parts.astype(WIDE), axis=0)
         out_rows = (own_rows(mixed1) + out_rows + bias2).astype(LOW)
 
-        expand_grad = dot(normed2, hidden_grad, 0, 0).reshape(n_row, feats, units)
-        reduce_grad = dot(cot_full, active, 0, 0).reshape(n_row, feats, units)
-        mlp_grad = grad_start(
-            jnp.concatenate([expand_grad.astype(LOW), reduce_grad.astype(LOW)], axis=2)
-        )
+        expand_grad = dot(normed2, hidden_grad, 0, 0).astype(LOW)
+        reduce_grad = dot(cot_full, active, 0, 0).astype(LOW)
+        expand_grad = expand_grad.reshape(n_row, feats, units)
+        reduce_grad = reduce_grad.reshape(n_row, feats, units)
+        mlp_grad = grad_start(jnp.concatenate([expand_grad, reduce_grad], axis=2))
         head_rows = lax.dynamic_slice_in_dim(merge_own, row * head_size, head_size, 0)
         context_grad = dot(mixed_low, head_rows, 1, 1).astype(LOW)
-        mlp_moved = row_exchange(after(mlp_grad, context_grad, out_parts))
+        mlp_moved = row_exchange(after(mlp_grad, out_parts))
         mlp_grad = grad_join(mlp_moved)
         expand_weight_grad = (
             lanes(mlp_grad[..., :units]).astype(WIDE)
@@ -582,12 +580,10 @@
         local = jnp.concatenate(
             [partial, jnp.sum(cotangent.astype(WIDE), axis=0)[None], local], axis=0
         )
-        shared = lax.all_gather(
-            jnp.concatenate(
-                [final[:, : 2 * span].reshape(2 * block, feats), split_wide(local)], axis=0
-            ),
-            "col",
-        )
+        spread_in = jnp.concatenate(
+            [final[:, : 2 * span].reshape(2 * block, feats), split_wide(local)], axis=0
+        )
+        shared = lax.all_gather(spread_in, "col")
         spread = shared[:, : 2 * block].reshape(n_col, n_row, 2 * span, feats)
         outputs = spread[:, :, :span].reshape(padded, feats)[:tokens]
         inputs_grad = spread[:, :, span:].reshape(padded, feats)[:tokens].astype(WIDE)
@@ -659,4 +655,5 @@
         P("row"),
     )
     body = make_body(mesh.shape["dp"], mesh.shape["row"], mesh.shape["col"])
+
     return jax.shard_map(body, mesh=mesh, in_specs=in_specs, out_specs=out_specs, check_vma=False)

time: 340 us -> 340 us (level)
  waiting for transfers between devices: 130 us -> 124 us
  starting transfers between devices: 58.4 us -> 63.4 us
    ppermute x9, starting transfers between devices: 8.92 us -> 12.7 us  [dp_swap(): return lax.ppermute(value, 'dp', [(0, 1), (1, 0)])]
    unnamed x167 -> x165, local copies, waits for them, and re-layouts: 18.1 us -> 18.1 us
where the time goes in v2:
time: 340 us; the launch traced here: 338 us
  waiting for transfers between devices  124 us (36%)
  starting transfers between devices  63.4 us (19%)
  local copies, waits for them, and re-layouts  50.1 us (15%)
  matrix products  34.2 us (10%)
  other arithmetic  32.3 us (9%)
  Pallas kernels  21.9 us (6%)
  blocking collectives  9.74 us (3%)
    all_to_all x10, waiting for transfers between devices, row_exchange(): return lax.all_to_all(blocks, 'row', 0, 0, tiled=True)  64.1 us
    ppermute x21, waiting for transfers between devices, col_swap(): return lax.ppermute(value, 'col', [(i, i ^ mask) for i in range(n_col)])  46.5 us
    all_to_all x10, starting transfers between devices, row_exchange(): return lax.all_to_all(blocks, 'row', 0, 0, tiled=True)  44.4 us
    dot_general x21, matrix products, dot(): lax.dot_general(left, right, (((left_dim,), (right_dim,)), ((), ())), pre...  34.2 us
    pallas_call x9, Pallas kernels, local_call(): pl.pallas_call(kernel, out_shape=[jax.ShapeDtypeStruct(shape, kind) for s...  21.9 us
    unnamed x165, local copies, waits for them, and re-layouts  18.1 us
    ppermute x9, waiting for transfers between devices, dp_swap(): return lax.ppermute(value, 'dp', [(0, 1), (1, 0)])  13.9 us
    ppermute x9, starting transfers between devices, dp_swap(): return lax.ppermute(value, 'dp', [(0, 1), (1, 0)])  12.7 us
  transfers between devices with their start and end apart: 40, of which 20 were waited for; matrix products, arithmetic and copies ran while one was open for 25% of the time, Pallas kernels for 5%

profile of v2, /device:TPU:0, one launch (start us, length us, event | category | flops | bytes accessed | tf_op | source)
XLA Modules:
  0.0 338.0 jit_solution(6147274363562466651)
XLA Ops:
  0.7 2.1 copy.112.input_ref
  3.3 3.2 shard_map.245
  6.5 2.3 copy.113
  8.8 6.5 %all-to-all-start = ((bf16[4,368,288]{1,2,0:T(8,128)(2,1)}), bf16[4,368,288]{1,2,0:T(8,128)(2,1)S(1)}, u32[]{:S(2)}, u32[]{:S(2)}) async-start(bf16[4,368,288]{1,2,0:T(8,128)(2,1)} %copy.113), calls=%async_computation | async-start | bytes 1769472 | tf_op jit(solution)/shard_map/all_to_all | solution.py:304
  18.6 18.9 %all-to-all-done = bf16[4,368,288]{1,2,0:T(8,128)(2,1)S(1)} async-done(((bf16[4,368,288]{1,2,0:T(8,128)(2,1)}), bf16[4,368,288]{1,2,0:T(8,128)(2,1)S(1)}, u32[]{:S(2)}, u32[]{:S(2)}) %all-to-all-start) | async-done | bytes 847904 | tf_op jit(solution)/shard_map/all_to_all | solution.py:304
  38.9 2.4 shard_map.246
  44.3 3.5 %all-to-all-start.1 = ((bf16[4,336,288]{1,2,0:T(8,128)(2,1)}), bf16[4,336,288]{1,2,0:T(8,128)(2,1)S(1)}, u32[]{:S(2)}, u32[]{:S(2)}) async-start(bf16[4,336,288]{1,2,0:T(8,128)(2,1)} %copy.117), calls=%async_computation.1 | async-start | bytes 1769472 | tf_op jit(solution)/shard_map/all_to_all | solution.py:304
  49.4 4.7 %collective-permute-done = bf16[192,1152]{1,0:T(8,128)(2,1)S(1)} collective-permute-done((bf16[192,1152]{1,0:T(8,128)(2,1)}, bf16[192,1152]{1,0:T(8,128)(2,1)S(1)}, u32[]{:S(2)}, u32[]{:S(2)}) %collective-permute-start) | collective-permute-done | bytes 442400 | tf_op jit(solution)/shard_map/ppermute | solution.py:298
  57.7 2.0 shard_map.247
  60.4 10.2 %all-to-all-done.1 = bf16[4,336,288]{1,2,0:T(8,128)(2,1)S(1)} async-done(((bf16[4,336,288]{1,2,0:T(8,128)(2,1)}), bf16[4,336,288]{1,2,0:T(8,128)(2,1)S(1)}, u32[]{:S(2)}, u32[]{:S(2)}) %all-to-all-start.1) | async-done | bytes 774176 | tf_op jit(solution)/shard_map/all_to_all | solution.py:304
  70.6 4.2 %all-to-all-start.2 = ((bf16[4,288,288]{2,1,0:T(8,128)(2,1)}), bf16[4,288,288]{2,1,0:T(8,128)(2,1)}, u32[]{:S(2)}, u32[]{:S(2)}) async-start(bf16[4,288,288]{2,1,0:T(8,128)(2,1)} %pad_maximum_fusion.2), calls=%async_computation.2 | async-start | bytes 1769472 | tf_op jit(solution)/shard_map/all_to_all | solution.py:304
  79.4 2.3 shard_map.248
  86.2 4.9 %collective-permute-done.8.other_ref = bf16[144,1152]{1,0:T(8,128)(2,1)} collective-permute-done((bf16[144,1152]{1,0:T(8,128)(2,1)}, bf16[144,1152]{1,0:T(8,128)(2,1)}, u32[]{:S(2)}, u32[]{:S(2)}) %collective-permute-start.8) | collective-permute-done | bytes 331808 | tf_op jit(solution)/shard_map/ppermute | solution.py:301
  91.1 5.7 %all-to-all-done.2.moved_ref = bf16[4,288,288]{2,1,0:T(8,128)(2,1)} async-done(((bf16[4,288,288]{2,1,0:T(8,128)(2,1)}), bf16[4,288,288]{2,1,0:T(8,128)(2,1)}, u32[]{:S(2)}, u32[]{:S(2)}) %all-to-all-start.2) | async-done | bytes 663584 | tf_op jit(solution)/shard_map/all_to_all | solution.py:304
  97.6 3.6 %all-to-all-start.3 = ((bf16[4,72,768]{2,1,0:T(8,128)(2,1)}), bf16[4,72,768]{2,1,0:T(8,128)(2,1)S(1)}, u32[]{:S(2)}, u32[]{:S(2)}) async-start(bf16[4,72,768]{2,1,0:T(8,128)(2,1)} %broadcast_in_dim.7), calls=%async_computation.3 | async-start | bytes 884736 | tf_op jit(solution)/shard_map/all_to_all | solution.py:304
  103.9 2.0 shard_map.251
  107.5 2.2 shard_map.249.mine_ref
  111.2 2.1 all-to-all-done.3
  115.7 8.3 %collective-permute-done.12 = bf16[288,1152]{1,0:T(8,128)(2,1)} collective-permute-done((bf16[288,1152]{1,0:T(8,128)(2,1)}, bf16[288,1152]{1,0:T(8,128)(2,1)}, u32[]{:S(2)}, u32[]{:S(2)}) %collective-permute-start.12) | collective-permute-done | bytes 663584 | tf_op jit(solution)/shard_map/ppermute | solution.py:298
  124.0 8.9 %collective-permute-done.9 = bf16[288,768]{1,0:T(8,128)(2,1)S(1)} collective-permute-done((bf16[288,768]{1,0:T(8,128)(2,1)S(1)}, bf16[288,768]{1,0:T(8,128)(2,1)S(1)}, u32[]{:S(2)}, u32[]{:S(2)}) %collective-permute-start.9) | collective-permute-done | bytes 442400 | tf_op jit(solution)/shard_map/ppermute | solution.py:298
  134.8 2.9 shard_map.250
  139.1 5.4 %fusion.116 = (f32[768]{0:T(1024)S(1)}, f32[768]{0:T(1024)S(1)}, f32[768,1152]{1,0:T(8,128)S(1)}) fusion(f32[1152]{0:T(1024)S(1)} %copy-done.72, bf16[288,1152]{1,0:T(8,128)(2,1)} %collective-permute-done.14, bf16[288,1152]{1,0:T(8,128)(2,1)} %collective-permute-done.13, bf16[288,1152]{1,0:T(8,128)(2,1)} %collective-permute-done.12, ...), kind=kOutput, calls=%fused_computation.255 | convolution fusion | flops 2080012800 | bytes 9742848 | tf_op jit(solution)/shard_map/dot_general | solution.py:29
  152.2 2.1 collective-permute-done.15
  156.3 12.1 %collective-permute-done.16 = bf16[192,1152]{1,0:T(8,128)(2,1)S(1)} collective-permute-done((bf16[192,1152]{1,0:T(8,128)(2,1)}, bf16[192,1152]{1,0:T(8,128)(2,1)S(1)}, u32[]{:S(2)}, u32[]{:S(2)}) %collective-permute-start.16) | collective-permute-done | bytes 442400 | tf_op jit(solution)/shard_map/ppermute | solution.py:298
  169.3 4.9 %all-to-all-start.4 = ((bf16[4,48,1152]{2,1,0:T(8,128)(2,1)}), bf16[4,48,1152]{2,1,0:T(8,128)(2,1)S(1)}, u32[]{:S(2)}, u32[]{:S(2)}) async-start(bf16[4,48,1152]{2,1,0:T(8,128)(2,1)} %bitcast.13), calls=%async_computation.4 | async-start | bytes 884736 | tf_op jit(solution)/shard_map/all_to_all | solution.py:304
  174.1 3.0 convolution_convert_fusion
  181.1 5.4 %all-to-all-done.4.part_ref = bf16[4,48,1152]{2,1,0:T(8,128)(2,1)S(1)} async-done(((bf16[4,48,1152]{2,1,0:T(8,128)(2,1)}), bf16[4,48,1152]{2,1,0:T(8,128)(2,1)S(1)}, u32[]{:S(2)}, u32[]{:S(2)}) %all-to-all-start.4) | async-done | bytes 442400 | tf_op jit(solution)/shard_map/all_to_all | solution.py:304
  187.3 2.3 shard_map.252
  189.5 3.7 %all-to-all-start.5 = ((bf16[4,48,1152]{2,1,0:T(8,128)(2,1)}), bf16[4,48,1152]{2,1,0:T(8,128)(2,1)S(1)}, u32[]{:S(2)}, u32[]{:S(2)}) async-start(bf16[4,48,1152]{2,1,0:T(8,128)(2,1)} %get-tuple-element.50), calls=%async_computation.5 | async-start | bytes 884736 | tf_op jit(solution)/shard_map/all_to_all | solution.py:304
  193.3 1.9 convert_add_fusion.1
  197.7 7.5 %all-to-all-done.5 = bf16[4,48,1152]{2,1,0:T(8,128)(2,1)S(1)} async-done(((bf16[4,48,1152]{2,1,0:T(8,128)(2,1)}), bf16[4,48,1152]{2,1,0:T(8,128)(2,1)S(1)}, u32[]{:S(2)}, u32[]{:S(2)}) %all-to-all-start.5) | async-done | bytes 442400 | tf_op jit(solution)/shard_map/all_to_all | solution.py:304
  205.8 2.7 convolution_convert_fusion.4
  209.0 3.4 %convolution_convert_fusion.3 = bf16[1152,269]{0,1:T(8,128)(2,1)} fusion(bf16[768,1152]{1,0:T(8,128)(2,1)} %constant_dynamic-update-slice_fusion, bf16[768,269]{0,1:T(8,128)(2,1)} %get-tuple-element.53), kind=kOutput, calls=%fused_computation.36 | convolution fusion | flops 476297856 | bytes 2802432 | tf_op jit(solution)/shard_map/dot_general | solution.py:29
  220.1 4.5 %all-to-all-start.7 = ((bf16[4,48,1152]{2,1,0:T(8,128)(2,1)}), bf16[4,48,1152]{2,1,0:T(8,128)(2,1)}, u32[]{:S(2)}, u32[]{:S(2)}) async-start(bf16[4,48,1152]{2,1,0:T(8,128)(2,1)} %bitcast.19), calls=%async_computation.7 | async-start | bytes 884736 | tf_op jit(solution)/shard_map/all_to_all | solution.py:304
  235.2 2.9 fusion.1
  241.1 2.5 add_convert_fusion.2
  243.6 4.9 %all-to-all-start.9 = ((bf16[4,144,538]{2,1,0:T(8,128)(2,1)}), bf16[4,144,538]{2,1,0:T(8,128)(2,1)}, u32[]{:S(2)}, u32[]{:S(2)}) async-start(bf16[4,144,538]{2,1,0:T(8,128)(2,1)} %add_convert_fusion.2), calls=%async_computation.9 | async-start | bytes 1474560 | tf_op jit(solution)/shard_map/all_to_all | solution.py:304
  248.5 1.9 convert_reduce_fusion.2
  258.3 8.5 %collective-permute-done.21 = bf16[192,1152]{1,0:T(8,128)(2,1)} collective-permute-done((bf16[192,1152]{1,0:T(8,128)(2,1)}, bf16[192,1152]{1,0:T(8,128)(2,1)}, u32[]{:S(2)}, u32[]{:S(2)}) %collective-permute-start.21) | collective-permute-done | bytes 442400 | tf_op jit(solution)/shard_map/ppermute | solution.py:298
  266.9 2.1 fusion.36
  269.0 4.8 %all-to-all-start.6 = ((bf16[4,48,1152]{2,1,0:T(8,128)(2,1)}), bf16[4,48,1152]{2,1,0:T(8,128)(2,1)S(1)}, u32[]{:S(2)}, u32[]{:S(2)}) async-start(bf16[4,48,1152]{2,1,0:T(8,128)(2,1)} %bitcast.17), calls=%async_computation.6 | async-start | bytes 884736 | tf_op jit(solution)/shard_map/all_to_all | solution.py:304
  278.7 7.1 %all-to-all-done.6.part_ref = bf16[4,48,1152]{2,1,0:T(8,128)(2,1)S(1)} async-done(((bf16[4,48,1152]{2,1,0:T(8,128)(2,1)}), bf16[4,48,1152]{2,1,0:T(8,128)(2,1)S(1)}, u32[]{:S(2)}, u32[]{:S(2)}) %all-to-all-start.6) | async-done | bytes 442400 | tf_op jit(solution)/shard_map/all_to_all | solution.py:304
  286.5 2.6 shard_map.253
  289.2 3.8 %all-to-all-start.8 = ((bf16[4,272,288]{2,1,0:T(8,128)(2,1)}), bf16[4,272,288]{2,1,0:T(8,128)(2,1)S(1)}, u32[]{:S(2)}, u32[]{:S(2)}) async-start(bf16[4,272,288]{2,1,0:T(8,128)(2,1)} %shard_map.253), calls=%async_computation.8 | async-start | bytes 1671168 | tf_op jit(solution)/shard_map/all_to_all | solution.py:304
  296.2 3.8 %collective-permute-done.27 = bf16[288,288]{1,0:T(8,128)(2,1)S(1)} collective-permute-done((bf16[288,288]{1,0:T(8,128)(2,1)S(1)}, bf16[288,288]{1,0:T(8,128)(2,1)S(1)}, u32[]{:S(2)}, u32[]{:S(2)}) %collective-permute-start.27) | collective-permute-done | bytes 165920 | tf_op jit(solution)/shard_map/ppermute | solution.py:301
  306.2 7.1 %all-to-all-done.8 = bf16[4,272,288]{2,1,0:T(8,128)(2,1)S(1)} async-done(((bf16[4,272,288]{2,1,0:T(8,128)(2,1)}), bf16[4,272,288]{2,1,0:T(8,128)(2,1)S(1)}, u32[]{:S(2)}, u32[]{:S(2)}) %all-to-all-start.8) | async-done | bytes 626720 | tf_op jit(solution)/shard_map/all_to_all | solution.py:304
  314.5 9.7 %all-gather.1 = bf16[4,417,288]{1,2,0:T(8,128)(2,1)S(1)} all-gather(bf16[1,417,288]{1,2,0:T(8,128)(2,1)S(1)} %maximum_bitcast_fusion), channel_id=2, replica_groups=mesh['dp'=2,'row'=4,'col'=4] {'col'}, dimensions={0}, use_global_device_ids=true | all-gather | bytes 1200960 | tf_op jit(solution)/shard_map/all_gather | solution.py:586
  330.7 3.6 %collective-permute-done.25 = f32[11,288]{1,0:T(8,128)S(1)} collective-permute-done((f32[11,288]{1,0:T(8,128)S(1)}, f32[11,288]{1,0:T(8,128)S(1)}, u32[]{:S(2)}, u32[]{:S(2)}) %collective-permute-start.25) | collective-permute-done | bytes 12704 | tf_op jit(solution)/shard_map/ppermute | solution.py:301
  (339 shorter events, 108.8 us)
Async XLA Ops:
  8.8 28.7 %all-to-all-start = ((bf16[4,368,288]{1,2,0:T(8,128)(2,1)}), bf16[4,368,288]{1,2,0:T(8,128)(2,1)S(1)}, u32[]{:S(2)}, u32[]{:S(2)}) async-start(bf16[4,368,288]{1,2,0:T(8,128)(2,1)} %copy.113), calls=%async_computation | async-start | bytes 1769472 | tf_op jit(solution)/shard_map/all_to_all | solution.py:304
  41.3 18.4 %collective-permute-start.1 = (bf16[192,1152]{1,0:T(8,128)(2,1)}, bf16[192,1152]{1,0:T(8,128)(2,1)S(1)}, u32[]{:S(2)}, u32[]{:S(2)}) collective-permute-start(bf16[192,1152]{1,0:T(8,128)(2,1)} %get-tuple-element.35), channel_id=1, source_target_pairs={{0,1},{1,0},{2,3},{3,2},{4,5},{5,4},{6,7},{7,6},{8,9},{9,8},{10,11... | collective-permute-start | bytes 1327112 | tf_op jit(solution)/shard_map/ppermute | solution.py:298
  41.3 12.8 %collective-permute-start = (bf16[192,1152]{1,0:T(8,128)(2,1)}, bf16[192,1152]{1,0:T(8,128)(2,1)S(1)}, u32[]{:S(2)}, u32[]{:S(2)}) collective-permute-start(bf16[192,1152]{1,0:T(8,128)(2,1)} %get-tuple-element.35), channel_id=1, source_target_pairs={{0,2},{1,3},{2,0},{3,1},{4,6},{5,7},{6,4},{7,5},{8,10},{9,11},{10,... | collective-permute-start | bytes 1327112 | tf_op jit(solution)/shard_map/ppermute | solution.py:298
  44.3 26.3 %all-to-all-start.1 = ((bf16[4,336,288]{1,2,0:T(8,128)(2,1)}), bf16[4,336,288]{1,2,0:T(8,128)(2,1)S(1)}, u32[]{:S(2)}, u32[]{:S(2)}) async-start(bf16[4,336,288]{1,2,0:T(8,128)(2,1)} %copy.117), calls=%async_computation.1 | async-start | bytes 1769472 | tf_op jit(solution)/shard_map/all_to_all | solution.py:304
  47.9 9.1 %collective-permute-start.3 = (bf16[576,216]{1,0:T(8,128)(2,1)S(1)}, bf16[576,216]{1,0:T(8,128)(2,1)S(1)}, u32[]{:S(2)}, u32[]{:S(2)}) collective-permute-start(bf16[576,216]{1,0:T(8,128)(2,1)S(1)} %copy-done.55), channel_id=1, source_target_pairs={{0,16},{16,0},{1,17},{17,1},{2,18},{18,2},{3,19},{19,3},{4,20},{20... | collective-permute-start | bytes 746504 | tf_op jit(solution)/shard_map/ppermute | solution.py:301
  54.1 20.7 %copy-start.30 = (bf16[192,1152]{1,0:T(8,128)(2,1)}, bf16[192,1152]{1,0:T(8,128)(2,1)S(1)}, u32[]{:S(2)}) copy-start(bf16[192,1152]{1,0:T(8,128)(2,1)S(1)} %collective-permute-done) | copy-start | bytes 1327108
  54.1 5.6 %collective-permute-start.2 = (bf16[192,1152]{1,0:T(8,128)(2,1)S(1)}, bf16[192,1152]{1,0:T(8,128)(2,1)S(1)}, u32[]{:S(2)}, u32[]{:S(2)}) collective-permute-start(bf16[192,1152]{1,0:T(8,128)(2,1)S(1)} %collective-permute-done), channel_id=1, source_target_pairs={{0,1},{1,0},{2,3},{3,2},{4,5},{5,4},{6,7},{7,6},{8,9},{9,8},{10,11... | collective-permute-start | bytes 1327112 | tf_op jit(solution)/shard_map/ppermute | solution.py:298
  70.6 26.2 %all-to-all-start.2 = ((bf16[4,288,288]{2,1,0:T(8,128)(2,1)}), bf16[4,288,288]{2,1,0:T(8,128)(2,1)}, u32[]{:S(2)}, u32[]{:S(2)}) async-start(bf16[4,288,288]{2,1,0:T(8,128)(2,1)} %pad_maximum_fusion.2), calls=%async_computation.2 | async-start | bytes 1769472 | tf_op jit(solution)/shard_map/all_to_all | solution.py:304
  81.8 9.3 %collective-permute-start.8 = (bf16[144,1152]{1,0:T(8,128)(2,1)}, bf16[144,1152]{1,0:T(8,128)(2,1)}, u32[]{:S(2)}, u32[]{:S(2)}) collective-permute-start(bf16[144,1152]{1,0:T(8,128)(2,1)} %get-tuple-element.45.mine_ref), channel_id=1, source_target_pairs={{0,16},{16,0},{1,17},{17,1},{2,18},{18,2},{3,19},{19,3},{4,20},{20... | collective-permute-start | bytes 995336 | tf_op jit(solution)/shard_map/ppermute | solution.py:301
  84.4 22.0 %collective-permute-start.4 = (bf16[192,1152]{1,0:T(8,128)(2,1)}, bf16[192,1152]{1,0:T(8,128)(2,1)S(1)}, u32[]{:S(2)}, u32[]{:S(2)}) collective-permute-start(bf16[192,1152]{1,0:T(8,128)(2,1)} %get-tuple-element.41), channel_id=1, source_target_pairs={{0,2},{1,3},{2,0},{3,1},{4,6},{5,7},{6,4},{7,5},{8,10},{9,11},{10,... | collective-permute-start | bytes 1327112 | tf_op jit(solution)/shard_map/ppermute | solution.py:298
  97.6 15.7 %all-to-all-start.3 = ((bf16[4,72,768]{2,1,0:T(8,128)(2,1)}), bf16[4,72,768]{2,1,0:T(8,128)(2,1)S(1)}, u32[]{:S(2)}, u32[]{:S(2)}) async-start(bf16[4,72,768]{2,1,0:T(8,128)(2,1)} %broadcast_in_dim.7), calls=%async_computation.3 | async-start | bytes 884736 | tf_op jit(solution)/shard_map/all_to_all | solution.py:304
  102.1 11.3 %collective-permute-start.5 = (bf16[192,1152]{1,0:T(8,128)(2,1)}, bf16[192,1152]{1,0:T(8,128)(2,1)S(1)}, u32[]{:S(2)}, u32[]{:S(2)}) collective-permute-start(bf16[192,1152]{1,0:T(8,128)(2,1)} %get-tuple-element.41), channel_id=1, source_target_pairs={{0,1},{1,0},{2,3},{3,2},{4,5},{5,4},{6,7},{7,6},{8,9},{9,8},{10,11... | collective-permute-start | bytes 1327112 | tf_op jit(solution)/shard_map/ppermute | solution.py:298
  105.9 18.1 %collective-permute-start.12 = (bf16[288,1152]{1,0:T(8,128)(2,1)}, bf16[288,1152]{1,0:T(8,128)(2,1)}, u32[]{:S(2)}, u32[]{:S(2)}) collective-permute-start(bf16[288,1152]{1,0:T(8,128)(2,1)} %shard_map.251), channel_id=1, source_target_pairs={{0,2},{1,3},{2,0},{3,1},{4,6},{5,7},{6,4},{7,5},{8,10},{9,11},{10,... | collective-permute-start | bytes 1990664 | tf_op jit(solution)/shard_map/ppermute | solution.py:298
  106.4 8.3 %collective-permute-start.6 = (bf16[192,1152]{1,0:T(8,128)(2,1)S(1)}, bf16[192,1152]{1,0:T(8,128)(2,1)S(1)}, u32[]{:S(2)}, u32[]{:S(2)}) collective-permute-start(bf16[192,1152]{1,0:T(8,128)(2,1)S(1)} %collective-permute-done.4), channel_id=1, source_target_pairs={{0,1},{1,0},{2,3},{3,2},{4,5},{5,4},{6,7},{7,6},{8,9},{9,8},{10,11... | collective-permute-start | bytes 1327112 | tf_op jit(solution)/shard_map/ppermute | solution.py:298
  109.7 24.9 %collective-permute-start.7 = (bf16[576,640]{1,0:T(8,128)(2,1)}, bf16[576,640]{1,0:T(8,128)(2,1)}, u32[]{:S(2)}, u32[]{:S(2)}) collective-permute-start(bf16[576,640]{1,0:T(8,128)(2,1)} %shard_map.249.mine_ref), channel_id=1, source_target_pairs={{0,16},{16,0},{1,17},{17,1},{2,18},{18,2},{3,19},{19,3},{4,20},{20... | collective-permute-start | bytes 2211848 | tf_op jit(solution)/shard_map/ppermute | solution.py:301
  113.3 25.7 %copy-start.18 = (bf16[4,72,768]{2,1,0:T(8,128)(2,1)}, bf16[4,72,768]{2,1,0:T(8,128)(2,1)S(1)}, u32[]{:S(2)}) copy-start(bf16[4,72,768]{2,1,0:T(8,128)(2,1)S(1)} %all-to-all-done.3) | copy-start | bytes 1327108
  113.3 19.6 %collective-permute-start.11 = (bf16[288,768]{1,0:T(8,128)(2,1)S(1)}, bf16[288,768]{1,0:T(8,128)(2,1)S(1)}, u32[]{:S(2)}, u32[]{:S(2)}) collective-permute-start(bf16[288,768]{1,0:T(8,128)(2,1)S(1)} %bitcast.114), channel_id=1, source_target_pairs={{0,1},{1,0},{2,3},{3,2},{4,5},{5,4},{6,7},{7,6},{8,9},{9,8},{10,11... | collective-permute-start | bytes 1327112 | tf_op jit(solution)/shard_map/ppermute | solution.py:298
  113.4 19.5 %collective-permute-start.9 = (bf16[288,768]{1,0:T(8,128)(2,1)S(1)}, bf16[288,768]{1,0:T(8,128)(2,1)S(1)}, u32[]{:S(2)}, u32[]{:S(2)}) collective-permute-start(bf16[288,768]{1,0:T(8,128)(2,1)S(1)} %bitcast.115), channel_id=1, source_target_pairs={{0,2},{1,3},{2,0},{3,1},{4,6},{5,7},{6,4},{7,5},{8,10},{9,11},{10,... | collective-permute-start | bytes 1327112 | tf_op jit(solution)/shard_map/ppermute | solution.py:298
  114.7 24.3 %collective-permute-start.13 = (bf16[288,1152]{1,0:T(8,128)(2,1)}, bf16[288,1152]{1,0:T(8,128)(2,1)}, u32[]{:S(2)}, u32[]{:S(2)}) collective-permute-start(bf16[288,1152]{1,0:T(8,128)(2,1)} %shard_map.251), channel_id=1, source_target_pairs={{0,1},{1,0},{2,3},{3,2},{4,5},{5,4},{6,7},{7,6},{8,9},{9,8},{10,11... | collective-permute-start | bytes 1990664 | tf_op jit(solution)/shard_map/ppermute | solution.py:298
  115.7 23.4 %copy-start.23 = (bf16[192,1152]{1,0:T(8,128)(2,1)S(1)}, bf16[192,1152]{1,0:T(8,128)(2,1)}, u32[]{:S(2)}) copy-start(bf16[192,1152]{1,0:T(8,128)(2,1)} %get-tuple-element.35) | copy-start | bytes 1327108
  115.7 23.4 %copy-start.27 = (bf16[192,1152]{1,0:T(8,128)(2,1)S(1)}, bf16[192,1152]{1,0:T(8,128)(2,1)}, u32[]{:S(2)}) copy-start(bf16[192,1152]{1,0:T(8,128)(2,1)} %copy-done.26) | copy-start | bytes 1327108
  115.7 23.4 %copy-start.31 = (bf16[192,1152]{1,0:T(8,128)(2,1)S(1)}, bf16[192,1152]{1,0:T(8,128)(2,1)}, u32[]{:S(2)}) copy-start(bf16[192,1152]{1,0:T(8,128)(2,1)} %copy-done.30) | copy-start | bytes 1327108
  115.7 23.4 %copy-start.35 = (bf16[192,1152]{1,0:T(8,128)(2,1)S(1)}, bf16[192,1152]{1,0:T(8,128)(2,1)}, u32[]{:S(2)}) copy-start(bf16[192,1152]{1,0:T(8,128)(2,1)} %copy-done.34) | copy-start | bytes 1327108
  115.7 23.4 %copy-start.72 = (f32[1152]{0:T(1024)S(1)}, f32[1152]{0:T(1024)}, u32[]{:S(2)}) copy-start(f32[1152]{0:T(1024)} %get-tuple-element.134) | copy-start | bytes 13828
  124.0 15.1 %collective-permute-start.14 = (bf16[288,1152]{1,0:T(8,128)(2,1)}, bf16[288,1152]{1,0:T(8,128)(2,1)}, u32[]{:S(2)}, u32[]{:S(2)}) collective-permute-start(bf16[288,1152]{1,0:T(8,128)(2,1)} %collective-permute-done.12), channel_id=1, source_target_pairs={{0,1},{1,0},{2,3},{3,2},{4,5},{5,4},{6,7},{7,6},{8,9},{9,8},{10,11... | collective-permute-start | bytes 1990664 | tf_op jit(solution)/shard_map/ppermute | solution.py:298
  132.9 1.9 collective-permute-start.10
  151.8 2.5 collective-permute-start.15
  155.8 12.6 %collective-permute-start.16 = (bf16[192,1152]{1,0:T(8,128)(2,1)}, bf16[192,1152]{1,0:T(8,128)(2,1)S(1)}, u32[]{:S(2)}, u32[]{:S(2)}) collective-permute-start(bf16[192,1152]{1,0:T(8,128)(2,1)} %slice.560), channel_id=1, source_target_pairs={{0,2},{1,3},{2,0},{3,1},{4,6},{5,7},{6,4},{7,5},{8,10},{9,11},{10,... | collective-permute-start | bytes 1327112 | tf_op jit(solution)/shard_map/ppermute | solution.py:298
  169.3 17.2 %all-to-all-start.4 = ((bf16[4,48,1152]{2,1,0:T(8,128)(2,1)}), bf16[4,48,1152]{2,1,0:T(8,128)(2,1)S(1)}, u32[]{:S(2)}, u32[]{:S(2)}) async-start(bf16[4,48,1152]{2,1,0:T(8,128)(2,1)} %bitcast.13), calls=%async_computation.4 | async-start | bytes 884736 | tf_op jit(solution)/shard_map/all_to_all | solution.py:304
  174.1 19.1 %copy-start.50 = (bf16[768,269]{0,1:T(8,128)(2,1)S(1)}, bf16[768,269]{0,1:T(8,128)(2,1)}, u32[]{:S(2)}) copy-start(bf16[768,269]{0,1:T(8,128)(2,1)} %get-tuple-element.53) | copy-start | bytes 1239556
  177.1 16.1 %collective-permute-start.22 = (bf16[384,1152]{1,0:T(8,128)(2,1)}, bf16[384,1152]{1,0:T(8,128)(2,1)}, u32[]{:S(2)}, u32[]{:S(2)}) collective-permute-start(bf16[384,1152]{1,0:T(8,128)(2,1)} %convolution_convert_fusion), channel_id=1, source_target_pairs={{0,1},{1,0},{2,3},{3,2},{4,5},{5,4},{6,7},{7,6},{8,9},{9,8},{10,11... | collective-permute-start | bytes 2654216 | tf_op jit(solution)/shard_map/ppermute | solution.py:298
  189.5 15.7 %all-to-all-start.5 = ((bf16[4,48,1152]{2,1,0:T(8,128)(2,1)}), bf16[4,48,1152]{2,1,0:T(8,128)(2,1)S(1)}, u32[]{:S(2)}, u32[]{:S(2)}) async-start(bf16[4,48,1152]{2,1,0:T(8,128)(2,1)} %get-tuple-element.50), calls=%async_computation.5 | async-start | bytes 884736 | tf_op jit(solution)/shard_map/all_to_all | solution.py:304
  197.2 21.0 %collective-permute-start.23 = (bf16[192,1152]{1,0:T(8,128)(2,1)}, bf16[192,1152]{1,0:T(8,128)(2,1)}, u32[]{:S(2)}, u32[]{:S(2)}) collective-permute-start(bf16[192,1152]{1,0:T(8,128)(2,1)} %slice.558), channel_id=1, source_target_pairs={{0,2},{1,3},{2,0},{3,1},{4,6},{5,7},{6,4},{7,5},{8,10},{9,11},{10,... | collective-permute-start | bytes 1327112 | tf_op jit(solution)/shard_map/ppermute | solution.py:298
  205.3 12.9 %collective-permute-start.17 = (bf16[192,1152]{1,0:T(8,128)(2,1)S(1)}, bf16[192,1152]{1,0:T(8,128)(2,1)}, u32[]{:S(2)}, u32[]{:S(2)}) collective-permute-start(bf16[192,1152]{1,0:T(8,128)(2,1)S(1)} %bitcast.118), channel_id=1, source_target_pairs={{0,2},{1,3},{2,0},{3,1},{4,6},{5,7},{6,4},{7,5},{8,10},{9,11},{10,... | collective-permute-start | bytes 1327112 | tf_op jit(solution)/shard_map/ppermute | solution.py:298
  215.0 26.1 %collective-permute-start.28 = (bf16[4,144,538]{2,1,0:T(8,128)(2,1)}, bf16[4,144,538]{2,1,0:T(8,128)(2,1)}, u32[]{:S(2)}, u32[]{:S(2)}) collective-permute-start(bf16[4,144,538]{2,1,0:T(8,128)(2,1)} %fusion.43), channel_id=1, source_target_pairs={{0,16},{16,0},{1,17},{17,1},{2,18},{18,2},{3,19},{19,3},{4,20},{20... | collective-permute-start | bytes 1859336 | tf_op jit(solution)/shard_map/ppermute | solution.py:301
  216.5 8.1 %collective-permute-start.18 = (bf16[192,1152]{1,0:T(8,128)(2,1)S(1)}, bf16[192,1152]{1,0:T(8,128)(2,1)S(1)}, u32[]{:S(2)}, u32[]{:S(2)}) collective-permute-start(bf16[192,1152]{1,0:T(8,128)(2,1)S(1)} %bitcast.119), channel_id=1, source_target_pairs={{0,1},{1,0},{2,3},{3,2},{4,5},{5,4},{6,7},{7,6},{8,9},{9,8},{10,11... | collective-permute-start | bytes 1327112 | tf_op jit(solution)/shard_map/ppermute | solution.py:298
  218.2 7.2 %collective-permute-start.19 = (bf16[192,1152]{1,0:T(8,128)(2,1)}, bf16[192,1152]{1,0:T(8,128)(2,1)}, u32[]{:S(2)}, u32[]{:S(2)}) collective-permute-start(bf16[192,1152]{1,0:T(8,128)(2,1)} %collective-permute-done.17), channel_id=1, source_target_pairs={{0,1},{1,0},{2,3},{3,2},{4,5},{5,4},{6,7},{7,6},{8,9},{9,8},{10,11... | collective-permute-start | bytes 1327112 | tf_op jit(solution)/shard_map/ppermute | solution.py:298
  220.1 23.5 %all-to-all-start.7 = ((bf16[4,48,1152]{2,1,0:T(8,128)(2,1)}), bf16[4,48,1152]{2,1,0:T(8,128)(2,1)}, u32[]{:S(2)}, u32[]{:S(2)}) async-start(bf16[4,48,1152]{2,1,0:T(8,128)(2,1)} %bitcast.19), calls=%async_computation.7 | async-start | bytes 884736 | tf_op jit(solution)/shard_map/all_to_all | solution.py:304
  234.9 15.5 %collective-permute-start.20 = (bf16[384,1152]{1,0:T(8,128)(2,1)}, bf16[384,1152]{1,0:T(8,128)(2,1)}, u32[]{:S(2)}, u32[]{:S(2)}) collective-permute-start(bf16[384,1152]{1,0:T(8,128)(2,1)} %convolution_convert_fusion.2), channel_id=1, source_target_pairs={{0,1},{1,0},{2,3},{3,2},{4,5},{5,4},{6,7},{7,6},{8,9},{9,8},{10,11... | collective-permute-start | bytes 2654216 | tf_op jit(solution)/shard_map/ppermute | solution.py:298
  243.6 25.4 %all-to-all-start.9 = ((bf16[4,144,538]{2,1,0:T(8,128)(2,1)}), bf16[4,144,538]{2,1,0:T(8,128)(2,1)}, u32[]{:S(2)}, u32[]{:S(2)}) async-start(bf16[4,144,538]{2,1,0:T(8,128)(2,1)} %add_convert_fusion.2), calls=%async_computation.9 | async-start | bytes 1474560 | tf_op jit(solution)/shard_map/all_to_all | solution.py:304
  254.3 12.6 %collective-permute-start.21 = (bf16[192,1152]{1,0:T(8,128)(2,1)}, bf16[192,1152]{1,0:T(8,128)(2,1)}, u32[]{:S(2)}, u32[]{:S(2)}) collective-permute-start(bf16[192,1152]{1,0:T(8,128)(2,1)} %slice.559), channel_id=1, source_target_pairs={{0,2},{1,3},{2,0},{3,1},{4,6},{5,7},{6,4},{7,5},{8,10},{9,11},{10,... | collective-permute-start | bytes 1327112 | tf_op jit(solution)/shard_map/ppermute | solution.py:298
  256.8 18.6 %collective-permute-start.24 = (bf16[4,144,216]{2,1,0:T(8,128)(2,1)}, bf16[4,144,216]{2,1,0:T(8,128)(2,1)}, u32[]{:S(2)}, u32[]{:S(2)}) collective-permute-start(bf16[4,144,216]{2,1,0:T(8,128)(2,1)} %constant_dynamic-slice_fusion), channel_id=1, source_target_pairs={{0,16},{16,0},{1,17},{17,1},{2,18},{18,2},{3,19},{19,3},{4,20},{20... | collective-permute-start | bytes 746504 | tf_op jit(solution)/shard_map/ppermute | solution.py:301
  269.0 16.8 %all-to-all-start.6 = ((bf16[4,48,1152]{2,1,0:T(8,128)(2,1)}), bf16[4,48,1152]{2,1,0:T(8,128)(2,1)S(1)}, u32[]{:S(2)}, u32[]{:S(2)}) async-start(bf16[4,48,1152]{2,1,0:T(8,128)(2,1)} %bitcast.17), calls=%async_computation.6 | async-start | bytes 884736 | tf_op jit(solution)/shard_map/all_to_all | solution.py:304
  277.2 23.6 %collective-permute-start.29 = (bf16[4,144,538]{2,1,0:T(8,128)(2,1)}, bf16[4,144,538]{2,1,0:T(8,128)(2,1)}, u32[]{:S(2)}, u32[]{:S(2)}) collective-permute-start(bf16[4,144,538]{2,1,0:T(8,128)(2,1)} %all-to-all-done.9), channel_id=1, source_target_pairs={{0,16},{16,0},{1,17},{17,1},{2,18},{18,2},{3,19},{19,3},{4,20},{20... | collective-permute-start | bytes 1859336 | tf_op jit(solution)/shard_map/ppermute | solution.py:301
  289.2 24.2 %all-to-all-start.8 = ((bf16[4,272,288]{2,1,0:T(8,128)(2,1)}), bf16[4,272,288]{2,1,0:T(8,128)(2,1)S(1)}, u32[]{:S(2)}, u32[]{:S(2)}) async-start(bf16[4,272,288]{2,1,0:T(8,128)(2,1)} %shard_map.253), calls=%async_computation.8 | async-start | bytes 1671168 | tf_op jit(solution)/shard_map/all_to_all | solution.py:304
  293.4 6.5 %collective-permute-start.27 = (bf16[288,288]{1,0:T(8,128)(2,1)S(1)}, bf16[288,288]{1,0:T(8,128)(2,1)S(1)}, u32[]{:S(2)}, u32[]{:S(2)}) collective-permute-start(bf16[288,288]{1,0:T(8,128)(2,1)S(1)} %convolution_convert_fusion.6), channel_id=1, source_target_pairs={{0,16},{16,0},{1,17},{17,1},{2,18},{18,2},{3,19},{19,3},{4,20},{20... | collective-permute-start | bytes 497672 | tf_op jit(solution)/shard_map/ppermute | solution.py:301
  324.4 11.2 %collective-permute-start.26 = (bf16[4,144,216]{2,1,0:T(8,128)(2,1)S(1)}, bf16[4,144,216]{2,1,0:T(8,128)(2,1)S(1)}, u32[]{:S(2)}, u32[]{:S(2)}) collective-permute-start(bf16[4,144,216]{2,1,0:T(8,128)(2,1)S(1)} %slice.374), channel_id=1, source_target_pairs={{0,16},{16,0},{1,17},{17,1},{2,18},{18,2},{3,19},{19,3},{4,20},{20... | collective-permute-start | bytes 746504 | tf_op jit(solution)/shard_map/ppermute | solution.py:301
  326.8 7.5 %collective-permute-start.25 = (f32[11,288]{1,0:T(8,128)S(1)}, f32[11,288]{1,0:T(8,128)S(1)}, u32[]{:S(2)}, u32[]{:S(2)}) collective-permute-start(f32[11,288]{1,0:T(8,128)S(1)} %pad_maximum_fusion.8), channel_id=1, source_target_pairs={{0,16},{16,0},{1,17},{17,1},{2,18},{18,2},{3,19},{19,3},{4,20},{20... | collective-permute-start | bytes 38024 | tf_op jit(solution)/shard_map/ppermute | solution.py:301
  (71 other events, 477.9 us)

commit v3 on v2

--- a/solution.py
+++ b/solution.py
@@ -182,20 +182,6 @@
             out_ref[pl.ds(second, rows), :] = other_ref[i * rows : (i + 1) * rows, :]
 
     return local_call(kernel, outs, rank.reshape(1).astype(jnp.int32), mine, other)[0]
-
-
-def mlp_blocks(moved, rows, used):
-    sources = moved.shape[0]
-
-    def kernel(_, moved_ref, out_ref):
-        for i in range(sources):
-            at = slice(i * rows, (i + 1) * rows)
-            out_ref[at, :used] = moved_ref[i, :rows, :used]
-            out_ref[at, used : 2 * used] = moved_ref[i, rows:, :used]
-            out_ref[at, 2 * used :] = jnp.zeros((rows, out_ref.shape[1] - 2 * used), LOW)
-
-    outs = [((sources * rows, -(-2 * used // 128) * 128), moved.dtype)]
-    return local_call(kernel, outs, jnp.zeros((1,), jnp.int32), moved)[0]
 
 
 def mlp_join(mine, other, rank, groups, used, paired):
@@ -373,9 +359,6 @@
         def everywhere(value):
             return [value] * n_row
 
-        def fit_lanes(blocks):
-            return [jnp.pad(b, ((0, 0), (0, feats - b.shape[1]))) for b in blocks]
-
         def pack(*pieces):
             return straight(jnp.stack([jnp.concatenate(group, axis=0) for group in zip(*pieces)]))
 
@@ -430,8 +413,18 @@
             everywhere(own_block(cot_in)),
             everywhere(half_of(merge_in, rank, 0) if paired else merge_in),
         )
-        third_out = pack(
-            fit_lanes(weight_move(expand_in, units)), fit_lanes(weight_move_rows(reduce_in, units))
+        mlp_lanes = -(-2 * units // 128) * 128
+        third_out = straight(
+            jnp.stack(
+                [
+                    jnp.pad(
+                        jnp.concatenate([e, r], axis=1), ((0, 0), (0, mlp_lanes - 2 * units))
+                    )
+                    for e, r in zip(
+                        weight_move(expand_in, units), weight_move_rows(reduce_in, units)
+                    )
+                ]
+            )
         )
         second = row_exchange(after(second_out, first))
         third = row_exchange(after(third_out, second))
@@ -452,7 +445,7 @@
         cot_rows, merge_rows = split_blocks(
             second, ((0, block, feats, True), (block, half, feats, True))
         )
-        mlp_part = mlp_blocks(third, half, units)
+        mlp_part = third.reshape(n_row * half, mlp_lanes)
 
         residual = x_full.astype(WIDE)
         unit1, inv1 = norm_forward(residual)
@@ -481,9 +474,8 @@
 
         group_context = row_gather(after(own_context, third, merge_other)).reshape(n_row * head_size, padded)
         context_parts = col_parts(group_context)
-        expand_own, reduce_own = mlp_join(
-            mlp_part, after(mlp_other, context_parts[-1]), rank, n_row, units, paired
-        )
+        mlp_other = after(mlp_other, group_context)
+        expand_own, reduce_own = mlp_join(mlp_part, mlp_other, rank, n_row, units, paired)
         context_full = jnp.concatenate(
             [
                 align_lanes(part, offset, near) if offset else part

time: 340 us -> 334 us (0.982)
  starting transfers between devices: 63.4 us -> 59.5 us
    ppermute x9, starting transfers between devices: 12.7 us -> 8.91 us  [dp_swap(): return lax.ppermute(value, 'dp', [(0, 1), (1, 0)])]
    pallas_call x9 -> x8, Pallas kernels: 21.9 us -> 19.6 us  [local_call(): pl.pallas_call(kernel, out_shape=[jax.ShapeDtypeStruct(shape, kind) for s...]
    unnamed x165 -> x163, local copies, waits for them, and re-layouts: 18.1 us -> 18.1 us
  transfers between devices with their start and end apart: 40 -> 40, of which waited for: 20 -> 19; matrix products, arithmetic and copies ran while one was open for 25% -> 25% of each run, Pallas kernels for 5% -> 4%
where the time goes in v3:
time: 334 us; the launch traced here: 332 us
  waiting for transfers between devices  125 us (37%)
  starting transfers between devices  59.5 us (18%)
  local copies, waits for them, and re-layouts  49.6 us (15%)
  matrix products  34.3 us (10%)
  other arithmetic  32.2 us (10%)
  Pallas kernels  19.6 us (6%)
  blocking collectives  9.74 us (3%)
    all_to_all x10, waiting for transfers between devices, row_exchange(): return lax.all_to_all(blocks, 'row', 0, 0, tiled=True)  63.8 us
    ppermute x21, waiting for transfers between devices, col_swap(): return lax.ppermute(value, 'col', [(i, i ^ mask) for i in range(n_col)])  46.5 us
    all_to_all x10, starting transfers between devices, row_exchange(): return lax.all_to_all(blocks, 'row', 0, 0, tiled=True)  44.4 us
    dot_general x21, matrix products, dot(): lax.dot_general(left, right, (((left_dim,), (right_dim,)), ((), ())), pre...  34.3 us
    pallas_call x8, Pallas kernels, local_call(): pl.pallas_call(kernel, out_shape=[jax.ShapeDtypeStruct(shape, kind) for s...  19.6 us
    unnamed x163, local copies, waits for them, and re-layouts  18.1 us
    ppermute x9, waiting for transfers between devices, dp_swap(): return lax.ppermute(value, 'dp', [(0, 1), (1, 0)])  14.9 us
    all_gather x1, blocking collectives, body(): shared = lax.all_gather(spread_in, 'col')  9.74 us
  transfers between devices with their start and end apart: 40, of which 19 were waited for; matrix products, arithmetic and copies ran while one was open for 25% of the time, Pallas kernels for 4%

profile of v3, /device:TPU:0, one launch (start us, length us, event | category | flops | bytes accessed | tf_op | source)
XLA Modules:
  0.0 332.1 jit_solution(15848458612970911535)
XLA Ops:
  0.7 2.1 copy.112.input_ref
  3.3 3.2 shard_map.245
  6.5 2.3 copy.113
  8.8 6.5 %all-to-all-start = ((bf16[4,368,288]{1,2,0:T(8,128)(2,1)}), bf16[4,368,288]{1,2,0:T(8,128)(2,1)S(1)}, u32[]{:S(2)}, u32[]{:S(2)}) async-start(bf16[4,368,288]{1,2,0:T(8,128)(2,1)} %copy.113), calls=%async_computation | async-start | bytes 1769472 | tf_op jit(solution)/shard_map/all_to_all | solution.py:290
  18.6 18.9 %all-to-all-done = bf16[4,368,288]{1,2,0:T(8,128)(2,1)S(1)} async-done(((bf16[4,368,288]{1,2,0:T(8,128)(2,1)}), bf16[4,368,288]{1,2,0:T(8,128)(2,1)S(1)}, u32[]{:S(2)}, u32[]{:S(2)}) %all-to-all-start) | async-done | bytes 847904 | tf_op jit(solution)/shard_map/all_to_all | solution.py:290
  38.9 2.4 shard_map.246
  44.3 3.5 %all-to-all-start.1 = ((bf16[4,336,288]{1,2,0:T(8,128)(2,1)}), bf16[4,336,288]{1,2,0:T(8,128)(2,1)S(1)}, u32[]{:S(2)}, u32[]{:S(2)}) async-start(bf16[4,336,288]{1,2,0:T(8,128)(2,1)} %copy.117), calls=%async_computation.1 | async-start | bytes 1769472 | tf_op jit(solution)/shard_map/all_to_all | solution.py:290
  49.4 4.7 %collective-permute-done = bf16[192,1152]{1,0:T(8,128)(2,1)S(1)} collective-permute-done((bf16[192,1152]{1,0:T(8,128)(2,1)}, bf16[192,1152]{1,0:T(8,128)(2,1)S(1)}, u32[]{:S(2)}, u32[]{:S(2)}) %collective-permute-start) | collective-permute-done | bytes 442400 | tf_op jit(solution)/shard_map/ppermute | solution.py:284
  57.7 1.9 shard_map.247
  60.3 10.3 %all-to-all-done.1 = bf16[4,336,288]{1,2,0:T(8,128)(2,1)S(1)} async-done(((bf16[4,336,288]{1,2,0:T(8,128)(2,1)}), bf16[4,336,288]{1,2,0:T(8,128)(2,1)S(1)}, u32[]{:S(2)}, u32[]{:S(2)}) %all-to-all-start.1) | async-done | bytes 774176 | tf_op jit(solution)/shard_map/all_to_all | solution.py:290
  70.6 4.2 %all-to-all-start.2 = ((bf16[4,144,640]{2,1,0:T(8,128)(2,1)}), bf16[4,144,640]{2,1,0:T(8,128)(2,1)}, u32[]{:S(2)}, u32[]{:S(2)}) async-start(bf16[4,144,640]{2,1,0:T(8,128)(2,1)} %pad_maximum_fusion.2), calls=%async_computation.2 | async-start | bytes 1474560 | tf_op jit(solution)/shard_map/all_to_all | solution.py:290
  80.1 2.3 shard_map.248
  86.9 4.9 %collective-permute-done.8.other_ref = bf16[144,1152]{1,0:T(8,128)(2,1)} collective-permute-done((bf16[144,1152]{1,0:T(8,128)(2,1)}, bf16[144,1152]{1,0:T(8,128)(2,1)}, u32[]{:S(2)}, u32[]{:S(2)}) %collective-permute-start.8) | collective-permute-done | bytes 331808 | tf_op jit(solution)/shard_map/ppermute | solution.py:287
  91.8 1.9 all-to-all-done.2
  94.4 3.6 %all-to-all-start.3 = ((bf16[4,72,768]{2,1,0:T(8,128)(2,1)}), bf16[4,72,768]{2,1,0:T(8,128)(2,1)S(1)}, u32[]{:S(2)}, u32[]{:S(2)}) async-start(bf16[4,72,768]{2,1,0:T(8,128)(2,1)} %broadcast_in_dim.7), calls=%async_computation.3 | async-start | bytes 884736 | tf_op jit(solution)/shard_map/all_to_all | solution.py:290
  102.2 2.0 shard_map.250
  105.6 4.6 %all-to-all-done.3 = bf16[4,72,768]{2,1,0:T(8,128)(2,1)S(1)} async-done(((bf16[4,72,768]{2,1,0:T(8,128)(2,1)}), bf16[4,72,768]{2,1,0:T(8,128)(2,1)S(1)}, u32[]{:S(2)}, u32[]{:S(2)}) %all-to-all-start.3) | async-done | bytes 442400 | tf_op jit(solution)/shard_map/all_to_all | solution.py:290
  112.6 9.7 %collective-permute-done.12 = bf16[288,1152]{1,0:T(8,128)(2,1)} collective-permute-done((bf16[288,1152]{1,0:T(8,128)(2,1)}, bf16[288,1152]{1,0:T(8,128)(2,1)}, u32[]{:S(2)}, u32[]{:S(2)}) %collective-permute-start.12) | collective-permute-done | bytes 663584 | tf_op jit(solution)/shard_map/ppermute | solution.py:284
  122.3 2.9 shard_map.249
  125.2 5.8 %collective-permute-done.9 = bf16[288,768]{1,0:T(8,128)(2,1)} collective-permute-done((bf16[288,768]{1,0:T(8,128)(2,1)S(1)}, bf16[288,768]{1,0:T(8,128)(2,1)}, u32[]{:S(2)}, u32[]{:S(2)}) %collective-permute-start.9) | collective-permute-done | bytes 442400 | tf_op jit(solution)/shard_map/ppermute | solution.py:284
  133.7 4.8 %fusion.117 = (f32[768]{0:T(1024)S(1)}, f32[768]{0:T(1024)S(1)}, f32[768,1152]{1,0:T(8,128)S(1)}) fusion(f32[1152]{0:T(1024)S(1)} %copy-done.73, bf16[288,1152]{1,0:T(8,128)(2,1)} %collective-permute-done.14, bf16[288,1152]{1,0:T(8,128)(2,1)} %collective-permute-done.13, bf16[288,1152]{1,0:T(8,128)(2,1)} %collective-permute-done.12, ...), kind=kOutput, calls=%fused_computation.255 | convolution fusion | flops 2080012800 | bytes 9742848 | tf_op jit(solution)/shard_map/dot_general | solution.py:29
  146.3 2.1 collective-permute-done.15
  150.4 12.1 %collective-permute-done.16 = bf16[192,1152]{1,0:T(8,128)(2,1)S(1)} collective-permute-done((bf16[192,1152]{1,0:T(8,128)(2,1)}, bf16[192,1152]{1,0:T(8,128)(2,1)S(1)}, u32[]{:S(2)}, u32[]{:S(2)}) %collective-permute-start.16) | collective-permute-done | bytes 442400 | tf_op jit(solution)/shard_map/ppermute | solution.py:284
  163.4 4.9 %all-to-all-start.4 = ((bf16[4,48,1152]{2,1,0:T(8,128)(2,1)}), bf16[4,48,1152]{2,1,0:T(8,128)(2,1)S(1)}, u32[]{:S(2)}, u32[]{:S(2)}) async-start(bf16[4,48,1152]{2,1,0:T(8,128)(2,1)} %bitcast.14), calls=%async_computation.4 | async-start | bytes 884736 | tf_op jit(solution)/shard_map/all_to_all | solution.py:290
  168.3 3.0 convolution_convert_fusion
  175.2 5.5 %all-to-all-done.4.part_ref = bf16[4,48,1152]{2,1,0:T(8,128)(2,1)S(1)} async-done(((bf16[4,48,1152]{2,1,0:T(8,128)(2,1)}), bf16[4,48,1152]{2,1,0:T(8,128)(2,1)S(1)}, u32[]{:S(2)}, u32[]{:S(2)}) %all-to-all-start.4) | async-done | bytes 442400 | tf_op jit(solution)/shard_map/all_to_all | solution.py:290
  181.5 2.3 shard_map.251
  183.7 3.7 %all-to-all-start.5 = ((bf16[4,48,1152]{2,1,0:T(8,128)(2,1)}), bf16[4,48,1152]{2,1,0:T(8,128)(2,1)S(1)}, u32[]{:S(2)}, u32[]{:S(2)}) async-start(bf16[4,48,1152]{2,1,0:T(8,128)(2,1)} %get-tuple-element.50), calls=%async_computation.5 | async-start | bytes 884736 | tf_op jit(solution)/shard_map/all_to_all | solution.py:290
  187.5 1.9 convert_add_fusion.1
  191.9 7.5 %all-to-all-done.5 = bf16[4,48,1152]{2,1,0:T(8,128)(2,1)S(1)} async-done(((bf16[4,48,1152]{2,1,0:T(8,128)(2,1)}), bf16[4,48,1152]{2,1,0:T(8,128)(2,1)S(1)}, u32[]{:S(2)}, u32[]{:S(2)}) %all-to-all-start.5) | async-done | bytes 442400 | tf_op jit(solution)/shard_map/all_to_all | solution.py:290
  200.0 2.7 convolution_convert_fusion.4
  203.2 3.4 %convolution_convert_fusion.3 = bf16[1152,269]{0,1:T(8,128)(2,1)} fusion(bf16[768,1152]{1,0:T(8,128)(2,1)} %constant_dynamic-update-slice_fusion, bf16[768,269]{0,1:T(8,128)(2,1)} %get-tuple-element.53), kind=kOutput, calls=%fused_computation.36 | convolution fusion | flops 476297856 | bytes 2802432 | tf_op jit(solution)/shard_map/dot_general | solution.py:29
  209.8 2.6 collective-permute-done.17
  214.2 4.5 %all-to-all-start.7 = ((bf16[4,48,1152]{2,1,0:T(8,128)(2,1)}), bf16[4,48,1152]{2,1,0:T(8,128)(2,1)}, u32[]{:S(2)}, u32[]{:S(2)}) async-start(bf16[4,48,1152]{2,1,0:T(8,128)(2,1)} %bitcast.20), calls=%async_computation.7 | async-start | bytes 884736 | tf_op jit(solution)/shard_map/all_to_all | solution.py:290
  229.4 3.0 fusion.1
  235.3 2.5 add_convert_fusion.2
  237.7 4.9 %all-to-all-start.9 = ((bf16[4,144,538]{2,1,0:T(8,128)(2,1)}), bf16[4,144,538]{2,1,0:T(8,128)(2,1)}, u32[]{:S(2)}, u32[]{:S(2)}) async-start(bf16[4,144,538]{2,1,0:T(8,128)(2,1)} %add_convert_fusion.2), calls=%async_computation.9 | async-start | bytes 1474560 | tf_op jit(solution)/shard_map/all_to_all | solution.py:290
  242.7 1.9 convert_reduce_fusion.2
  251.5 9.5 %collective-permute-done.21 = bf16[192,1152]{1,0:T(8,128)(2,1)} collective-permute-done((bf16[192,1152]{1,0:T(8,128)(2,1)}, bf16[192,1152]{1,0:T(8,128)(2,1)}, u32[]{:S(2)}, u32[]{:S(2)}) %collective-permute-start.21) | collective-permute-done | bytes 442400 | tf_op jit(solution)/shard_map/ppermute | solution.py:284
  261.0 2.1 fusion.36
  263.1 4.8 %all-to-all-start.6 = ((bf16[4,48,1152]{2,1,0:T(8,128)(2,1)}), bf16[4,48,1152]{2,1,0:T(8,128)(2,1)S(1)}, u32[]{:S(2)}, u32[]{:S(2)}) async-start(bf16[4,48,1152]{2,1,0:T(8,128)(2,1)} %bitcast.18), calls=%async_computation.6 | async-start | bytes 884736 | tf_op jit(solution)/shard_map/all_to_all | solution.py:290
  271.9 8.0 %all-to-all-done.6.part_ref = bf16[4,48,1152]{2,1,0:T(8,128)(2,1)S(1)} async-done(((bf16[4,48,1152]{2,1,0:T(8,128)(2,1)}), bf16[4,48,1152]{2,1,0:T(8,128)(2,1)S(1)}, u32[]{:S(2)}, u32[]{:S(2)}) %all-to-all-start.6) | async-done | bytes 442400 | tf_op jit(solution)/shard_map/all_to_all | solution.py:290
  280.7 2.6 shard_map.252
  283.3 3.8 %all-to-all-start.8 = ((bf16[4,272,288]{2,1,0:T(8,128)(2,1)}), bf16[4,272,288]{2,1,0:T(8,128)(2,1)S(1)}, u32[]{:S(2)}, u32[]{:S(2)}) async-start(bf16[4,272,288]{2,1,0:T(8,128)(2,1)} %shard_map.252), calls=%async_computation.8 | async-start | bytes 1671168 | tf_op jit(solution)/shard_map/all_to_all | solution.py:290
  289.4 4.7 %collective-permute-done.27 = bf16[288,288]{1,0:T(8,128)(2,1)S(1)} collective-permute-done((bf16[288,288]{1,0:T(8,128)(2,1)S(1)}, bf16[288,288]{1,0:T(8,128)(2,1)S(1)}, u32[]{:S(2)}, u32[]{:S(2)}) %collective-permute-start.27) | collective-permute-done | bytes 165920 | tf_op jit(solution)/shard_map/ppermute | solution.py:287
  300.4 7.1 %all-to-all-done.8 = bf16[4,272,288]{2,1,0:T(8,128)(2,1)S(1)} async-done(((bf16[4,272,288]{2,1,0:T(8,128)(2,1)}), bf16[4,272,288]{2,1,0:T(8,128)(2,1)S(1)}, u32[]{:S(2)}, u32[]{:S(2)}) %all-to-all-start.8) | async-done | bytes 626720 | tf_op jit(solution)/shard_map/all_to_all | solution.py:290
  308.7 9.7 %all-gather.1 = bf16[4,417,288]{1,2,0:T(8,128)(2,1)S(1)} all-gather(bf16[1,417,288]{1,2,0:T(8,128)(2,1)S(1)} %maximum_bitcast_fusion), channel_id=2, replica_groups=mesh['dp'=2,'row'=4,'col'=4] {'col'}, dimensions={0}, use_global_device_ids=true | all-gather | bytes 1200960 | tf_op jit(solution)/shard_map/all_gather | solution.py:578
  324.8 3.6 %collective-permute-done.25 = f32[11,288]{1,0:T(8,128)S(1)} collective-permute-done((f32[11,288]{1,0:T(8,128)S(1)}, f32[11,288]{1,0:T(8,128)S(1)}, u32[]{:S(2)}, u32[]{:S(2)}) %collective-permute-start.25) | collective-permute-done | bytes 12704 | tf_op jit(solution)/shard_map/ppermute | solution.py:287
  (335 shorter events, 103.3 us)
Async XLA Ops:
  8.8 28.7 %all-to-all-start = ((bf16[4,368,288]{1,2,0:T(8,128)(2,1)}), bf16[4,368,288]{1,2,0:T(8,128)(2,1)S(1)}, u32[]{:S(2)}, u32[]{:S(2)}) async-start(bf16[4,368,288]{1,2,0:T(8,128)(2,1)} %copy.113), calls=%async_computation | async-start | bytes 1769472 | tf_op jit(solution)/shard_map/all_to_all | solution.py:290
  41.3 18.4 %collective-permute-start.1 = (bf16[192,1152]{1,0:T(8,128)(2,1)}, bf16[192,1152]{1,0:T(8,128)(2,1)S(1)}, u32[]{:S(2)}, u32[]{:S(2)}) collective-permute-start(bf16[192,1152]{1,0:T(8,128)(2,1)} %get-tuple-element.35), channel_id=1, source_target_pairs={{0,1},{1,0},{2,3},{3,2},{4,5},{5,4},{6,7},{7,6},{8,9},{9,8},{10,11... | collective-permute-start | bytes 1327112 | tf_op jit(solution)/shard_map/ppermute | solution.py:284
  41.3 12.8 %collective-permute-start = (bf16[192,1152]{1,0:T(8,128)(2,1)}, bf16[192,1152]{1,0:T(8,128)(2,1)S(1)}, u32[]{:S(2)}, u32[]{:S(2)}) collective-permute-start(bf16[192,1152]{1,0:T(8,128)(2,1)} %get-tuple-element.35), channel_id=1, source_target_pairs={{0,2},{1,3},{2,0},{3,1},{4,6},{5,7},{6,4},{7,5},{8,10},{9,11},{10,... | collective-permute-start | bytes 1327112 | tf_op jit(solution)/shard_map/ppermute | solution.py:284
  44.3 26.3 %all-to-all-start.1 = ((bf16[4,336,288]{1,2,0:T(8,128)(2,1)}), bf16[4,336,288]{1,2,0:T(8,128)(2,1)S(1)}, u32[]{:S(2)}, u32[]{:S(2)}) async-start(bf16[4,336,288]{1,2,0:T(8,128)(2,1)} %copy.117), calls=%async_computation.1 | async-start | bytes 1769472 | tf_op jit(solution)/shard_map/all_to_all | solution.py:290
  47.9 9.1 %collective-permute-start.3 = (bf16[576,216]{1,0:T(8,128)(2,1)S(1)}, bf16[576,216]{1,0:T(8,128)(2,1)S(1)}, u32[]{:S(2)}, u32[]{:S(2)}) collective-permute-start(bf16[576,216]{1,0:T(8,128)(2,1)S(1)} %copy-done.56), channel_id=1, source_target_pairs={{0,16},{16,0},{1,17},{17,1},{2,18},{18,2},{3,19},{19,3},{4,20},{20... | collective-permute-start | bytes 746504 | tf_op jit(solution)/shard_map/ppermute | solution.py:287
  54.1 22.6 %copy-start.30 = (bf16[192,1152]{1,0:T(8,128)(2,1)}, bf16[192,1152]{1,0:T(8,128)(2,1)S(1)}, u32[]{:S(2)}) copy-start(bf16[192,1152]{1,0:T(8,128)(2,1)S(1)} %collective-permute-done) | copy-start | bytes 1327108
  54.1 5.6 %collective-permute-start.2 = (bf16[192,1152]{1,0:T(8,128)(2,1)S(1)}, bf16[192,1152]{1,0:T(8,128)(2,1)S(1)}, u32[]{:S(2)}, u32[]{:S(2)}) collective-permute-start(bf16[192,1152]{1,0:T(8,128)(2,1)S(1)} %collective-permute-done), channel_id=1, source_target_pairs={{0,1},{1,0},{2,3},{3,2},{4,5},{5,4},{6,7},{7,6},{8,9},{9,8},{10,11... | collective-permute-start | bytes 1327112 | tf_op jit(solution)/shard_map/ppermute | solution.py:284
  70.6 23.1 %all-to-all-start.2 = ((bf16[4,144,640]{2,1,0:T(8,128)(2,1)}), bf16[4,144,640]{2,1,0:T(8,128)(2,1)}, u32[]{:S(2)}, u32[]{:S(2)}) async-start(bf16[4,144,640]{2,1,0:T(8,128)(2,1)} %pad_maximum_fusion.2), calls=%async_computation.2 | async-start | bytes 1474560 | tf_op jit(solution)/shard_map/all_to_all | solution.py:290
  82.5 9.3 %collective-permute-start.8 = (bf16[144,1152]{1,0:T(8,128)(2,1)}, bf16[144,1152]{1,0:T(8,128)(2,1)}, u32[]{:S(2)}, u32[]{:S(2)}) collective-permute-start(bf16[144,1152]{1,0:T(8,128)(2,1)} %get-tuple-element.45.mine_ref), channel_id=1, source_target_pairs={{0,16},{16,0},{1,17},{17,1},{2,18},{18,2},{3,19},{19,3},{4,20},{20... | collective-permute-start | bytes 995336 | tf_op jit(solution)/shard_map/ppermute | solution.py:287
  85.1 19.6 %collective-permute-start.4 = (bf16[192,1152]{1,0:T(8,128)(2,1)}, bf16[192,1152]{1,0:T(8,128)(2,1)S(1)}, u32[]{:S(2)}, u32[]{:S(2)}) collective-permute-start(bf16[192,1152]{1,0:T(8,128)(2,1)} %get-tuple-element.41), channel_id=1, source_target_pairs={{0,2},{1,3},{2,0},{3,1},{4,6},{5,7},{6,4},{7,5},{8,10},{9,11},{10,... | collective-permute-start | bytes 1327112 | tf_op jit(solution)/shard_map/ppermute | solution.py:284
  94.4 15.7 %all-to-all-start.3 = ((bf16[4,72,768]{2,1,0:T(8,128)(2,1)}), bf16[4,72,768]{2,1,0:T(8,128)(2,1)S(1)}, u32[]{:S(2)}, u32[]{:S(2)}) async-start(bf16[4,72,768]{2,1,0:T(8,128)(2,1)} %broadcast_in_dim.7), calls=%async_computation.3 | async-start | bytes 884736 | tf_op jit(solution)/shard_map/all_to_all | solution.py:290
  98.9 11.3 %collective-permute-start.5 = (bf16[192,1152]{1,0:T(8,128)(2,1)}, bf16[192,1152]{1,0:T(8,128)(2,1)S(1)}, u32[]{:S(2)}, u32[]{:S(2)}) collective-permute-start(bf16[192,1152]{1,0:T(8,128)(2,1)} %get-tuple-element.41), channel_id=1, source_target_pairs={{0,1},{1,0},{2,3},{3,2},{4,5},{5,4},{6,7},{7,6},{8,9},{9,8},{10,11... | collective-permute-start | bytes 1327112 | tf_op jit(solution)/shard_map/ppermute | solution.py:284
  98.9 23.4 %collective-permute-start.7 = (bf16[576,640]{1,0:T(8,128)(2,1)}, bf16[576,640]{1,0:T(8,128)(2,1)}, u32[]{:S(2)}, u32[]{:S(2)}) collective-permute-start(bf16[576,640]{1,0:T(8,128)(2,1)} %bitcast.12.mine_ref), channel_id=1, source_target_pairs={{0,16},{16,0},{1,17},{17,1},{2,18},{18,2},{3,19},{19,3},{4,20},{20... | collective-permute-start | bytes 2211848 | tf_op jit(solution)/shard_map/ppermute | solution.py:287
  104.2 18.1 %collective-permute-start.12 = (bf16[288,1152]{1,0:T(8,128)(2,1)}, bf16[288,1152]{1,0:T(8,128)(2,1)}, u32[]{:S(2)}, u32[]{:S(2)}) collective-permute-start(bf16[288,1152]{1,0:T(8,128)(2,1)} %shard_map.250), channel_id=1, source_target_pairs={{0,2},{1,3},{2,0},{3,1},{4,6},{5,7},{6,4},{7,5},{8,10},{9,11},{10,... | collective-permute-start | bytes 1990664 | tf_op jit(solution)/shard_map/ppermute | solution.py:284
  104.7 6.9 %collective-permute-start.6 = (bf16[192,1152]{1,0:T(8,128)(2,1)S(1)}, bf16[192,1152]{1,0:T(8,128)(2,1)S(1)}, u32[]{:S(2)}, u32[]{:S(2)}) collective-permute-start(bf16[192,1152]{1,0:T(8,128)(2,1)S(1)} %collective-permute-done.4), channel_id=1, source_target_pairs={{0,1},{1,0},{2,3},{3,2},{4,5},{5,4},{6,7},{7,6},{8,9},{9,8},{10,11... | collective-permute-start | bytes 1327112 | tf_op jit(solution)/shard_map/ppermute | solution.py:284
  110.2 23.5 %copy-start.18 = (bf16[4,72,768]{2,1,0:T(8,128)(2,1)}, bf16[4,72,768]{2,1,0:T(8,128)(2,1)S(1)}, u32[]{:S(2)}) copy-start(bf16[4,72,768]{2,1,0:T(8,128)(2,1)S(1)} %all-to-all-done.3) | copy-start | bytes 1327108
  110.2 20.9 %collective-permute-start.10 = (bf16[288,768]{1,0:T(8,128)(2,1)S(1)}, bf16[288,768]{1,0:T(8,128)(2,1)}, u32[]{:S(2)}, u32[]{:S(2)}) collective-permute-start(bf16[288,768]{1,0:T(8,128)(2,1)S(1)} %bitcast.115), channel_id=1, source_target_pairs={{0,1},{1,0},{2,3},{3,2},{4,5},{5,4},{6,7},{7,6},{8,9},{9,8},{10,11... | collective-permute-start | bytes 1327112 | tf_op jit(solution)/shard_map/ppermute | solution.py:284
  110.2 20.8 %collective-permute-start.9 = (bf16[288,768]{1,0:T(8,128)(2,1)S(1)}, bf16[288,768]{1,0:T(8,128)(2,1)}, u32[]{:S(2)}, u32[]{:S(2)}) collective-permute-start(bf16[288,768]{1,0:T(8,128)(2,1)S(1)} %bitcast.116), channel_id=1, source_target_pairs={{0,2},{1,3},{2,0},{3,1},{4,6},{5,7},{6,4},{7,5},{8,10},{9,11},{10,... | collective-permute-start | bytes 1327112 | tf_op jit(solution)/shard_map/ppermute | solution.py:284
  111.6 22.1 %collective-permute-start.13 = (bf16[288,1152]{1,0:T(8,128)(2,1)}, bf16[288,1152]{1,0:T(8,128)(2,1)}, u32[]{:S(2)}, u32[]{:S(2)}) collective-permute-start(bf16[288,1152]{1,0:T(8,128)(2,1)} %shard_map.250), channel_id=1, source_target_pairs={{0,1},{1,0},{2,3},{3,2},{4,5},{5,4},{6,7},{7,6},{8,9},{9,8},{10,11... | collective-permute-start | bytes 1990664 | tf_op jit(solution)/shard_map/ppermute | solution.py:284
  112.5 21.1 %copy-start.23 = (bf16[192,1152]{1,0:T(8,128)(2,1)S(1)}, bf16[192,1152]{1,0:T(8,128)(2,1)}, u32[]{:S(2)}) copy-start(bf16[192,1152]{1,0:T(8,128)(2,1)} %get-tuple-element.35) | copy-start | bytes 1327108
  112.5 21.1 %copy-start.27 = (bf16[192,1152]{1,0:T(8,128)(2,1)S(1)}, bf16[192,1152]{1,0:T(8,128)(2,1)}, u32[]{:S(2)}) copy-start(bf16[192,1152]{1,0:T(8,128)(2,1)} %copy-done.26) | copy-start | bytes 1327108
  112.5 21.1 %copy-start.31 = (bf16[192,1152]{1,0:T(8,128)(2,1)S(1)}, bf16[192,1152]{1,0:T(8,128)(2,1)}, u32[]{:S(2)}) copy-start(bf16[192,1152]{1,0:T(8,128)(2,1)} %copy-done.30) | copy-start | bytes 1327108
  112.5 21.1 %copy-start.35 = (bf16[192,1152]{1,0:T(8,128)(2,1)S(1)}, bf16[192,1152]{1,0:T(8,128)(2,1)}, u32[]{:S(2)}) copy-start(bf16[192,1152]{1,0:T(8,128)(2,1)} %copy-done.34) | copy-start | bytes 1327108
  112.5 21.2 %copy-start.73 = (f32[1152]{0:T(1024)S(1)}, f32[1152]{0:T(1024)}, u32[]{:S(2)}) copy-start(f32[1152]{0:T(1024)} %get-tuple-element.134) | copy-start | bytes 13828
  122.3 11.3 %collective-permute-start.14 = (bf16[288,1152]{1,0:T(8,128)(2,1)}, bf16[288,1152]{1,0:T(8,128)(2,1)}, u32[]{:S(2)}, u32[]{:S(2)}) collective-permute-start(bf16[288,1152]{1,0:T(8,128)(2,1)} %collective-permute-done.12), channel_id=1, source_target_pairs={{0,1},{1,0},{2,3},{3,2},{4,5},{5,4},{6,7},{7,6},{8,9},{9,8},{10,11... | collective-permute-start | bytes 1990664 | tf_op jit(solution)/shard_map/ppermute | solution.py:284
  131.0 2.4 collective-permute-start.11
  145.7 2.6 collective-permute-start.15
  149.9 12.7 %collective-permute-start.16 = (bf16[192,1152]{1,0:T(8,128)(2,1)}, bf16[192,1152]{1,0:T(8,128)(2,1)S(1)}, u32[]{:S(2)}, u32[]{:S(2)}) collective-permute-start(bf16[192,1152]{1,0:T(8,128)(2,1)} %slice.559), channel_id=1, source_target_pairs={{0,2},{1,3},{2,0},{3,1},{4,6},{5,7},{6,4},{7,5},{8,10},{9,11},{10,... | collective-permute-start | bytes 1327112 | tf_op jit(solution)/shard_map/ppermute | solution.py:284
  163.4 17.3 %all-to-all-start.4 = ((bf16[4,48,1152]{2,1,0:T(8,128)(2,1)}), bf16[4,48,1152]{2,1,0:T(8,128)(2,1)S(1)}, u32[]{:S(2)}, u32[]{:S(2)}) async-start(bf16[4,48,1152]{2,1,0:T(8,128)(2,1)} %bitcast.14), calls=%async_computation.4 | async-start | bytes 884736 | tf_op jit(solution)/shard_map/all_to_all | solution.py:290
  168.3 19.2 %copy-start.51 = (bf16[768,269]{0,1:T(8,128)(2,1)S(1)}, bf16[768,269]{0,1:T(8,128)(2,1)}, u32[]{:S(2)}) copy-start(bf16[768,269]{0,1:T(8,128)(2,1)} %get-tuple-element.53) | copy-start | bytes 1239556
  171.3 16.1 %collective-permute-start.22 = (bf16[384,1152]{1,0:T(8,128)(2,1)}, bf16[384,1152]{1,0:T(8,128)(2,1)}, u32[]{:S(2)}, u32[]{:S(2)}) collective-permute-start(bf16[384,1152]{1,0:T(8,128)(2,1)} %convolution_convert_fusion), channel_id=1, source_target_pairs={{0,1},{1,0},{2,3},{3,2},{4,5},{5,4},{6,7},{7,6},{8,9},{9,8},{10,11... | collective-permute-start | bytes 2654216 | tf_op jit(solution)/shard_map/ppermute | solution.py:284
  183.7 15.7 %all-to-all-start.5 = ((bf16[4,48,1152]{2,1,0:T(8,128)(2,1)}), bf16[4,48,1152]{2,1,0:T(8,128)(2,1)S(1)}, u32[]{:S(2)}, u32[]{:S(2)}) async-start(bf16[4,48,1152]{2,1,0:T(8,128)(2,1)} %get-tuple-element.50), calls=%async_computation.5 | async-start | bytes 884736 | tf_op jit(solution)/shard_map/all_to_all | solution.py:290
  191.4 21.0 %collective-permute-start.23 = (bf16[192,1152]{1,0:T(8,128)(2,1)}, bf16[192,1152]{1,0:T(8,128)(2,1)}, u32[]{:S(2)}, u32[]{:S(2)}) collective-permute-start(bf16[192,1152]{1,0:T(8,128)(2,1)} %slice.557), channel_id=1, source_target_pairs={{0,2},{1,3},{2,0},{3,1},{4,6},{5,7},{6,4},{7,5},{8,10},{9,11},{10,... | collective-permute-start | bytes 1327112 | tf_op jit(solution)/shard_map/ppermute | solution.py:284
  199.4 12.9 %collective-permute-start.17 = (bf16[192,1152]{1,0:T(8,128)(2,1)S(1)}, bf16[192,1152]{1,0:T(8,128)(2,1)}, u32[]{:S(2)}, u32[]{:S(2)}) collective-permute-start(bf16[192,1152]{1,0:T(8,128)(2,1)S(1)} %bitcast.119), channel_id=1, source_target_pairs={{0,2},{1,3},{2,0},{3,1},{4,6},{5,7},{6,4},{7,5},{8,10},{9,11},{10,... | collective-permute-start | bytes 1327112 | tf_op jit(solution)/shard_map/ppermute | solution.py:284
  209.2 26.1 %collective-permute-start.28 = (bf16[4,144,538]{2,1,0:T(8,128)(2,1)}, bf16[4,144,538]{2,1,0:T(8,128)(2,1)}, u32[]{:S(2)}, u32[]{:S(2)}) collective-permute-start(bf16[4,144,538]{2,1,0:T(8,128)(2,1)} %fusion.43), channel_id=1, source_target_pairs={{0,16},{16,0},{1,17},{17,1},{2,18},{18,2},{3,19},{19,3},{4,20},{20... | collective-permute-start | bytes 1859336 | tf_op jit(solution)/shard_map/ppermute | solution.py:287
  209.8 9.0 %collective-permute-start.18 = (bf16[192,1152]{1,0:T(8,128)(2,1)S(1)}, bf16[192,1152]{1,0:T(8,128)(2,1)S(1)}, u32[]{:S(2)}, u32[]{:S(2)}) collective-permute-start(bf16[192,1152]{1,0:T(8,128)(2,1)S(1)} %bitcast.120), channel_id=1, source_target_pairs={{0,1},{1,0},{2,3},{3,2},{4,5},{5,4},{6,7},{7,6},{8,9},{9,8},{10,11... | collective-permute-start | bytes 1327112 | tf_op jit(solution)/shard_map/ppermute | solution.py:284
  212.4 7.2 %collective-permute-start.19 = (bf16[192,1152]{1,0:T(8,128)(2,1)}, bf16[192,1152]{1,0:T(8,128)(2,1)}, u32[]{:S(2)}, u32[]{:S(2)}) collective-permute-start(bf16[192,1152]{1,0:T(8,128)(2,1)} %collective-permute-done.17), channel_id=1, source_target_pairs={{0,1},{1,0},{2,3},{3,2},{4,5},{5,4},{6,7},{7,6},{8,9},{9,8},{10,11... | collective-permute-start | bytes 1327112 | tf_op jit(solution)/shard_map/ppermute | solution.py:284
  214.2 23.5 %all-to-all-start.7 = ((bf16[4,48,1152]{2,1,0:T(8,128)(2,1)}), bf16[4,48,1152]{2,1,0:T(8,128)(2,1)}, u32[]{:S(2)}, u32[]{:S(2)}) async-start(bf16[4,48,1152]{2,1,0:T(8,128)(2,1)} %bitcast.20), calls=%async_computation.7 | async-start | bytes 884736 | tf_op jit(solution)/shard_map/all_to_all | solution.py:290
  229.1 15.5 %collective-permute-start.20 = (bf16[384,1152]{1,0:T(8,128)(2,1)}, bf16[384,1152]{1,0:T(8,128)(2,1)}, u32[]{:S(2)}, u32[]{:S(2)}) collective-permute-start(bf16[384,1152]{1,0:T(8,128)(2,1)} %convolution_convert_fusion.2), channel_id=1, source_target_pairs={{0,1},{1,0},{2,3},{3,2},{4,5},{5,4},{6,7},{7,6},{8,9},{9,8},{10,11... | collective-permute-start | bytes 2654216 | tf_op jit(solution)/shard_map/ppermute | solution.py:284
  237.7 25.4 %all-to-all-start.9 = ((bf16[4,144,538]{2,1,0:T(8,128)(2,1)}), bf16[4,144,538]{2,1,0:T(8,128)(2,1)}, u32[]{:S(2)}, u32[]{:S(2)}) async-start(bf16[4,144,538]{2,1,0:T(8,128)(2,1)} %add_convert_fusion.2), calls=%async_computation.9 | async-start | bytes 1474560 | tf_op jit(solution)/shard_map/all_to_all | solution.py:290
  248.4 12.6 %collective-permute-start.21 = (bf16[192,1152]{1,0:T(8,128)(2,1)}, bf16[192,1152]{1,0:T(8,128)(2,1)}, u32[]{:S(2)}, u32[]{:S(2)}) collective-permute-start(bf16[192,1152]{1,0:T(8,128)(2,1)} %slice.558), channel_id=1, source_target_pairs={{0,2},{1,3},{2,0},{3,1},{4,6},{5,7},{6,4},{7,5},{8,10},{9,11},{10,... | collective-permute-start | bytes 1327112 | tf_op jit(solution)/shard_map/ppermute | solution.py:284
  251.0 18.6 %collective-permute-start.24 = (bf16[4,144,216]{2,1,0:T(8,128)(2,1)}, bf16[4,144,216]{2,1,0:T(8,128)(2,1)}, u32[]{:S(2)}, u32[]{:S(2)}) collective-permute-start(bf16[4,144,216]{2,1,0:T(8,128)(2,1)} %constant_dynamic-slice_fusion.1), channel_id=1, source_target_pairs={{0,16},{16,0},{1,17},{17,1},{2,18},{18,2},{3,19},{19,3},{4,20},{20... | collective-permute-start | bytes 746504 | tf_op jit(solution)/shard_map/ppermute | solution.py:287
  263.1 16.8 %all-to-all-start.6 = ((bf16[4,48,1152]{2,1,0:T(8,128)(2,1)}), bf16[4,48,1152]{2,1,0:T(8,128)(2,1)S(1)}, u32[]{:S(2)}, u32[]{:S(2)}) async-start(bf16[4,48,1152]{2,1,0:T(8,128)(2,1)} %bitcast.18), calls=%async_computation.6 | async-start | bytes 884736 | tf_op jit(solution)/shard_map/all_to_all | solution.py:290
  271.4 23.6 %collective-permute-start.29 = (bf16[4,144,538]{2,1,0:T(8,128)(2,1)}, bf16[4,144,538]{2,1,0:T(8,128)(2,1)}, u32[]{:S(2)}, u32[]{:S(2)}) collective-permute-start(bf16[4,144,538]{2,1,0:T(8,128)(2,1)} %all-to-all-done.9), channel_id=1, source_target_pairs={{0,16},{16,0},{1,17},{17,1},{2,18},{18,2},{3,19},{19,3},{4,20},{20... | collective-permute-start | bytes 1859336 | tf_op jit(solution)/shard_map/ppermute | solution.py:287
  283.3 24.2 %all-to-all-start.8 = ((bf16[4,272,288]{2,1,0:T(8,128)(2,1)}), bf16[4,272,288]{2,1,0:T(8,128)(2,1)S(1)}, u32[]{:S(2)}, u32[]{:S(2)}) async-start(bf16[4,272,288]{2,1,0:T(8,128)(2,1)} %shard_map.252), calls=%async_computation.8 | async-start | bytes 1671168 | tf_op jit(solution)/shard_map/all_to_all | solution.py:290
  287.6 6.5 %collective-permute-start.27 = (bf16[288,288]{1,0:T(8,128)(2,1)S(1)}, bf16[288,288]{1,0:T(8,128)(2,1)S(1)}, u32[]{:S(2)}, u32[]{:S(2)}) collective-permute-start(bf16[288,288]{1,0:T(8,128)(2,1)S(1)} %convolution_convert_fusion.6), channel_id=1, source_target_pairs={{0,16},{16,0},{1,17},{17,1},{2,18},{18,2},{3,19},{19,3},{4,20},{20... | collective-permute-start | bytes 497672 | tf_op jit(solution)/shard_map/ppermute | solution.py:287
  318.6 11.2 %collective-permute-start.26 = (bf16[4,144,216]{2,1,0:T(8,128)(2,1)S(1)}, bf16[4,144,216]{2,1,0:T(8,128)(2,1)S(1)}, u32[]{:S(2)}, u32[]{:S(2)}) collective-permute-start(bf16[4,144,216]{2,1,0:T(8,128)(2,1)S(1)} %slice.373), channel_id=1, source_target_pairs={{0,16},{16,0},{1,17},{17,1},{2,18},{18,2},{3,19},{19,3},{4,20},{20... | collective-permute-start | bytes 746504 | tf_op jit(solution)/shard_map/ppermute | solution.py:287
  320.0 8.5 %collective-permute-start.25 = (f32[11,288]{1,0:T(8,128)S(1)}, f32[11,288]{1,0:T(8,128)S(1)}, u32[]{:S(2)}, u32[]{:S(2)}) collective-permute-start(f32[11,288]{1,0:T(8,128)S(1)} %pad_maximum_fusion.8), channel_id=1, source_target_pairs={{0,16},{16,0},{1,17},{17,1},{2,18},{18,2},{3,19},{19,3},{4,20},{20... | collective-permute-start | bytes 38024 | tf_op jit(solution)/shard_map/ppermute | solution.py:287
  (70 other events, 470.8 us)

commit v4 on v3

--- a/solution.py
+++ b/solution.py
@@ -33,6 +33,10 @@
 
 def pick(blocks, index, axis=0):
     return lax.dynamic_index_in_dim(blocks, index, axis, keepdims=False)
+
+
+def place(blocks, block, index):
+    return lax.dynamic_update_index_in_dim(blocks, block, index, 0)
 
 
 def after(values, *others):
@@ -175,11 +179,13 @@
     outs = [((2 * mine.shape[0], mine.shape[1]), mine.dtype)]
 
     def kernel(rank_ref, mine_ref, other_ref, out_ref):
-        for i in range(groups):
+        @pl.loop(0, groups)
+        def _(i):
+            at = pl.ds(pl.multiple_of(i * rows, 16), rows)
             first = pl.multiple_of((2 * i + rank_ref[0]) * rows, 16)
             second = pl.multiple_of((2 * i + 1 - rank_ref[0]) * rows, 16)
-            out_ref[pl.ds(first, rows), :] = mine_ref[i * rows : (i + 1) * rows, :]
-            out_ref[pl.ds(second, rows), :] = other_ref[i * rows : (i + 1) * rows, :]
+            out_ref[pl.ds(first, rows), :] = mine_ref[at, :]
+            out_ref[pl.ds(second, rows), :] = other_ref[at, :]
 
     return local_call(kernel, outs, rank.reshape(1).astype(jnp.int32), mine, other)[0]
 
@@ -190,8 +196,9 @@
     rows = mine.shape[0] // groups
 
     def kernel(rank_ref, mine_ref, other_ref, *out_refs):
-        for i in range(groups):
-            at = slice(i * rows, (i + 1) * rows)
+        @pl.loop(0, groups)
+        def _(i):
+            at = pl.ds(pl.multiple_of(i * rows, 16), rows)
             first = pl.multiple_of((2 * i + rank_ref[0]) * rows, 16)
             second = pl.multiple_of((2 * i + 1 - rank_ref[0]) * rows, 16)
             for k, out_ref in enumerate(out_refs):
@@ -289,8 +296,14 @@
     def row_exchange(blocks):
         return lax.all_to_all(blocks, "row", 0, 0, tiled=True)
 
-    def row_gather(value):
-        return row_exchange(jnp.broadcast_to(value[None], (n_row,) + value.shape))
+    def row_share(value):
+        row = lax.axis_index("row")
+        blocks = jnp.zeros((n_row,) + value.shape, value.dtype)
+        for k in range(n_row):
+            pairs = [(i, (i + k) % n_row) for i in range(n_row)]
+            piece = lax.ppermute(value, "row", pairs) if k else value
+            blocks = place(blocks, piece, (row - k) % n_row)
+        return blocks
 
     def col_parts(value):
         parts = [value]
@@ -472,7 +485,9 @@
         cot_full = col_gather(cot_rows)
         mlp_other = dp_swap(mlp_part) if paired else mlp_part
 
-        group_context = row_gather(after(own_context, third, merge_other)).reshape(n_row * head_size, padded)
+        group_context = row_share(after(own_context, merge_other)).reshape(
+            n_row * head_size, padded
+        )
         context_parts = col_parts(group_context)
         mlp_other = after(mlp_other, group_context)
         expand_own, reduce_own = mlp_join(mlp_part, mlp_other, rank, n_row, units, paired)

time: 334 us -> 347 us (1.039)
  matrix products: 34.3 us -> 40 us
  starting transfers between devices: 59.5 us -> 63.3 us
    ppermute x0 -> x3, waiting for transfers between devices: none -> 22.1 us  [row_share(): piece = lax.ppermute(value, 'row', pairs) if k else value]
    all_to_all x10 -> x9, waiting for transfers between devices: 63.8 us -> 48.5 us  [row_exchange(): return lax.all_to_all(blocks, 'row', 0, 0, tiled=True)]
    ppermute x21, waiting for transfers between devices: 46.5 us -> 34.4 us  [col_swap(): return lax.ppermute(value, 'col', [(i, i ^ mask) for i in range(n_col)])]
    dot_general x21, matrix products: 34.3 us -> 40 us  [dot(): lax.dot_general(left, right, (((left_dim,), (right_dim,)), ((), ())), pre...]
    all_to_all x10 -> x9, starting transfers between devices: 44.4 us -> 38.8 us  [row_exchange(): return lax.all_to_all(blocks, 'row', 0, 0, tiled=True)]
    ppermute x21, starting transfers between devices: 6.25 us -> 11.4 us  [col_swap(): return lax.ppermute(value, 'col', [(i, i ^ mask) for i in range(n_col)])]
    ppermute x0 -> x3, starting transfers between devices: none -> 5.15 us  [row_share(): piece = lax.ppermute(value, 'row', pairs) if k else value]
    ppermute x9, waiting for transfers between devices: 14.9 us -> 19.7 us  [dp_swap(): return lax.ppermute(value, 'dp', [(0, 1), (1, 0)])]
  transfers between devices with their start and end apart: 40 -> 42, of which waited for: 19 -> 20; matrix products, arithmetic and copies ran while one was open for 25% -> 27% of each run, Pallas kernels for 4% -> 3%
where the time goes in v4:
time: 347 us; the launch traced here: 345 us
  waiting for transfers between devices  125 us (36%)
  starting transfers between devices  63.3 us (18%)
  local copies, waits for them, and re-layouts  51.3 us (15%)
  matrix products  40 us (12%)
  other arithmetic  32.9 us (9%)
  Pallas kernels  19.7 us (6%)
  blocking collectives  10.8 us (3%)
    all_to_all x9, waiting for transfers between devices, row_exchange(): return lax.all_to_all(blocks, 'row', 0, 0, tiled=True)  48.5 us
    dot_general x21, matrix products, dot(): lax.dot_general(left, right, (((left_dim,), (right_dim,)), ((), ())), pre...  40 us
    all_to_all x9, starting transfers between devices, row_exchange(): return lax.all_to_all(blocks, 'row', 0, 0, tiled=True)  38.8 us
    ppermute x21, waiting for transfers between devices, col_swap(): return lax.ppermute(value, 'col', [(i, i ^ mask) for i in range(n_col)])  34.4 us
    ppermute x3, waiting for transfers between devices, row_share(): piece = lax.ppermute(value, 'row', pairs) if k else value  22.1 us
    pallas_call x8, Pallas kernels, local_call(): pl.pallas_call(kernel, out_shape=[jax.ShapeDtypeStruct(shape, kind) for s...  19.7 us
    ppermute x9, waiting for transfers between devices, dp_swap(): return lax.ppermute(value, 'dp', [(0, 1), (1, 0)])  19.7 us
    unnamed x145, local copies, waits for them, and re-layouts  19.1 us
  transfers between devices with their start and end apart: 42, of which 20 were waited for; matrix products, arithmetic and copies ran while one was open for 27% of the time, Pallas kernels for 3%

profile of v4, /device:TPU:0, one launch (start us, length us, event | category | flops | bytes accessed | tf_op | source)
XLA Modules:
  0.0 344.6 jit_solution(9625631824222618978)
XLA Ops:
  0.7 2.1 copy.112.input_ref
  3.3 3.2 shard_map.245
  6.5 2.3 copy.113
  8.8 6.5 %all-to-all-start = ((bf16[4,368,288]{1,2,0:T(8,128)(2,1)}), bf16[4,368,288]{1,2,0:T(8,128)(2,1)S(1)}, u32[]{:S(2)}, u32[]{:S(2)}) async-start(bf16[4,368,288]{1,2,0:T(8,128)(2,1)} %copy.113), calls=%async_computation | async-start | bytes 1769472 | tf_op jit(solution)/shard_map/all_to_all | solution.py:297
  20.0 17.5 %all-to-all-done = bf16[4,368,288]{1,2,0:T(8,128)(2,1)S(1)} async-done(((bf16[4,368,288]{1,2,0:T(8,128)(2,1)}), bf16[4,368,288]{1,2,0:T(8,128)(2,1)S(1)}, u32[]{:S(2)}, u32[]{:S(2)}) %all-to-all-start) | async-done | bytes 847904 | tf_op jit(solution)/shard_map/all_to_all | solution.py:297
  38.9 2.4 shard_map.246
  44.3 3.6 %all-to-all-start.1 = ((bf16[4,336,288]{1,2,0:T(8,128)(2,1)}), bf16[4,336,288]{1,2,0:T(8,128)(2,1)S(1)}, u32[]{:S(2)}, u32[]{:S(2)}) async-start(bf16[4,336,288]{1,2,0:T(8,128)(2,1)} %copy.117), calls=%async_computation.1 | async-start | bytes 1769472 | tf_op jit(solution)/shard_map/all_to_all | solution.py:297
  49.5 4.6 %collective-permute-done = bf16[192,1152]{1,0:T(8,128)(2,1)} collective-permute-done((bf16[192,1152]{1,0:T(8,128)(2,1)}, bf16[192,1152]{1,0:T(8,128)(2,1)}, u32[]{:S(2)}, u32[]{:S(2)}) %collective-permute-start) | collective-permute-done | bytes 442400 | tf_op jit(solution)/shard_map/ppermute | solution.py:291
  61.8 2.3 fusion.33
  66.7 4.0 %all-to-all-done.1 = bf16[4,336,288]{1,2,0:T(8,128)(2,1)S(1)} async-done(((bf16[4,336,288]{1,2,0:T(8,128)(2,1)}), bf16[4,336,288]{1,2,0:T(8,128)(2,1)S(1)}, u32[]{:S(2)}, u32[]{:S(2)}) %all-to-all-start.1) | async-done | bytes 774176 | tf_op jit(solution)/shard_map/all_to_all | solution.py:297
  72.1 2.3 shard_map.248
  77.8 3.5 %all-to-all-start.2 = ((bf16[4,144,640]{2,1,0:T(8,128)(2,1)}), bf16[4,144,640]{2,1,0:T(8,128)(2,1)S(1)}, u32[]{:S(2)}, u32[]{:S(2)}) async-start(bf16[4,144,640]{2,1,0:T(8,128)(2,1)} %pad_maximum_fusion.2), calls=%async_computation.2 | async-start | bytes 1474560 | tf_op jit(solution)/shard_map/all_to_all | solution.py:297
  87.7 12.7 %collective-permute-done.9 = bf16[72,768]{1,0:T(8,128)(2,1)S(1)} collective-permute-done((bf16[72,768]{1,0:T(8,128)(2,1)S(1)}, bf16[72,768]{1,0:T(8,128)(2,1)S(1)}, u32[]{:S(2)}, u32[]{:S(2)}) %collective-permute-start.9) | collective-permute-done | bytes 110624 | tf_op jit(solution)/shard_map/ppermute | solution.py:304
  100.4 3.8 %collective-permute-start.10 = (bf16[72,768]{1,0:T(8,128)(2,1)S(1)}, bf16[72,768]{1,0:T(8,128)(2,1)S(1)}, u32[]{:S(2)}, u32[]{:S(2)}) collective-permute-start(bf16[72,768]{1,0:T(8,128)(2,1)S(1)} %convolution_convert_fusion.7), channel_id=1, source_target_pairs={{0,8},{4,12},{8,0},{12,4},{1,9},{5,13},{9,1},{13,5},{2,10},{6,14},... | collective-permute-start | bytes 331784 | tf_op jit(solution)/shard_map/ppermute | solution.py:304
  104.2 4.7 %collective-permute-done.10 = bf16[72,768]{1,0:T(8,128)(2,1)S(1)} collective-permute-done((bf16[72,768]{1,0:T(8,128)(2,1)S(1)}, bf16[72,768]{1,0:T(8,128)(2,1)S(1)}, u32[]{:S(2)}, u32[]{:S(2)}) %collective-permute-start.10) | collective-permute-done | bytes 110624 | tf_op jit(solution)/shard_map/ppermute | solution.py:304
  108.9 4.7 %collective-permute-done.11 = bf16[72,768]{1,0:T(8,128)(2,1)S(1)} collective-permute-done((bf16[72,768]{1,0:T(8,128)(2,1)S(1)}, bf16[72,768]{1,0:T(8,128)(2,1)S(1)}, u32[]{:S(2)}, u32[]{:S(2)}) %collective-permute-start.11) | collective-permute-done | bytes 110624 | tf_op jit(solution)/shard_map/ppermute | solution.py:304
  119.1 7.3 %collective-permute-done.12 = bf16[288,768]{1,0:T(8,128)(2,1)} collective-permute-done((bf16[288,768]{1,0:T(8,128)(2,1)S(1)}, bf16[288,768]{1,0:T(8,128)(2,1)}, u32[]{:S(2)}, u32[]{:S(2)}) %collective-permute-start.12) | collective-permute-done | bytes 442400 | tf_op jit(solution)/shard_map/ppermute | solution.py:291
  126.4 2.0 fusion.119
  132.4 5.6 %fusion.117 = (f32[768]{0:T(1024)S(1)}, f32[768]{0:T(1024)S(1)}, f32[768,1152]{1,0:T(8,128)S(1)}) fusion(f32[1152]{0:T(1024)S(1)} %copy-done.62, bf16[288,1152]{1,0:T(8,128)(2,1)} %collective-permute-done.17, bf16[288,1152]{1,0:T(8,128)(2,1)} %collective-permute-done.16, bf16[288,1152]{1,0:T(8,128)(2,1)} %collective-permute-done.15, ...), kind=kOutput, calls=%fused_computation.259 | convolution fusion | flops 2080012800 | bytes 9742848 | tf_op jit(solution)/shard_map/dot_general | solution.py:29
  139.8 2.2 subtract_multiply_fusion
  142.0 7.1 %collective-permute-done.7.other_ref = bf16[576,640]{1,0:T(8,128)(2,1)} collective-permute-done((bf16[576,640]{1,0:T(8,128)(2,1)S(1)}, bf16[576,640]{1,0:T(8,128)(2,1)}, u32[]{:S(2)}, u32[]{:S(2)}) %collective-permute-start.7) | collective-permute-done | bytes 737312 | tf_op jit(solution)/shard_map/ppermute | solution.py:294
  149.0 3.0 shard_map.249
  152.1 4.1 %multiply_convert_fusion.1 = (bf16[768,269]{0,1:T(8,128)(2,1)}, f32[768,269]{0,1:T(8,128)S(1)}) fusion(f32[269]{0:T(512)S(1)} %copy-done.65, bf16[1152,269]{1,0:T(8,128)(2,1)} %get-tuple-element.49, f32[768,1152]{1,0:T(8,128)} %subtract_multiply_fusion, f32[1152]{0:T(1024)S(1)} %copy-done.61, f32[1152]{0:T(1024)S(1)} %copy-done.60), kind=kOutput, calls=%fused_computation.102 | convolution fusion | flops 480708096 | bytes 5408564 | tf_op jit(solution)/shard_map/dot_general | solution.py:29
  158.8 2.4 collective-permute-done.18
  164.3 10.9 %collective-permute-done.19 = bf16[192,1152]{1,0:T(8,128)(2,1)S(1)} collective-permute-done((bf16[192,1152]{1,0:T(8,128)(2,1)}, bf16[192,1152]{1,0:T(8,128)(2,1)S(1)}, u32[]{:S(2)}, u32[]{:S(2)}) %collective-permute-start.19) | collective-permute-done | bytes 442400 | tf_op jit(solution)/shard_map/ppermute | solution.py:291
  176.0 3.5 %all-to-all-start.3 = ((bf16[4,48,1152]{2,1,0:T(8,128)(2,1)}), bf16[4,48,1152]{2,1,0:T(8,128)(2,1)S(1)}, u32[]{:S(2)}, u32[]{:S(2)}) async-start(bf16[4,48,1152]{2,1,0:T(8,128)(2,1)} %bitcast.18), calls=%async_computation.3 | async-start | bytes 884736 | tf_op jit(solution)/shard_map/all_to_all | solution.py:297
  179.5 3.0 convolution_convert_fusion
  186.5 5.4 %all-to-all-done.3.part_ref = bf16[4,48,1152]{2,1,0:T(8,128)(2,1)S(1)} async-done(((bf16[4,48,1152]{2,1,0:T(8,128)(2,1)}), bf16[4,48,1152]{2,1,0:T(8,128)(2,1)S(1)}, u32[]{:S(2)}, u32[]{:S(2)}) %all-to-all-start.3) | async-done | bytes 442400 | tf_op jit(solution)/shard_map/all_to_all | solution.py:297
  192.7 2.3 shard_map.251
  195.0 3.7 %all-to-all-start.4 = ((bf16[4,48,1152]{2,1,0:T(8,128)(2,1)}), bf16[4,48,1152]{2,1,0:T(8,128)(2,1)S(1)}, u32[]{:S(2)}, u32[]{:S(2)}) async-start(bf16[4,48,1152]{2,1,0:T(8,128)(2,1)} %get-tuple-element.50), calls=%async_computation.4 | async-start | bytes 884736 | tf_op jit(solution)/shard_map/all_to_all | solution.py:297
  204.2 6.5 %all-to-all-done.4 = bf16[4,48,1152]{2,1,0:T(8,128)(2,1)S(1)} async-done(((bf16[4,48,1152]{2,1,0:T(8,128)(2,1)}), bf16[4,48,1152]{2,1,0:T(8,128)(2,1)S(1)}, u32[]{:S(2)}, u32[]{:S(2)}) %all-to-all-start.4) | async-done | bytes 442400 | tf_op jit(solution)/shard_map/all_to_all | solution.py:297
  212.2 2.7 convolution_convert_fusion.4
  215.4 3.4 convolution_convert_fusion.3
  225.6 4.5 %all-to-all-start.6 = ((bf16[4,48,1152]{2,1,0:T(8,128)(2,1)}), bf16[4,48,1152]{2,1,0:T(8,128)(2,1)}, u32[]{:S(2)}, u32[]{:S(2)}) async-start(bf16[4,48,1152]{2,1,0:T(8,128)(2,1)} %bitcast.24), calls=%async_computation.6 | async-start | bytes 884736 | tf_op jit(solution)/shard_map/all_to_all | solution.py:297
  240.7 3.3 fusion.1
  246.9 2.5 add_convert_fusion.2
  249.4 4.9 %all-to-all-start.8 = ((bf16[4,144,538]{2,1,0:T(8,128)(2,1)}), bf16[4,144,538]{2,1,0:T(8,128)(2,1)}, u32[]{:S(2)}, u32[]{:S(2)}) async-start(bf16[4,144,538]{2,1,0:T(8,128)(2,1)} %add_convert_fusion.2), calls=%async_computation.8 | async-start | bytes 1474560 | tf_op jit(solution)/shard_map/all_to_all | solution.py:297
  261.6 2.0 convolution_convert_fusion.5
  265.2 7.4 %collective-permute-done.24 = bf16[192,1152]{1,0:T(8,128)(2,1)} collective-permute-done((bf16[192,1152]{1,0:T(8,128)(2,1)}, bf16[192,1152]{1,0:T(8,128)(2,1)}, u32[]{:S(2)}, u32[]{:S(2)}) %collective-permute-start.24) | collective-permute-done | bytes 442400 | tf_op jit(solution)/shard_map/ppermute | solution.py:291
  272.6 2.1 fusion.36
  274.7 4.8 %all-to-all-start.5 = ((bf16[4,48,1152]{2,1,0:T(8,128)(2,1)}), bf16[4,48,1152]{2,1,0:T(8,128)(2,1)S(1)}, u32[]{:S(2)}, u32[]{:S(2)}) async-start(bf16[4,48,1152]{2,1,0:T(8,128)(2,1)} %bitcast.22), calls=%async_computation.5 | async-start | bytes 884736 | tf_op jit(solution)/shard_map/all_to_all | solution.py:297
  282.5 9.0 %all-to-all-done.5.part_ref = bf16[4,48,1152]{2,1,0:T(8,128)(2,1)S(1)} async-done(((bf16[4,48,1152]{2,1,0:T(8,128)(2,1)}), bf16[4,48,1152]{2,1,0:T(8,128)(2,1)S(1)}, u32[]{:S(2)}, u32[]{:S(2)}) %all-to-all-start.5) | async-done | bytes 442400 | tf_op jit(solution)/shard_map/all_to_all | solution.py:297
  292.2 2.7 shard_map.252
  294.8 3.8 %all-to-all-start.7 = ((bf16[4,272,288]{2,1,0:T(8,128)(2,1)}), bf16[4,272,288]{2,1,0:T(8,128)(2,1)S(1)}, u32[]{:S(2)}, u32[]{:S(2)}) async-start(bf16[4,272,288]{2,1,0:T(8,128)(2,1)} %shard_map.252), calls=%async_computation.7 | async-start | bytes 1671168 | tf_op jit(solution)/shard_map/all_to_all | solution.py:297
  300.9 5.7 %collective-permute-done.30 = bf16[288,288]{1,0:T(8,128)(2,1)S(1)} collective-permute-done((bf16[288,288]{1,0:T(8,128)(2,1)S(1)}, bf16[288,288]{1,0:T(8,128)(2,1)S(1)}, u32[]{:S(2)}, u32[]{:S(2)}) %collective-permute-start.30) | collective-permute-done | bytes 165920 | tf_op jit(solution)/shard_map/ppermute | solution.py:294
  312.8 6.1 %all-to-all-done.7 = bf16[4,272,288]{2,1,0:T(8,128)(2,1)S(1)} async-done(((bf16[4,272,288]{2,1,0:T(8,128)(2,1)}), bf16[4,272,288]{2,1,0:T(8,128)(2,1)S(1)}, u32[]{:S(2)}, u32[]{:S(2)}) %all-to-all-start.7) | async-done | bytes 626720 | tf_op jit(solution)/shard_map/all_to_all | solution.py:297
  320.1 10.8 %all-gather.1 = bf16[4,417,288]{1,2,0:T(8,128)(2,1)S(1)} all-gather(bf16[1,417,288]{1,2,0:T(8,128)(2,1)S(1)} %maximum_bitcast_fusion), channel_id=2, replica_groups=mesh['dp'=2,'row'=4,'col'=4] {'col'}, dimensions={0}, use_global_device_ids=true | all-gather | bytes 1200960 | tf_op jit(solution)/shard_map/all_gather | solution.py:593
  337.3 3.6 %collective-permute-done.28 = f32[11,288]{1,0:T(8,128)S(1)} collective-permute-done((f32[11,288]{1,0:T(8,128)S(1)}, f32[11,288]{1,0:T(8,128)S(1)}, u32[]{:S(2)}, u32[]{:S(2)}) %collective-permute-start.28) | collective-permute-done | bytes 12704 | tf_op jit(solution)/shard_map/ppermute | solution.py:294
  (325 shorter events, 114.5 us)
Async XLA Ops:
  8.8 28.7 %all-to-all-start = ((bf16[4,368,288]{1,2,0:T(8,128)(2,1)}), bf16[4,368,288]{1,2,0:T(8,128)(2,1)S(1)}, u32[]{:S(2)}, u32[]{:S(2)}) async-start(bf16[4,368,288]{1,2,0:T(8,128)(2,1)} %copy.113), calls=%async_computation | async-start | bytes 1769472 | tf_op jit(solution)/shard_map/all_to_all | solution.py:297
  41.3 18.5 %collective-permute-start.1 = (bf16[192,1152]{1,0:T(8,128)(2,1)}, bf16[192,1152]{1,0:T(8,128)(2,1)S(1)}, u32[]{:S(2)}, u32[]{:S(2)}) collective-permute-start(bf16[192,1152]{1,0:T(8,128)(2,1)} %get-tuple-element.35), channel_id=1, source_target_pairs={{0,1},{1,0},{2,3},{3,2},{4,5},{5,4},{6,7},{7,6},{8,9},{9,8},{10,11... | collective-permute-start | bytes 1327112 | tf_op jit(solution)/shard_map/ppermute | solution.py:291
  41.3 12.9 %collective-permute-start = (bf16[192,1152]{1,0:T(8,128)(2,1)}, bf16[192,1152]{1,0:T(8,128)(2,1)}, u32[]{:S(2)}, u32[]{:S(2)}) collective-permute-start(bf16[192,1152]{1,0:T(8,128)(2,1)} %get-tuple-element.35), channel_id=1, source_target_pairs={{0,2},{1,3},{2,0},{3,1},{4,6},{5,7},{6,4},{7,5},{8,10},{9,11},{10,... | collective-permute-start | bytes 1327112 | tf_op jit(solution)/shard_map/ppermute | solution.py:291
  43.0 16.8 %copy-start.19 = (bf16[192,1152]{1,0:T(8,128)(2,1)S(1)}, bf16[192,1152]{1,0:T(8,128)(2,1)}, u32[]{:S(2)}) copy-start(bf16[192,1152]{1,0:T(8,128)(2,1)} %get-tuple-element.35) | copy-start | bytes 1327108
  44.3 17.4 %copy-start.68 = (f32[216]{0:T(256)S(1)}, f32[216]{0:T(256)}, u32[]{:S(2)}) copy-start(f32[216]{0:T(256)} %pad_maximum_fusion.9) | copy-start | bytes 2596
  44.3 26.4 %all-to-all-start.1 = ((bf16[4,336,288]{1,2,0:T(8,128)(2,1)}), bf16[4,336,288]{1,2,0:T(8,128)(2,1)S(1)}, u32[]{:S(2)}, u32[]{:S(2)}) async-start(bf16[4,336,288]{1,2,0:T(8,128)(2,1)} %copy.117), calls=%async_computation.1 | async-start | bytes 1769472 | tf_op jit(solution)/shard_map/all_to_all | solution.py:297
  48.0 9.1 %collective-permute-start.3 = (bf16[576,216]{1,0:T(8,128)(2,1)S(1)}, bf16[576,216]{1,0:T(8,128)(2,1)S(1)}, u32[]{:S(2)}, u32[]{:S(2)}) collective-permute-start(bf16[576,216]{1,0:T(8,128)(2,1)S(1)} %copy-done.46), channel_id=1, source_target_pairs={{0,16},{16,0},{1,17},{17,1},{2,18},{18,2},{3,19},{19,3},{4,20},{20... | collective-permute-start | bytes 746504 | tf_op jit(solution)/shard_map/ppermute | solution.py:294
  54.2 5.6 %collective-permute-start.2 = (bf16[192,1152]{1,0:T(8,128)(2,1)}, bf16[192,1152]{1,0:T(8,128)(2,1)S(1)}, u32[]{:S(2)}, u32[]{:S(2)}) collective-permute-start(bf16[192,1152]{1,0:T(8,128)(2,1)} %collective-permute-done), channel_id=1, source_target_pairs={{0,1},{1,0},{2,3},{3,2},{4,5},{5,4},{6,7},{7,6},{8,9},{9,8},{10,11... | collective-permute-start | bytes 1327112 | tf_op jit(solution)/shard_map/ppermute | solution.py:291
  59.7 72.7 %copy-start.22 = (bf16[192,1152]{1,0:T(8,128)(2,1)}, bf16[192,1152]{1,0:T(8,128)(2,1)S(1)}, u32[]{:S(2)}) copy-start(bf16[192,1152]{1,0:T(8,128)(2,1)S(1)} %collective-permute-done.1) | copy-start | bytes 1327108
  74.4 9.3 %collective-permute-start.8 = (bf16[144,1152]{1,0:T(8,128)(2,1)}, bf16[144,1152]{1,0:T(8,128)(2,1)}, u32[]{:S(2)}, u32[]{:S(2)}) collective-permute-start(bf16[144,1152]{1,0:T(8,128)(2,1)} %get-tuple-element.45.mine_ref), channel_id=1, source_target_pairs={{0,16},{16,0},{1,17},{17,1},{2,18},{18,2},{3,19},{19,3},{4,20},{20... | collective-permute-start | bytes 995336 | tf_op jit(solution)/shard_map/ppermute | solution.py:294
  77.2 40.0 %collective-permute-start.5 = (bf16[192,1152]{1,0:T(8,128)(2,1)}, bf16[192,1152]{1,0:T(8,128)(2,1)}, u32[]{:S(2)}, u32[]{:S(2)}) collective-permute-start(bf16[192,1152]{1,0:T(8,128)(2,1)} %get-tuple-element.41), channel_id=1, source_target_pairs={{0,1},{1,0},{2,3},{3,2},{4,5},{5,4},{6,7},{7,6},{8,9},{9,8},{10,11... | collective-permute-start | bytes 1327112 | tf_op jit(solution)/shard_map/ppermute | solution.py:291
  77.3 36.5 %collective-permute-start.4 = (bf16[192,1152]{1,0:T(8,128)(2,1)}, bf16[192,1152]{1,0:T(8,128)(2,1)}, u32[]{:S(2)}, u32[]{:S(2)}) collective-permute-start(bf16[192,1152]{1,0:T(8,128)(2,1)} %get-tuple-element.41), channel_id=1, source_target_pairs={{0,2},{1,3},{2,0},{3,1},{4,6},{5,7},{6,4},{7,5},{8,10},{9,11},{10,... | collective-permute-start | bytes 1327112 | tf_op jit(solution)/shard_map/ppermute | solution.py:291
  77.8 52.7 %all-to-all-start.2 = ((bf16[4,144,640]{2,1,0:T(8,128)(2,1)}), bf16[4,144,640]{2,1,0:T(8,128)(2,1)S(1)}, u32[]{:S(2)}, u32[]{:S(2)}) async-start(bf16[4,144,640]{2,1,0:T(8,128)(2,1)} %pad_maximum_fusion.2), calls=%async_computation.2 | async-start | bytes 1474560 | tf_op jit(solution)/shard_map/all_to_all | solution.py:297
  85.7 46.7 %collective-permute-start.16 = (bf16[288,1152]{1,0:T(8,128)(2,1)}, bf16[288,1152]{1,0:T(8,128)(2,1)}, u32[]{:S(2)}, u32[]{:S(2)}) collective-permute-start(bf16[288,1152]{1,0:T(8,128)(2,1)} %shard_map.250), channel_id=1, source_target_pairs={{0,1},{1,0},{2,3},{3,2},{4,5},{5,4},{6,7},{7,6},{8,9},{9,8},{10,11... | collective-permute-start | bytes 1990664 | tf_op jit(solution)/shard_map/ppermute | solution.py:291
  85.7 42.7 %collective-permute-start.15 = (bf16[288,1152]{1,0:T(8,128)(2,1)}, bf16[288,1152]{1,0:T(8,128)(2,1)}, u32[]{:S(2)}, u32[]{:S(2)}) collective-permute-start(bf16[288,1152]{1,0:T(8,128)(2,1)} %shard_map.250), channel_id=1, source_target_pairs={{0,2},{1,3},{2,0},{3,1},{4,6},{5,7},{6,4},{7,5},{8,10},{9,11},{10,... | collective-permute-start | bytes 1990664 | tf_op jit(solution)/shard_map/ppermute | solution.py:291
  86.2 14.2 %collective-permute-start.9 = (bf16[72,768]{1,0:T(8,128)(2,1)S(1)}, bf16[72,768]{1,0:T(8,128)(2,1)S(1)}, u32[]{:S(2)}, u32[]{:S(2)}) collective-permute-start(bf16[72,768]{1,0:T(8,128)(2,1)S(1)} %convolution_convert_fusion.7), channel_id=1, source_target_pairs={{0,4},{4,8},{8,12},{12,0},{1,5},{5,9},{9,13},{13,1},{2,6},{6,10},{... | collective-permute-start | bytes 331784 | tf_op jit(solution)/shard_map/ppermute | solution.py:304
  100.4 8.4 %collective-permute-start.10 = (bf16[72,768]{1,0:T(8,128)(2,1)S(1)}, bf16[72,768]{1,0:T(8,128)(2,1)S(1)}, u32[]{:S(2)}, u32[]{:S(2)}) collective-permute-start(bf16[72,768]{1,0:T(8,128)(2,1)S(1)} %convolution_convert_fusion.7), channel_id=1, source_target_pairs={{0,8},{4,12},{8,0},{12,4},{1,9},{5,13},{9,1},{13,5},{2,10},{6,14},... | collective-permute-start | bytes 331784 | tf_op jit(solution)/shard_map/ppermute | solution.py:304
  108.9 4.7 %collective-permute-start.11 = (bf16[72,768]{1,0:T(8,128)(2,1)S(1)}, bf16[72,768]{1,0:T(8,128)(2,1)S(1)}, u32[]{:S(2)}, u32[]{:S(2)}) collective-permute-start(bf16[72,768]{1,0:T(8,128)(2,1)S(1)} %convolution_convert_fusion.7), channel_id=1, source_target_pairs={{0,12},{4,0},{8,4},{12,8},{1,13},{5,1},{9,5},{13,9},{2,14},{6,2},{... | collective-permute-start | bytes 331784 | tf_op jit(solution)/shard_map/ppermute | solution.py:304
  113.6 18.8 %copy-start.18 = (bf16[4,72,768]{2,1,0:T(8,128)(2,1)}, bf16[4,72,768]{2,1,0:T(8,128)(2,1)S(1)}, u32[]{:S(2)}) copy-start(bf16[4,72,768]{2,1,0:T(8,128)(2,1)S(1)} %bitcast_dynamic-update-slice_fusion) | copy-start | bytes 1327108
  113.6 15.3 %collective-permute-start.13 = (bf16[288,768]{1,0:T(8,128)(2,1)S(1)}, bf16[288,768]{1,0:T(8,128)(2,1)S(1)}, u32[]{:S(2)}, u32[]{:S(2)}) collective-permute-start(bf16[288,768]{1,0:T(8,128)(2,1)S(1)} %bitcast.128), channel_id=1, source_target_pairs={{0,1},{1,0},{2,3},{3,2},{4,5},{5,4},{6,7},{7,6},{8,9},{9,8},{10,11... | collective-permute-start | bytes 1327112 | tf_op jit(solution)/shard_map/ppermute | solution.py:291
  113.7 12.7 %collective-permute-start.12 = (bf16[288,768]{1,0:T(8,128)(2,1)S(1)}, bf16[288,768]{1,0:T(8,128)(2,1)}, u32[]{:S(2)}, u32[]{:S(2)}) collective-permute-start(bf16[288,768]{1,0:T(8,128)(2,1)S(1)} %bitcast.129), channel_id=1, source_target_pairs={{0,2},{1,3},{2,0},{3,1},{4,6},{5,7},{6,4},{7,5},{8,10},{9,11},{10,... | collective-permute-start | bytes 1327112 | tf_op jit(solution)/shard_map/ppermute | solution.py:291
  117.1 12.6 %collective-permute-start.6 = (bf16[192,1152]{1,0:T(8,128)(2,1)}, bf16[192,1152]{1,0:T(8,128)(2,1)S(1)}, u32[]{:S(2)}, u32[]{:S(2)}) collective-permute-start(bf16[192,1152]{1,0:T(8,128)(2,1)} %collective-permute-done.4), channel_id=1, source_target_pairs={{0,1},{1,0},{2,3},{3,2},{4,5},{5,4},{6,7},{7,6},{8,9},{9,8},{10,11... | collective-permute-start | bytes 1327112 | tf_op jit(solution)/shard_map/ppermute | solution.py:291
  126.4 4.7 %collective-permute-start.14 = (bf16[288,768]{1,0:T(8,128)(2,1)}, bf16[288,768]{1,0:T(8,128)(2,1)}, u32[]{:S(2)}, u32[]{:S(2)}) collective-permute-start(bf16[288,768]{1,0:T(8,128)(2,1)} %collective-permute-done.12), channel_id=1, source_target_pairs={{0,1},{1,0},{2,3},{3,2},{4,5},{5,4},{6,7},{7,6},{8,9},{9,8},{10,11... | collective-permute-start | bytes 1327112 | tf_op jit(solution)/shard_map/ppermute | solution.py:291
  128.4 4.0 %collective-permute-start.17 = (bf16[288,1152]{1,0:T(8,128)(2,1)}, bf16[288,1152]{1,0:T(8,128)(2,1)}, u32[]{:S(2)}, u32[]{:S(2)}) collective-permute-start(bf16[288,1152]{1,0:T(8,128)(2,1)} %collective-permute-done.15), channel_id=1, source_target_pairs={{0,1},{1,0},{2,3},{3,2},{4,5},{5,4},{6,7},{7,6},{8,9},{9,8},{10,11... | collective-permute-start | bytes 1990664 | tf_op jit(solution)/shard_map/ppermute | solution.py:291
  130.5 18.5 %collective-permute-start.7 = (bf16[576,640]{1,0:T(8,128)(2,1)S(1)}, bf16[576,640]{1,0:T(8,128)(2,1)}, u32[]{:S(2)}, u32[]{:S(2)}) collective-permute-start(bf16[576,640]{1,0:T(8,128)(2,1)S(1)} %bitcast.119), channel_id=1, source_target_pairs={{0,16},{16,0},{1,17},{17,1},{2,18},{18,2},{3,19},{19,3},{4,20},{20... | collective-permute-start | bytes 2211848 | tf_op jit(solution)/shard_map/ppermute | solution.py:294
  158.7 2.5 collective-permute-start.18
  162.8 12.4 %collective-permute-start.19 = (bf16[192,1152]{1,0:T(8,128)(2,1)}, bf16[192,1152]{1,0:T(8,128)(2,1)S(1)}, u32[]{:S(2)}, u32[]{:S(2)}) collective-permute-start(bf16[192,1152]{1,0:T(8,128)(2,1)} %slice.559), channel_id=1, source_target_pairs={{0,2},{1,3},{2,0},{3,1},{4,6},{5,7},{6,4},{7,5},{8,10},{9,11},{10,... | collective-permute-start | bytes 1327112 | tf_op jit(solution)/shard_map/ppermute | solution.py:291
  176.0 15.9 %all-to-all-start.3 = ((bf16[4,48,1152]{2,1,0:T(8,128)(2,1)}), bf16[4,48,1152]{2,1,0:T(8,128)(2,1)S(1)}, u32[]{:S(2)}, u32[]{:S(2)}) async-start(bf16[4,48,1152]{2,1,0:T(8,128)(2,1)} %bitcast.18), calls=%async_computation.3 | async-start | bytes 884736 | tf_op jit(solution)/shard_map/all_to_all | solution.py:297
  179.5 19.2 %copy-start.12 = (bf16[1152,269]{1,0:T(8,128)(2,1)S(1)}, bf16[1152,269]{1,0:T(8,128)(2,1)}, u32[]{:S(2)}) copy-start(bf16[1152,269]{1,0:T(8,128)(2,1)} %get-tuple-element.48) | copy-start | bytes 1859332
  179.5 19.2 %copy-start.41 = (bf16[768,269]{0,1:T(8,128)(2,1)S(1)}, bf16[768,269]{0,1:T(8,128)(2,1)}, u32[]{:S(2)}) copy-start(bf16[768,269]{0,1:T(8,128)(2,1)} %get-tuple-element.53) | copy-start | bytes 1239556
  182.5 16.1 %collective-permute-start.25 = (bf16[384,1152]{1,0:T(8,128)(2,1)}, bf16[384,1152]{1,0:T(8,128)(2,1)}, u32[]{:S(2)}, u32[]{:S(2)}) collective-permute-start(bf16[384,1152]{1,0:T(8,128)(2,1)} %convolution_convert_fusion), channel_id=1, source_target_pairs={{0,1},{1,0},{2,3},{3,2},{4,5},{5,4},{6,7},{7,6},{8,9},{9,8},{10,11... | collective-permute-start | bytes 2654216 | tf_op jit(solution)/shard_map/ppermute | solution.py:291
  195.0 15.7 %all-to-all-start.4 = ((bf16[4,48,1152]{2,1,0:T(8,128)(2,1)}), bf16[4,48,1152]{2,1,0:T(8,128)(2,1)S(1)}, u32[]{:S(2)}, u32[]{:S(2)}) async-start(bf16[4,48,1152]{2,1,0:T(8,128)(2,1)} %get-tuple-element.50), calls=%async_computation.4 | async-start | bytes 884736 | tf_op jit(solution)/shard_map/all_to_all | solution.py:297
  202.7 21.0 %collective-permute-start.26 = (bf16[192,1152]{1,0:T(8,128)(2,1)}, bf16[192,1152]{1,0:T(8,128)(2,1)}, u32[]{:S(2)}, u32[]{:S(2)}) collective-permute-start(bf16[192,1152]{1,0:T(8,128)(2,1)} %slice.557), channel_id=1, source_target_pairs={{0,2},{1,3},{2,0},{3,1},{4,6},{5,7},{6,4},{7,5},{8,10},{9,11},{10,... | collective-permute-start | bytes 1327112 | tf_op jit(solution)/shard_map/ppermute | solution.py:291
  210.7 13.0 %collective-permute-start.20 = (bf16[192,1152]{1,0:T(8,128)(2,1)S(1)}, bf16[192,1152]{1,0:T(8,128)(2,1)}, u32[]{:S(2)}, u32[]{:S(2)}) collective-permute-start(bf16[192,1152]{1,0:T(8,128)(2,1)S(1)} %bitcast.125), channel_id=1, source_target_pairs={{0,2},{1,3},{2,0},{3,1},{4,6},{5,7},{6,4},{7,5},{8,10},{9,11},{10,... | collective-permute-start | bytes 1327112 | tf_op jit(solution)/shard_map/ppermute | solution.py:291
  221.5 25.5 %collective-permute-start.31 = (bf16[4,144,538]{2,1,0:T(8,128)(2,1)}, bf16[4,144,538]{2,1,0:T(8,128)(2,1)}, u32[]{:S(2)}, u32[]{:S(2)}) collective-permute-start(bf16[4,144,538]{2,1,0:T(8,128)(2,1)} %fusion.43), channel_id=1, source_target_pairs={{0,16},{16,0},{1,17},{17,1},{2,18},{18,2},{3,19},{19,3},{4,20},{20... | collective-permute-start | bytes 1859336 | tf_op jit(solution)/shard_map/ppermute | solution.py:294
  222.0 8.1 %collective-permute-start.21 = (bf16[192,1152]{1,0:T(8,128)(2,1)S(1)}, bf16[192,1152]{1,0:T(8,128)(2,1)S(1)}, u32[]{:S(2)}, u32[]{:S(2)}) collective-permute-start(bf16[192,1152]{1,0:T(8,128)(2,1)S(1)} %bitcast.126), channel_id=1, source_target_pairs={{0,1},{1,0},{2,3},{3,2},{4,5},{5,4},{6,7},{7,6},{8,9},{9,8},{10,11... | collective-permute-start | bytes 1327112 | tf_op jit(solution)/shard_map/ppermute | solution.py:291
  223.7 7.2 %collective-permute-start.22 = (bf16[192,1152]{1,0:T(8,128)(2,1)}, bf16[192,1152]{1,0:T(8,128)(2,1)}, u32[]{:S(2)}, u32[]{:S(2)}) collective-permute-start(bf16[192,1152]{1,0:T(8,128)(2,1)} %collective-permute-done.20), channel_id=1, source_target_pairs={{0,1},{1,0},{2,3},{3,2},{4,5},{5,4},{6,7},{7,6},{8,9},{9,8},{10,11... | collective-permute-start | bytes 1327112 | tf_op jit(solution)/shard_map/ppermute | solution.py:291
  225.6 23.8 %all-to-all-start.6 = ((bf16[4,48,1152]{2,1,0:T(8,128)(2,1)}), bf16[4,48,1152]{2,1,0:T(8,128)(2,1)}, u32[]{:S(2)}, u32[]{:S(2)}) async-start(bf16[4,48,1152]{2,1,0:T(8,128)(2,1)} %bitcast.24), calls=%async_computation.6 | async-start | bytes 884736 | tf_op jit(solution)/shard_map/all_to_all | solution.py:297
  240.4 15.8 %collective-permute-start.23 = (bf16[384,1152]{1,0:T(8,128)(2,1)}, bf16[384,1152]{1,0:T(8,128)(2,1)}, u32[]{:S(2)}, u32[]{:S(2)}) collective-permute-start(bf16[384,1152]{1,0:T(8,128)(2,1)} %convolution_convert_fusion.2), channel_id=1, source_target_pairs={{0,1},{1,0},{2,3},{3,2},{4,5},{5,4},{6,7},{7,6},{8,9},{9,8},{10,11... | collective-permute-start | bytes 2654216 | tf_op jit(solution)/shard_map/ppermute | solution.py:291
  249.4 25.3 %all-to-all-start.8 = ((bf16[4,144,538]{2,1,0:T(8,128)(2,1)}), bf16[4,144,538]{2,1,0:T(8,128)(2,1)}, u32[]{:S(2)}, u32[]{:S(2)}) async-start(bf16[4,144,538]{2,1,0:T(8,128)(2,1)} %add_convert_fusion.2), calls=%async_computation.8 | async-start | bytes 1474560 | tf_op jit(solution)/shard_map/all_to_all | solution.py:297
  260.1 12.5 %collective-permute-start.24 = (bf16[192,1152]{1,0:T(8,128)(2,1)}, bf16[192,1152]{1,0:T(8,128)(2,1)}, u32[]{:S(2)}, u32[]{:S(2)}) collective-permute-start(bf16[192,1152]{1,0:T(8,128)(2,1)} %slice.558), channel_id=1, source_target_pairs={{0,2},{1,3},{2,0},{3,1},{4,6},{5,7},{6,4},{7,5},{8,10},{9,11},{10,... | collective-permute-start | bytes 1327112 | tf_op jit(solution)/shard_map/ppermute | solution.py:291
  264.6 16.5 %collective-permute-start.27 = (bf16[4,144,216]{2,1,0:T(8,128)(2,1)}, bf16[4,144,216]{2,1,0:T(8,128)(2,1)S(1)}, u32[]{:S(2)}, u32[]{:S(2)}) collective-permute-start(bf16[4,144,216]{2,1,0:T(8,128)(2,1)} %constant_dynamic-slice_fusion.1), channel_id=1, source_target_pairs={{0,16},{16,0},{1,17},{17,1},{2,18},{18,2},{3,19},{19,3},{4,20},{20... | collective-permute-start | bytes 746504 | tf_op jit(solution)/shard_map/ppermute | solution.py:294
  274.7 16.7 %all-to-all-start.5 = ((bf16[4,48,1152]{2,1,0:T(8,128)(2,1)}), bf16[4,48,1152]{2,1,0:T(8,128)(2,1)S(1)}, u32[]{:S(2)}, u32[]{:S(2)}) async-start(bf16[4,48,1152]{2,1,0:T(8,128)(2,1)} %bitcast.22), calls=%async_computation.5 | async-start | bytes 884736 | tf_op jit(solution)/shard_map/all_to_all | solution.py:297
  281.9 25.5 %collective-permute-start.32 = (bf16[4,144,538]{2,1,0:T(8,128)(2,1)}, bf16[4,144,538]{2,1,0:T(8,128)(2,1)}, u32[]{:S(2)}, u32[]{:S(2)}) collective-permute-start(bf16[4,144,538]{2,1,0:T(8,128)(2,1)} %all-to-all-done.8), channel_id=1, source_target_pairs={{0,16},{16,0},{1,17},{17,1},{2,18},{18,2},{3,19},{19,3},{4,20},{20... | collective-permute-start | bytes 1859336 | tf_op jit(solution)/shard_map/ppermute | solution.py:294
  294.8 24.1 %all-to-all-start.7 = ((bf16[4,272,288]{2,1,0:T(8,128)(2,1)}), bf16[4,272,288]{2,1,0:T(8,128)(2,1)S(1)}, u32[]{:S(2)}, u32[]{:S(2)}) async-start(bf16[4,272,288]{2,1,0:T(8,128)(2,1)} %shard_map.252), calls=%async_computation.7 | async-start | bytes 1671168 | tf_op jit(solution)/shard_map/all_to_all | solution.py:297
  300.1 6.4 %collective-permute-start.30 = (bf16[288,288]{1,0:T(8,128)(2,1)S(1)}, bf16[288,288]{1,0:T(8,128)(2,1)S(1)}, u32[]{:S(2)}, u32[]{:S(2)}) collective-permute-start(bf16[288,288]{1,0:T(8,128)(2,1)S(1)} %convolution_convert_fusion.6), channel_id=1, source_target_pairs={{0,16},{16,0},{1,17},{17,1},{2,18},{18,2},{3,19},{19,3},{4,20},{20... | collective-permute-start | bytes 497672 | tf_op jit(solution)/shard_map/ppermute | solution.py:294
  331.1 11.2 %collective-permute-start.29 = (bf16[4,144,216]{2,1,0:T(8,128)(2,1)S(1)}, bf16[4,144,216]{2,1,0:T(8,128)(2,1)S(1)}, u32[]{:S(2)}, u32[]{:S(2)}) collective-permute-start(bf16[4,144,216]{2,1,0:T(8,128)(2,1)S(1)} %slice.373), channel_id=1, source_target_pairs={{0,16},{16,0},{1,17},{17,1},{2,18},{18,2},{3,19},{19,3},{4,20},{20... | collective-permute-start | bytes 746504 | tf_op jit(solution)/shard_map/ppermute | solution.py:294
  332.5 8.5 %collective-permute-start.28 = (f32[11,288]{1,0:T(8,128)S(1)}, f32[11,288]{1,0:T(8,128)S(1)}, u32[]{:S(2)}, u32[]{:S(2)}) collective-permute-start(f32[11,288]{1,0:T(8,128)S(1)} %pad_maximum_fusion.8), channel_id=1, source_target_pairs={{0,16},{16,0},{1,17},{17,1},{2,18},{18,2},{3,19},{19,3},{4,20},{20... | collective-permute-start | bytes 38024 | tf_op jit(solution)/shard_map/ppermute | solution.py:294
  (63 other events, 371.2 us)
